TPU v7x, 128 devices: a whole 4x4x4 slice. The times are simulated.
128 devices in a mesh: rows: 16 (over x, z), cols: 4 (over y), slab: 2 (over core).
Axes of the slice: x: 4, y: 4, z: 4, core: 2. Of those that a mesh axis runs over, the one named last changes fastest.
Arguments:
- density_blocks: bfloat16 [8192, 4096], P(('rows', 'cols', 'slab')), may hold values from -6 to 6
- block_owner: int32 [8192, 1], P(('rows', 'cols', 'slab')), may hold values from 0 to 127; in each aligned block of 64 rows (0 to 63, 64 to 127, ...) at most 2 rows name the same one
- block_plane: int32 [8192], P(('rows', 'cols', 'slab')), may hold values from 0 to 7
- block_segment: int32 [8192], P(('rows', 'cols', 'slab')), may hold values from 0 to 7
- block_kinds: int32 [8192, 2], P(('rows', 'cols', 'slab')), may hold values from 0 to 3
- basis: bfloat16 [4, 64, 4096], replicated, may hold values from -1.015625 to 1.015625
- ext_potential: float32 [1024, 4096], P(('rows', 'cols', 'slab')), may hold values from -6 to 6
Outputs:
- density: float32 [1024, 4096], P(('rows', 'cols', 'slab'))
- matrix_blocks: bfloat16 [8192, 4096], P(('rows', 'cols', 'slab'))
Inputs may be any that keep to these rules, and one draw needn't show every extreme that they name: `block_owner`: among the blocks of one device no owner is named more than 2 times; some owner is named exactly 2 times.
All inputs are finite; a program needn't handle non-finite values.
Results may differ from a plain program's by a relative error of at most 0.0095.
Values may be sent and summed in bfloat16 or wider, within the bound.
No kernel may reach another device: no remote copies, remote signals or barrier semaphores. Data moves between devices by JAX's collectives and lax.ppermute only.
A program may use at most 128 MiB of HBM per device.

v0:
```python
import jax
import jax.numpy as jnp
from jax import lax
from jax.sharding import PartitionSpec as P

CZB = 8
SEGW = 512


def shifted(x, axis, by):
    size = lax.axis_size(axis)
    return lax.ppermute(x, axis, [(i, (i + by) % size) for i in range(size)])


def pick_basis(kind_ids, basis):
    kind_hot = (kind_ids[:, None] == jnp.arange(basis.shape[0], dtype=jnp.int32)[None, :]).astype(
        jnp.bfloat16
    )
    return jnp.einsum("bk,knc->bnc", kind_hot, basis, preferred_element_type=jnp.float32).astype(
        jnp.bfloat16
    )


def placement(meta_batch, czb_count, zext, segs):
    offsets = jnp.arange(czb_count, dtype=jnp.int32)
    plane_hot = (
        meta_batch[:, 0][:, None, None] + offsets[None, :, None]
        == jnp.arange(zext, dtype=jnp.int32)[None, None, :]
    ).astype(jnp.float32)
    seg_hot = (meta_batch[:, 1][:, None] == jnp.arange(segs, dtype=jnp.int32)[None, :]).astype(
        jnp.float32
    )
    place = plane_hot[:, :, :, None] * seg_hot[:, None, None, :]
    return place.reshape(meta_batch.shape[0] * czb_count, zext * segs)


def local(
    density_blocks, block_owner, block_plane, block_segment, block_kinds, basis, ext_potential
):
    device_count = lax.axis_size(("rows", "cols", "slab"))
    block_count = density_blocks.shape[0]
    capacity = max(2, (2 * block_count + device_count - 1) // device_count)
    width = basis.shape[1]
    cube_cells = basis.shape[2]
    zplanes = ext_potential.shape[0]
    segs = ext_potential.shape[1] // SEGW
    owner_index = block_owner[:, 0]
    one_hot = (owner_index[:, None] == jnp.arange(device_count, dtype=jnp.int32)[None, :]).astype(
        jnp.int32
    )
    rank_within = jnp.sum((jnp.cumsum(one_hot, axis=0) - one_hot) * one_hot, axis=1)
    slot_index = owner_index * capacity + rank_within
    block_meta = jnp.stack(
        [block_plane, block_segment, block_kinds[:, 0], block_kinds[:, 1]], axis=1
    )
    slot_total = device_count * capacity
    send_blocks = (
        jnp.zeros((slot_total, density_blocks.shape[1]), jnp.bfloat16)
        .at[slot_index]
        .set(density_blocks)
    )
    send_meta = jnp.zeros((slot_total, 4), jnp.int32).at[slot_index].set(block_meta)
    got_blocks, got_meta = (
        lax.all_to_all(
            send_blocks, ("rows", "cols", "slab"), split_axis=0, concat_axis=0, tiled=True
        ),
        lax.all_to_all(
            send_meta, ("rows", "cols", "slab"), split_axis=0, concat_axis=0, tiled=True
        ),
    )
    per_batch = min(32, slot_total)
    batch_count = slot_total // per_batch
    meta_batches = got_meta.reshape(batch_count, per_batch, 4)
    block_batches = got_blocks.reshape(batch_count, per_batch, width, width)
    zext = zplanes + CZB - 1
    extended_rows = zext * segs

    def deposit(grid_rows, batch_item):
        block_batch, meta_batch = batch_item
        row_basis = pick_basis(meta_batch[:, 2], basis)
        col_basis = pick_basis(meta_batch[:, 3], basis)
        half_product = jnp.einsum(
            "bmn,bnc->bmc", block_batch, col_basis, preferred_element_type=jnp.float32
        ).astype(jnp.bfloat16)
        product_tile = jnp.einsum(
            "bmc,bmc->bc", row_basis, half_product, preferred_element_type=jnp.float32
        )
        place = placement(meta_batch, CZB, zext, segs)
        added = jnp.einsum(
            "rz,rw->zw", place, product_tile.reshape(-1, SEGW), precision=lax.Precision.HIGHEST
        )
        return (grid_rows + added, None)

    grid_rows, _ = lax.scan(
        deposit, jnp.zeros((extended_rows, SEGW), jnp.float32), (block_batches, meta_batches)
    )
    owned_rows = zplanes * segs
    rim_rows = (CZB - 1) * segs
    arrived = shifted(grid_rows[owned_rows:], ("rows", "cols", "slab"), 1)
    owned = grid_rows[:owned_rows]
    owned = jnp.concatenate([owned[:rim_rows] + arrived, owned[rim_rows:]], axis=0)
    density = owned.reshape(zplanes, -1)
    potential = (ext_potential + 0.5 * density).reshape(owned_rows, SEGW)
    upper_rim = shifted(potential[:rim_rows], ("rows", "cols", "slab"), -1)
    potential_ext = jnp.concatenate([potential, upper_rim], axis=0)

    def integrate(carry, meta_batch):
        row_basis = pick_basis(meta_batch[:, 2], basis)
        col_basis = pick_basis(meta_batch[:, 3], basis)
        place = placement(meta_batch, CZB, zext, segs)
        pot_tile = jnp.einsum(
            "rz,zw->rw", place, potential_ext, precision=lax.Precision.HIGHEST
        ).reshape(per_batch, cube_cells)
        weighted = (row_basis.astype(jnp.float32) * pot_tile[:, None, :]).astype(jnp.bfloat16)
        matrix_tile = jnp.einsum(
            "bmc,bnc->bmn", weighted, col_basis, preferred_element_type=jnp.float32
        ).astype(jnp.bfloat16)
        return (carry, matrix_tile.reshape(per_batch, width * width))

    _, matrix_tiles = lax.scan(integrate, jnp.zeros((), jnp.float32), meta_batches)
    matrix_slots = matrix_tiles.reshape(slot_total, width * width)
    returned = lax.all_to_all(
        matrix_slots, ("rows", "cols", "slab"), split_axis=0, concat_axis=0, tiled=True
    )
    matrix_blocks = returned[slot_index]
    return (density, matrix_blocks)


def solution(mesh):
    placed = (
        P(("rows", "cols", "slab"), None),
        P(("rows", "cols", "slab"), None),
        P(("rows", "cols", "slab")),
        P(("rows", "cols", "slab")),
        P(("rows", "cols", "slab"), None),
        P(),
        P(("rows", "cols", "slab"), None),
    )
    return jax.shard_map(
        local,
        mesh=mesh,
        in_specs=placed,
        out_specs=(P(("rows", "cols", "slab"), None), P(("rows", "cols", "slab"), None)),
        check_vma=False,
    )
```

profile of v0, /device:TPU:1, one launch (start us, length us, event | category | flops | bytes accessed | tf_op | source)
XLA Modules:
  0.0 1267.3 jit_solution(5213833292374901474)
XLA Ops:
  5.1 11.5 all-to-all-start
  21.9 4.7 all-to-all-done
  26.6 5.5 all-to-all-start.1
  32.2 29.7 %all-to-all-done.1 = bf16[128,2,4096]{2,1,0:T(2,128)(2,1)} async-done(((bf16[128,2,4096]{2,1,0:T(2,128)(2,1)}), bf16[128,2,4096]{2,1,0:T(2,128)(2,1)}, u32[]{:S(2)}, u32[]{:S(2)}) %all-to-all-start.1) | async-done | bytes 2097184 | tf_op jit(solution)/shard_map/all_to_all | solution.py:64
  61.9 7.8 reshape.153
  69.8 685.6 %while.22 = (s32[]{:T(128)}, f32[120,512]{1,0:T(8,128)S(1)}, s32[8,32,4]{1,2,0:T(4,128)S(1)}, bf16[4,64,4096]{2,1,0:T(8,128)(2,1)S(1)}, bf16[8,32,64,64]{3,2,1,0:T(8,128)(2,1)}, /*index=5*/s32[]{:T(128)}, s32[]{:T(128)}) while((s32[]{:T(128)}, f32[120,512]{1,0:T(8,128)S(1)}, s32[8,32,4]{1,2,0:T(4,128)S(1)}, ...), condition=%wide.region_5.6_spmd.clone, body=%wide.region_4.5_spmd.clone.sunk | while | flops 1438677504 | bytes 74945624 | solution.py:94
  91.8 8.2 fusion.89
  100.0 8.2 fusion.90
  108.2 59.7 %fusion.91 = f32[32,4096]{1,0:T(8,128)S(1)} fusion(bf16[32,64,4096]{2,0,1:T(8,128)(2,1)} %fusion.89, bf16[32,64,4096]{2,0,1:T(8,128)(2,1)} %fusion.90, bf16[8,32,64,64]{3,2,1,0:T(8,128)(2,1)} %get-tuple-element.210, s32[]{:T(128)} %get-tuple-element.199), kind=kOutput, calls=%fused_computation.32.clone.1 | convolution fusion | flops 1115553792 | bytes 34603520 | tf_op jit(solution)/shard_map/while/body/eval_jaxpr/bmn,bnc->bmc/dot_general | solution.py:82
  169.7 2.6 mul.117
  172.8 8.2 fusion.89
  181.0 8.2 fusion.90
  189.2 59.6 %fusion.91 = f32[32,4096]{1,0:T(8,128)S(1)} fusion(bf16[32,64,4096]{2,0,1:T(8,128)(2,1)} %fusion.89, bf16[32,64,4096]{2,0,1:T(8,128)(2,1)} %fusion.90, bf16[8,32,64,64]{3,2,1,0:T(8,128)(2,1)} %get-tuple-element.210, s32[]{:T(128)} %get-tuple-element.199), kind=kOutput, calls=%fused_computation.32.clone.1 | convolution fusion | flops 1115553792 | bytes 34603520 | tf_op jit(solution)/shard_map/while/body/eval_jaxpr/bmn,bnc->bmc/dot_general | solution.py:82
  250.7 2.6 mul.117
  253.8 8.2 fusion.89
  262.0 8.2 fusion.90
  270.2 59.6 %fusion.91 = f32[32,4096]{1,0:T(8,128)S(1)} fusion(bf16[32,64,4096]{2,0,1:T(8,128)(2,1)} %fusion.89, bf16[32,64,4096]{2,0,1:T(8,128)(2,1)} %fusion.90, bf16[8,32,64,64]{3,2,1,0:T(8,128)(2,1)} %get-tuple-element.210, s32[]{:T(128)} %get-tuple-element.199), kind=kOutput, calls=%fused_computation.32.clone.1 | convolution fusion | flops 1115553792 | bytes 34603520 | tf_op jit(solution)/shard_map/while/body/eval_jaxpr/bmn,bnc->bmc/dot_general | solution.py:82
  331.7 2.6 mul.117
  334.8 8.2 fusion.89
  343.0 8.2 fusion.90
  351.2 59.6 %fusion.91 = f32[32,4096]{1,0:T(8,128)S(1)} fusion(bf16[32,64,4096]{2,0,1:T(8,128)(2,1)} %fusion.89, bf16[32,64,4096]{2,0,1:T(8,128)(2,1)} %fusion.90, bf16[8,32,64,64]{3,2,1,0:T(8,128)(2,1)} %get-tuple-element.210, s32[]{:T(128)} %get-tuple-element.199), kind=kOutput, calls=%fused_computation.32.clone.1 | convolution fusion | flops 1115553792 | bytes 34603520 | tf_op jit(solution)/shard_map/while/body/eval_jaxpr/bmn,bnc->bmc/dot_general | solution.py:82
  415.8 8.2 fusion.89
  424.0 8.2 fusion.90
  432.1 59.6 %fusion.91 = f32[32,4096]{1,0:T(8,128)S(1)} fusion(bf16[32,64,4096]{2,0,1:T(8,128)(2,1)} %fusion.89, bf16[32,64,4096]{2,0,1:T(8,128)(2,1)} %fusion.90, bf16[8,32,64,64]{3,2,1,0:T(8,128)(2,1)} %get-tuple-element.210, s32[]{:T(128)} %get-tuple-element.199), kind=kOutput, calls=%fused_computation.32.clone.1 | convolution fusion | flops 1115553792 | bytes 34603520 | tf_op jit(solution)/shard_map/while/body/eval_jaxpr/bmn,bnc->bmc/dot_general | solution.py:82
  493.6 2.6 mul.117
  496.7 8.2 fusion.89
  504.9 8.2 fusion.90
  513.1 59.6 %fusion.91 = f32[32,4096]{1,0:T(8,128)S(1)} fusion(bf16[32,64,4096]{2,0,1:T(8,128)(2,1)} %fusion.89, bf16[32,64,4096]{2,0,1:T(8,128)(2,1)} %fusion.90, bf16[8,32,64,64]{3,2,1,0:T(8,128)(2,1)} %get-tuple-element.210, s32[]{:T(128)} %get-tuple-element.199), kind=kOutput, calls=%fused_computation.32.clone.1 | convolution fusion | flops 1115553792 | bytes 34603520 | tf_op jit(solution)/shard_map/while/body/eval_jaxpr/bmn,bnc->bmc/dot_general | solution.py:82
  577.7 8.2 fusion.89
  585.9 8.2 fusion.90
  594.1 59.6 %fusion.91 = f32[32,4096]{1,0:T(8,128)S(1)} fusion(bf16[32,64,4096]{2,0,1:T(8,128)(2,1)} %fusion.89, bf16[32,64,4096]{2,0,1:T(8,128)(2,1)} %fusion.90, bf16[8,32,64,64]{3,2,1,0:T(8,128)(2,1)} %get-tuple-element.210, s32[]{:T(128)} %get-tuple-element.199), kind=kOutput, calls=%fused_computation.32.clone.1 | convolution fusion | flops 1115553792 | bytes 34603520 | tf_op jit(solution)/shard_map/while/body/eval_jaxpr/bmn,bnc->bmc/dot_general | solution.py:82
  658.7 8.2 fusion.89
  666.9 8.2 fusion.90
  675.1 59.6 %fusion.91 = f32[32,4096]{1,0:T(8,128)S(1)} fusion(bf16[32,64,4096]{2,0,1:T(8,128)(2,1)} %fusion.89, bf16[32,64,4096]{2,0,1:T(8,128)(2,1)} %fusion.90, bf16[8,32,64,64]{3,2,1,0:T(8,128)(2,1)} %get-tuple-element.210, s32[]{:T(128)} %get-tuple-element.199), kind=kOutput, calls=%fused_computation.32.clone.1 | convolution fusion | flops 1115553792 | bytes 34603520 | tf_op jit(solution)/shard_map/while/body/eval_jaxpr/bmn,bnc->bmc/dot_general | solution.py:82
  758.7 7.9 collective-permute-start.1
  767.6 450.9 %while.21 = (s32[]{:T(128)}, bf16[8,32,4096]{2,1,0:T(8,128)(2,1)}, s32[8,32,4]{1,2,0:T(4,128)S(1)}, bf16[4,64,4096]{2,1,0:T(8,128)(2,1)S(1)}, f32[120,512]{1,0:T(8,128)S(1)}, /*index=5*/s32[]{:T(128)}) while((s32[]{:T(128)}, bf16[8,32,4096]{2,1,0:T(8,128)(2,1)}, s32[8,32,4]{1,2,0:T(4,128)S(1)}, bf16[4,64,4096]{2,1,0:T(8,128)(2,1)S(1)}, ...), condition=%wide.region_7.8_spmd, body=%wide.region_6.7_spmd.sunk | while | flops 1422039552 | bytes 75486280 | solution.py:120
  772.7 8.2 fusion.74
  781.0 8.2 fusion.75
  789.1 32.6 %fusion.79 = bf16[32,64,64]{2,1,0:T(8,128)(2,1)} fusion(bf16[32,64,4096]{2,0,1:T(8,128)(2,1)} %fusion.74, bf16[32,64,4096]{2,0,1:T(8,128)(2,1)} %fusion.75, f32[32,4096]{1,0:T(8,128)S(1)} %mul.113), kind=kOutput, calls=%fused_computation.12.clone.1 | convolution fusion | flops 1099038720 | bytes 34340864 | tf_op jit(solution)/shard_map/while/body/eval_jaxpr/bmc,bnc->bmn/dot_general | solution.py:115
  829.1 8.2 fusion.74
  837.3 8.2 fusion.75
  845.5 32.6 %fusion.79 = bf16[32,64,64]{2,1,0:T(8,128)(2,1)} fusion(bf16[32,64,4096]{2,0,1:T(8,128)(2,1)} %fusion.74, bf16[32,64,4096]{2,0,1:T(8,128)(2,1)} %fusion.75, f32[32,4096]{1,0:T(8,128)S(1)} %mul.113), kind=kOutput, calls=%fused_computation.12.clone.1 | convolution fusion | flops 1099038720 | bytes 34340864 | tf_op jit(solution)/shard_map/while/body/eval_jaxpr/bmc,bnc->bmn/dot_general | solution.py:115
  885.5 8.2 fusion.74
  893.7 8.2 fusion.75
  901.9 32.6 %fusion.79 = bf16[32,64,64]{2,1,0:T(8,128)(2,1)} fusion(bf16[32,64,4096]{2,0,1:T(8,128)(2,1)} %fusion.74, bf16[32,64,4096]{2,0,1:T(8,128)(2,1)} %fusion.75, f32[32,4096]{1,0:T(8,128)S(1)} %mul.113), kind=kOutput, calls=%fused_computation.12.clone.1 | convolution fusion | flops 1099038720 | bytes 34340864 | tf_op jit(solution)/shard_map/while/body/eval_jaxpr/bmc,bnc->bmn/dot_general | solution.py:115
  941.8 8.2 fusion.74
  950.0 8.2 fusion.75
  958.2 32.6 %fusion.79 = bf16[32,64,64]{2,1,0:T(8,128)(2,1)} fusion(bf16[32,64,4096]{2,0,1:T(8,128)(2,1)} %fusion.74, bf16[32,64,4096]{2,0,1:T(8,128)(2,1)} %fusion.75, f32[32,4096]{1,0:T(8,128)S(1)} %mul.113), kind=kOutput, calls=%fused_computation.12.clone.1 | convolution fusion | flops 1099038720 | bytes 34340864 | tf_op jit(solution)/shard_map/while/body/eval_jaxpr/bmc,bnc->bmn/dot_general | solution.py:115
  998.2 8.2 fusion.74
  1006.4 8.2 fusion.75
  1014.6 32.6 %fusion.79 = bf16[32,64,64]{2,1,0:T(8,128)(2,1)} fusion(bf16[32,64,4096]{2,0,1:T(8,128)(2,1)} %fusion.74, bf16[32,64,4096]{2,0,1:T(8,128)(2,1)} %fusion.75, f32[32,4096]{1,0:T(8,128)S(1)} %mul.113), kind=kOutput, calls=%fused_computation.12.clone.1 | convolution fusion | flops 1099038720 | bytes 34340864 | tf_op jit(solution)/shard_map/while/body/eval_jaxpr/bmc,bnc->bmn/dot_general | solution.py:115
  1054.6 8.2 fusion.74
  1062.8 8.2 fusion.75
  1071.0 32.6 %fusion.79 = bf16[32,64,64]{2,1,0:T(8,128)(2,1)} fusion(bf16[32,64,4096]{2,0,1:T(8,128)(2,1)} %fusion.74, bf16[32,64,4096]{2,0,1:T(8,128)(2,1)} %fusion.75, f32[32,4096]{1,0:T(8,128)S(1)} %mul.113), kind=kOutput, calls=%fused_computation.12.clone.1 | convolution fusion | flops 1099038720 | bytes 34340864 | tf_op jit(solution)/shard_map/while/body/eval_jaxpr/bmc,bnc->bmn/dot_general | solution.py:115
  1110.9 8.2 fusion.74
  1119.1 8.2 fusion.75
  1127.3 32.6 %fusion.79 = bf16[32,64,64]{2,1,0:T(8,128)(2,1)} fusion(bf16[32,64,4096]{2,0,1:T(8,128)(2,1)} %fusion.74, bf16[32,64,4096]{2,0,1:T(8,128)(2,1)} %fusion.75, f32[32,4096]{1,0:T(8,128)S(1)} %mul.113), kind=kOutput, calls=%fused_computation.12.clone.1 | convolution fusion | flops 1099038720 | bytes 34340864 | tf_op jit(solution)/shard_map/while/body/eval_jaxpr/bmc,bnc->bmn/dot_general | solution.py:115
  1167.3 8.2 fusion.74
  1175.5 8.2 fusion.75
  1183.7 32.6 %fusion.79 = bf16[32,64,64]{2,1,0:T(8,128)(2,1)} fusion(bf16[32,64,4096]{2,0,1:T(8,128)(2,1)} %fusion.74, bf16[32,64,4096]{2,0,1:T(8,128)(2,1)} %fusion.75, f32[32,4096]{1,0:T(8,128)S(1)} %mul.113), kind=kOutput, calls=%fused_computation.12.clone.1 | convolution fusion | flops 1099038720 | bytes 34340864 | tf_op jit(solution)/shard_map/while/body/eval_jaxpr/bmc,bnc->bmn/dot_general | solution.py:115
  1218.5 4.4 all_to_all.24
  1222.9 10.0 all-to-all-start.2
  1232.9 29.8 %all-to-all-done.2 = bf16[128,2,4096]{2,1,0:T(2,128)(2,1)} async-done(((bf16[128,2,4096]{2,1,0:T(2,128)(2,1)}), bf16[128,2,4096]{2,1,0:T(2,128)(2,1)}, u32[]{:S(2)}, u32[]{:S(2)}) %all-to-all-start.2) | async-done | bytes 2097184 | tf_op jit(solution)/shard_map/all_to_all | solution.py:122
  1262.7 2.7 all_to_all.26
  (192 shorter events, 102.6 us)
Async XLA Ops:
  3.0 18.9 %copy-start.3 = (s32[64]{0:T(128)}, s32[64]{0:T(128)S(1)}, u32[]{:S(2)}) copy-start(s32[64]{0:T(128)S(1)} %fusion.38) | copy-start | bytes 772
  5.1 21.4 %all-to-all-start = ((s32[128,2,4]{2,1,0:T(2,128)}), s32[128,2,4]{2,1,0:T(2,128)S(1)}, u32[]{:S(2)}, u32[]{:S(2)}) async-start(s32[128,2,4]{2,1,0:T(2,128)} %bitcast.14), calls=%async_computation | async-start | bytes 262144 | tf_op jit(solution)/shard_map/all_to_all | solution.py:67
  26.6 35.4 %all-to-all-start.1 = ((bf16[128,2,4096]{2,1,0:T(2,128)(2,1)}), bf16[128,2,4096]{2,1,0:T(2,128)(2,1)}, u32[]{:S(2)}, u32[]{:S(2)}) async-start(bf16[128,2,4096]{2,1,0:T(2,128)(2,1)} %all_to_all.22), calls=%async_computation.1 | async-start | bytes 4194304 | tf_op jit(solution)/shard_map/all_to_all | solution.py:64
  32.2 37.6 %copy-start = (bf16[4,64,4096]{2,1,0:T(8,128)(2,1)S(1)}, bf16[4,64,4096]{2,1,0:T(8,128)(2,1)}, u32[]{:S(2)}) copy-start(bf16[4,64,4096]{2,1,0:T(8,128)(2,1)} %param.16) | copy-start | bytes 6291460
  69.8 688.8 %copy-start.2 = (f32[8,4096]{1,0:T(8,128)S(1)}, f32[8,4096]{1,0:T(8,128)}, u32[]{:S(2)}) copy-start(f32[8,4096]{1,0:T(8,128)} %param.17) | copy-start | bytes 393220
  755.4 3.1 collective-permute-start
  758.6 9.0 copy-start.1
  758.7 8.9 collective-permute-start.1
  1222.9 10.0 copy-start.4
  1222.9 39.9 %all-to-all-start.2 = ((bf16[128,2,4096]{2,1,0:T(2,128)(2,1)}), bf16[128,2,4096]{2,1,0:T(2,128)(2,1)}, u32[]{:S(2)}, u32[]{:S(2)}) async-start(bf16[128,2,4096]{2,1,0:T(2,128)(2,1)} %all_to_all.24), calls=%async_computation.2 | async-start | bytes 4194304 | tf_op jit(solution)/shard_map/all_to_all | solution.py:122
where the time goes:
time: 1270 us
  matrix products  1010 us (80%)
  local copies, waits for them, and re-layouts  85.4 us (7%)
  waiting for transfers between devices  67 us (5%)
  loops' own time  38.6 us (3%)
  starting transfers between devices  36.2 us (3%)
  other arithmetic  30.4 us (2%)
    dot_general x8, matrix products, deposit(): jnp.einsum('bmn,bnc->bmc', block_batch, col_basis, preferred_element_type...  477 us
    dot_general x32, matrix products, pick_basis(): jnp.einsum('bk,knc->bnc', kind_hot, basis, preferred_element_type=jnp.flo...  262 us
    dot_general x8, matrix products, integrate(): jnp.einsum('bmc,bnc->bmn', weighted, col_basis, preferred_element_type=jn...  261 us
    mul x16, local copies, waits for them, and re-layouts, placement(): place = plane_hot[:, :, :, None] * seg_hot[:, None, None, :]  42.3 us
    another operation x1, loops' own time, local(): lax.scan(deposit, jnp.zeros((extended_rows, SEGW), jnp.float32), (block_b...  38.3 us
    all_to_all x1, waiting for transfers between devices, local(): lax.all_to_all(matrix_slots, ('rows', 'cols', 'slab'), split_axis=0, conc...  29.8 us
    all_to_all x1, waiting for transfers between devices, local(): lax.all_to_all(send_blocks, ('rows', 'cols', 'slab'), split_axis=0, conca...  29.7 us
    mul x16, other arithmetic, placement(): place = plane_hot[:, :, :, None] * seg_hot[:, None, None, :]  25.7 us
  transfers between devices with their start and end apart: 5, of which 5 were waited for; matrix products, arithmetic and copies ran while one was open for 0% of the time, Pallas kernels for 0%

commit v1 on v0

v1 whole, which is shorter than its diff:
```python
import jax
import jax.numpy as jnp
from jax import lax
from jax.experimental import pallas as pl
from jax.experimental.pallas import tpu as pltpu
from jax.sharding import PartitionSpec as P

AXES = ("rows", "cols", "slab")
F32 = jnp.float32
BF16 = jnp.bfloat16
NB = 64
BS = 64
KINDS = 4
CZB = 8
SEGW = 512
SEGS = 8
DEVS = 128
CELLS = CZB * SEGW
PLANE = SEGS * SEGW
LANES = 128
LPS = SEGW // LANES
GROUP = 8
SENDW = 2 * SEGW + LANES

SMEM = pl.BlockSpec(memory_space=pltpu.SMEM)
VMEM = pl.BlockSpec(memory_space=pltpu.VMEM)


def whole(shape):
    return pl.BlockSpec(shape, lambda i: (0,) * len(shape))


def tiles_kernel(
    owner, plane, seg, kinds, dens_ref, basis_ref, out_ref, pn, lhs, a32, tiles, idx
):
    i = pl.program_id(0)

    @pl.when(i == 0)
    def _():
        @pl.loop(0, 2 * DEVS)
        def _(o):
            idx[o] = NB

        @pl.loop(0, NB)
        def _(b):
            o = owner[b, 0]
            first = idx[2 * o]
            second = idx[2 * o + 1]
            free = first == NB
            idx[2 * o] = jnp.where(free, b, first)
            idx[2 * o + 1] = jnp.where(free, second, b)

        for j in range(BS // 2):
            x = dens_ref[:, LANES * j : LANES * (j + 1)].astype(F32)
            pn[pl.ds(2 * j, NB, stride=BS), :] = x
            pn[pl.ds(2 * j + 1, NB, stride=BS), :] = pltpu.roll(x, BS, 1)
        low = lax.broadcasted_iota(jnp.int32, (BS, LANES), 1) < BS

        @pl.loop(0, NB)
        def _(b):
            rows = pl.ds(pl.multiple_of(b * BS, BS), BS)
            kb = kinds[b, 1]
            v = jnp.where(low, pn[rows, :], 0.0)
            v = jnp.where(kb % 2 == 1, pltpu.roll(v, BS, 1), v)
            lhs[rows, 0:LANES] = jnp.where(kb < 2, v, 0.0).astype(BF16)
            lhs[rows, LANES : 2 * LANES] = jnp.where(kb < 2, 0.0, v).astype(BF16)

        tiles[pl.ds(NB * CZB, CZB), :] = jnp.zeros((CZB, SEGW), F32)

    a32[...] = basis_ref[...].reshape(KINDS * BS, SEGW).astype(F32)

    @pl.loop(0, NB // GROUP)
    def _(g):
        rows = pl.ds(pl.multiple_of(g * GROUP * BS, GROUP * BS), GROUP * BS)
        half = jnp.dot(
            lhs[rows, :],
            basis_ref[...].reshape(KINDS * BS, SEGW),
            preferred_element_type=F32,
        )
        for t in range(GROUP):
            b = g * GROUP + t
            a = a32[pl.ds(pl.multiple_of(kinds[b, 0] * BS, BS), BS), :]
            part = jnp.sum(a * half[t * BS : (t + 1) * BS], axis=0, keepdims=True)
            tiles[pl.ds(b * CZB + i, 1), :] = part

    @pl.when(i == CZB - 1)
    def _():
        lane = lax.broadcasted_iota(jnp.int32, (CZB, LANES), 1)

        @pl.loop(0, DEVS // 2)
        def _(q):
            rows = pl.ds(pl.multiple_of(q * 16, 16), 16)
            slots = [idx[4 * q + r] for r in range(4)]
            parts = [tiles[pl.ds(pl.multiple_of(b * CZB, CZB), CZB), :] for b in slots]
            codes = []
            for b in slots:
                held = jnp.minimum(b, NB - 1)
                codes.append((plane[held] * SEGS + seg[held]).astype(F32))
            marks = [
                jnp.where(lane == 0, codes[2 * r], jnp.where(lane == 1, codes[2 * r + 1], 0.0))
                for r in range(2)
            ]
            out_ref[rows, 0:SEGW] = jnp.concatenate([parts[0], parts[2]], axis=0).astype(BF16)
            out_ref[rows, SEGW : 2 * SEGW] = jnp.concatenate(
                [parts[1], parts[3]], axis=0
            ).astype(BF16)
            out_ref[rows, 2 * SEGW :] = jnp.concatenate(marks, axis=0).astype(BF16)


def gather_kernel(got_ref, ext_ref, own_ref, rim_ref, half_ref, code_ref, marks, codes, acc, sem):
    marks[...] = got_ref[:, 2 * SEGW :].astype(F32)
    across = marks[pl.ds(0, DEVS, stride=CZB), :].T
    codes[...] = across[0:8, :].astype(jnp.int32)
    copy = pltpu.make_async_copy(codes, code_ref, sem)
    copy.start()
    acc[...] = jnp.zeros_like(acc)
    copy.wait()

    @pl.loop(0, DEVS // 2)
    def _(q):
        rows = pl.ds(pl.multiple_of(q * 16, 16), 16)
        for r in range(2):
            both = got_ref[rows, r * SEGW : (r + 1) * SEGW].astype(F32)
            for t in range(2):
                code = code_ref[r, 2 * q + t]
                p = code // SEGS
                s = code % SEGS
                for l in range(LPS):
                    at = (s * LPS + l, pl.ds(p, CZB), slice(None))
                    acc[at] = acc[at] + both[t * CZB : (t + 1) * CZB, l * LANES : (l + 1) * LANES]

    for l in range(PLANE // LANES):
        cells = slice(l * LANES, (l + 1) * LANES)
        own = acc[l, 0:CZB, :]
        own_ref[:, cells] = own
        rim_ref[:, cells] = acc[l, CZB : 2 * CZB, :]
        half_ref[:, cells] = ext_ref[:, cells] + 0.5 * own


def cubes_kernel(code_ref, own_ref, rim_ref, ext_ref, below_ref, above_ref, dens_ref, out_ref, pot):
    for l in range(PLANE // LANES):
        cells = slice(l * LANES, (l + 1) * LANES)
        density = own_ref[:, cells] + below_ref[:, cells]
        dens_ref[:, cells] = density
        pot[l, 0:CZB, :] = ext_ref[:, cells] + 0.5 * density
        pot[l, CZB : 2 * CZB, :] = above_ref[:, cells] + 0.5 * rim_ref[:, cells]

    @pl.loop(0, DEVS)
    def _(d):
        rows = pl.ds(pl.multiple_of(d * 16, 16), 16)
        c0 = code_ref[0, d]
        c1 = code_ref[1, d]
        for l in range(LPS):
            first = pot[(c0 % SEGS) * LPS + l, pl.ds(c0 // SEGS, CZB), :]
            second = pot[(c1 % SEGS) * LPS + l, pl.ds(c1 // SEGS, CZB), :]
            out_ref[rows, l * LANES : (l + 1) * LANES] = jnp.concatenate(
                [first, second], axis=0
            ).astype(BF16)


def matrix_kernel(owner, kinds, ret_ref, basis_ref, out_ref, acc, pot, vn, seen, base):
    i = pl.program_id(0)

    @pl.when(i == 0)
    def _():
        @pl.loop(0, DEVS)
        def _(o):
            seen[o] = 0

        @pl.loop(0, NB)
        def _(b):
            o = owner[b, 0]
            rank = seen[o]
            seen[o] = rank + 1
            base[b] = b * 16 + rank * CZB
            pot[pl.ds(pl.multiple_of(b * 16, 16), 16), :] = ret_ref[
                pl.ds(pl.multiple_of(o * 16, 16), 16), :
            ].astype(F32)

        acc[...] = jnp.zeros_like(acc)

    @pl.loop(0, NB // GROUP)
    def _(g):
        rows = pl.ds(pl.multiple_of(g * GROUP * BS, GROUP * BS), GROUP * BS)
        parts = []
        for t in range(GROUP):
            b = g * GROUP + t
            cell = jnp.broadcast_to(pot[pl.ds(base[b] + i, 1), :], (BS, SEGW)).astype(BF16)
            parts.append(basis_ref[kinds[b, 0]] * cell)
        weighted = jnp.concatenate(parts, axis=0)
        acc[rows, :] = acc[rows, :] + lax.dot_general(
            weighted,
            basis_ref[...].reshape(KINDS * BS, SEGW),
            (((1,), (1,)), ((), ())),
            preferred_element_type=F32,
        )

    @pl.when(i == CZB - 1)
    def _():
        @pl.loop(0, NB)
        def _(b):
            rows = pl.ds(pl.multiple_of(b * BS, BS), BS)
            kb = kinds[b, 1]
            v = jnp.where(kb < 2, acc[rows, 0:LANES], acc[rows, LANES : 2 * LANES])
            vn[rows, :] = jnp.where(kb % 2 == 1, pltpu.roll(v, BS, 1), v)

        low = lax.broadcasted_iota(jnp.int32, (NB, LANES), 1) < BS
        for j in range(BS // 2):
            even = vn[pl.ds(2 * j, NB, stride=BS), :]
            odd = pltpu.roll(vn[pl.ds(2 * j + 1, NB, stride=BS), :], BS, 1)
            out_ref[:, LANES * j : LANES * (j + 1)] = jnp.where(low, even, odd).astype(BF16)


def make_tiles(owner, plane, seg, kinds, density_blocks, basis):
    return pl.pallas_call(
        tiles_kernel,
        grid=(CZB,),
        in_specs=[
            SMEM,
            SMEM,
            SMEM,
            SMEM,
            whole((NB, BS * BS)),
            pl.BlockSpec((KINDS, BS, SEGW), lambda i: (0, 0, i)),
        ],
        out_specs=whole((DEVS * CZB, SENDW)),
        out_shape=jax.ShapeDtypeStruct((DEVS * CZB, SENDW), BF16),
        scratch_shapes=[
            pltpu.VMEM((NB * BS, LANES), F32),
            pltpu.VMEM((NB * BS, KINDS * BS), BF16),
            pltpu.VMEM((KINDS * BS, SEGW), F32),
            pltpu.VMEM(((NB + 1) * CZB, SEGW), F32),
            pltpu.SMEM((2 * DEVS,), jnp.int32),
        ],
        name="tiles",
    )(owner, plane, seg, kinds, density_blocks, basis)


def gather_tiles(got, ext_potential):
    slab = jax.ShapeDtypeStruct((CZB, PLANE), F32)
    return pl.pallas_call(
        gather_kernel,
        in_specs=[VMEM, VMEM],
        out_specs=[VMEM, VMEM, VMEM, SMEM],
        out_shape=[slab, slab, slab, jax.ShapeDtypeStruct((8, DEVS), jnp.int32)],
        scratch_shapes=[
            pltpu.VMEM((DEVS * CZB, LANES), F32),
            pltpu.VMEM((8, DEVS), jnp.int32),
            pltpu.VMEM((PLANE // LANES, 2 * CZB, LANES), F32),
            pltpu.SemaphoreType.DMA,
        ],
        name="gather_tiles",
    )(got, ext_potential)


def cut_cubes(codes, own, rim, ext_potential, below, above):
    return pl.pallas_call(
        cubes_kernel,
        in_specs=[SMEM] + [VMEM] * 5,
        out_specs=[VMEM, VMEM],
        out_shape=[
            jax.ShapeDtypeStruct((CZB, PLANE), F32),
            jax.ShapeDtypeStruct((DEVS * 16, SEGW), BF16),
        ],
        scratch_shapes=[pltpu.VMEM((PLANE // LANES, 2 * CZB, LANES), F32)],
        name="cut_cubes",
    )(codes, own, rim, ext_potential, below, above)


def make_matrices(owner, kinds, returned, basis):
    return pl.pallas_call(
        matrix_kernel,
        grid=(CZB,),
        in_specs=[
            SMEM,
            SMEM,
            whole((DEVS * 16, SEGW)),
            pl.BlockSpec((KINDS, BS, SEGW), lambda i: (0, 0, i)),
        ],
        out_specs=whole((NB, BS * BS)),
        out_shape=jax.ShapeDtypeStruct((NB, BS * BS), BF16),
        scratch_shapes=[
            pltpu.VMEM((NB * BS, KINDS * BS), F32),
            pltpu.VMEM((NB * 16, SEGW), F32),
            pltpu.VMEM((NB * BS, LANES), F32),
            pltpu.SMEM((DEVS,), jnp.int32),
            pltpu.SMEM((NB,), jnp.int32),
        ],
        name="matrices",
    )(owner, kinds, returned, basis)


def shifted(x, by):
    size = lax.axis_size(AXES)
    return lax.ppermute(x, AXES, [(i, (i + by) % size) for i in range(size)])


def exchanged(x):
    return lax.all_to_all(x, AXES, split_axis=0, concat_axis=0, tiled=True)


def local(
    density_blocks, block_owner, block_plane, block_segment, block_kinds, basis, ext_potential
):
    sent = make_tiles(
        block_owner, block_plane, block_segment, block_kinds, density_blocks, basis
    )
    own, rim, half, codes = gather_tiles(exchanged(sent), ext_potential)
    below = shifted(rim, 1)
    above = shifted(half, -1)
    density, cubes = cut_cubes(codes, own, rim, ext_potential, below, above)
    matrices = make_matrices(block_owner, block_kinds, exchanged(cubes), basis)
    return density, matrices


def solution(mesh):
    rows = P(AXES, None)
    flat = P(AXES)
    return jax.shard_map(
        local,
        mesh=mesh,
        in_specs=(rows, rows, flat, flat, rows, P(), rows),
        out_specs=(rows, rows),
        check_vma=False,
    )
```

time: 1270 us -> 173 us (0.14)
  matrix products: 1010 us -> 0 us
  blocking collectives: 0 us -> 86.6 us
  local copies, waits for them, and re-layouts: 85.4 us -> 3.42 us
  Pallas kernels: 0 us -> 76.9 us
  waiting for transfers between devices: 67 us -> 2.86 us
  loops' own time: 38.6 us -> 0 us
  starting transfers between devices: 36.2 us -> 1.81 us
  other arithmetic: 30.4 us -> 0 us
    dot_general x64 -> x0, matrix products: 1010 us -> none  [the longest x8 477 us: deposit(): jnp.einsum('bmn,bnc->bmc', block_batch, col_basis, preferred_element_type...]
    all_to_all x0 -> x2, blocking collectives: none -> 86.6 us  [exchanged(): return lax.all_to_all(x, AXES, split_axis=0, concat_axis=0, tiled=True)]
    pallas_call x0 -> x4, Pallas kernels: none -> 76.9 us  [the longest x1 34.3 us: make_tiles(): pl.pallas_call(tiles_kernel, grid=(CZB,), in_specs=[SMEM, SMEM, SMEM, SME...]
    all_to_all x3 -> x0, waiting for transfers between devices: 64.2 us -> none  [the longest x1 29.8 us: local(): lax.all_to_all(matrix_slots, ('rows', 'cols', 'slab'), split_axis=0, conc...]
    mul x24 -> x0, local copies, waits for them, and re-layouts: 43.1 us -> none  [the longest x16 42.3 us: placement(): place = plane_hot[:, :, :, None] * seg_hot[:, None, None, :]]
    another operation x2 -> x0, loops' own time: 38.6 us -> none  [the longest x1 38.3 us: local(): lax.scan(deposit, jnp.zeros((extended_rows, SEGW), jnp.float32), (block_b...]
    all_to_all x3 -> x0, starting transfers between devices: 27 us -> none  [the longest x1 11.5 us: local(): lax.all_to_all(send_meta, ('rows', 'cols', 'slab'), split_axis=0, concat_...]
    mul x16 -> x0, other arithmetic: 25.7 us -> none  [placement(): place = plane_hot[:, :, :, None] * seg_hot[:, None, None, :]]
  transfers between devices with their start and end apart: 5 -> 2, of which waited for: 5 -> 1; matrix products, arithmetic and copies ran while one was open for 0% -> 0% of each run, Pallas kernels for 0% -> 0%
where the time goes in v1:
time: 173 us; the launch traced here: 172 us
  blocking collectives  86.6 us (50%)
  Pallas kernels  76.9 us (44%)
  local copies, waits for them, and re-layouts  3.42 us (2%)
  waiting for transfers between devices  2.86 us (2%)
  starting transfers between devices  1.81 us (1%)
    all_to_all x2, blocking collectives, exchanged(): return lax.all_to_all(x, AXES, split_axis=0, concat_axis=0, tiled=True)  86.6 us
    pallas_call x1, Pallas kernels, make_tiles(): pl.pallas_call(tiles_kernel, grid=(CZB,), in_specs=[SMEM, SMEM, SMEM, SME...  34.3 us
    pallas_call x1, Pallas kernels, make_matrices(): pl.pallas_call(matrix_kernel, grid=(CZB,), in_specs=[SMEM, SMEM, whole((D...  32.2 us
    pallas_call x1, Pallas kernels, gather_tiles(): pl.pallas_call(gather_kernel, in_specs=[VMEM, VMEM], out_specs=[VMEM, VME...  5.27 us
    pallas_call x1, Pallas kernels, cut_cubes(): pl.pallas_call(cubes_kernel, in_specs=[SMEM] + [VMEM] * 5, out_specs=[VME...  5.15 us
  transfers between devices with their start and end apart: 2, of which 1 were waited for; matrix products, arithmetic and copies ran while one was open for 0% of the time, Pallas kernels for 0%

profile of v1, /device:TPU:1, one launch (start us, length us, event | category | flops | bytes accessed | tf_op | source)
XLA Modules:
  0.0 172.2 jit_solution(854298608003479126)
XLA Ops:
  0.6 1.4 copy.9.owner
  2.0 1.4 copy.10.kinds
  3.3 34.3 %tiles.1 = bf16[1024,1152]{1,0:T(8,128)(2,1)} custom-call(s32[64,1]{1,0:T(8,128)} %copy.9.owner, s32[64]{0:T(128)} %plane.1, s32[64]{0:T(128)} %seg.1, s32[64,2]{1,0:T(8,128)} %copy.10.kinds, bf16[64,4096]{1,0:T(8,128)(2,1)} %dens_ref.1, bf16[4,64,4096]{2,1,0:T(8,128)(2,1)} %basis_ref.3), custom_call_target="tpu_custom_call" | custom-call | tf_op jit(solution)/shard_map/tiles/pallas_call | solution.py:215
  37.6 44.7 %all_to_all.22 = bf16[128,8,1152]{2,1,0:T(8,128)(2,1)} all-to-all(bf16[128,8,1152]{2,1,0:T(8,128)(2,1)} %bitcast.5), channel_id=1, replica_groups=mesh['rows'=16,'cols'=4,'slab'=2] {'rows','cols','slab'}, dimensions={0} | all-to-all | bytes 4718592 | tf_op jit(solution)/shard_map/all_to_all | solution.py:299
  82.3 5.3 %gather_tiles.1 = (f32[8,4096]{1,0:T(8,128)}, f32[8,4096]{1,0:T(8,128)}, f32[8,4096]{1,0:T(8,128)}, s32[8,128]{1,0:T(8,128)}) custom-call(bf16[1024,1152]{1,0:T(8,128)(2,1)} %bitcast.4, f32[8,4096]{1,0:T(8,128)} %ext_ref.3), custom_call_target="tpu_custom_call" | custom-call | tf_op jit(solution)/shard_map/gather_tiles/pallas_call | solution.py:241
  87.6 1.3 collective-permute-start.1
  88.9 0.5 collective-permute-start
  89.4 2.9 %collective-permute-done.1.above_ref = f32[8,4096]{1,0:T(8,128)S(1)} collective-permute-done((f32[8,4096]{1,0:T(8,128)}, f32[8,4096]{1,0:T(8,128)S(1)}, u32[]{:S(2)}, u32[]{:S(2)}) %collective-permute-start.1) | collective-permute-done | bytes 131104 | tf_op jit(solution)/shard_map/ppermute | solution.py:295
  92.2 0.0 copy-start
  92.2 0.0 collective-permute-done.below_ref
  92.2 0.0 copy-start.1
  92.2 0.6 copy-done
  92.9 0.1 copy-done.1
  92.9 5.1 %cut_cubes.1 = (f32[8,4096]{1,0:T(8,128)}, bf16[2048,512]{1,0:T(8,128)(2,1)}) custom-call(s32[8,128]{1,0:T(8,128)} %get-tuple-element.8.code_ref, f32[8,4096]{1,0:T(8,128)} %get-tuple-element.9.own_ref, f32[8,4096]{1,0:T(8,128)} %get-tuple-element.10.rim_ref, f32[8,4096]{1,0:T(8,128)} %ext_ref.3, f32[8,4096]{1,0:T(8,128)} %copy-done.1, f32[8,4096]{1,0:T(8,128)} %copy-done), custom_call_target="tpu_custom_call" | custom-call | tf_op jit(solution)/shard_map/cut_cubes/pallas_call | solution.py:257
  98.1 42.0 %all_to_all.23 = bf16[128,16,512]{2,1,0:T(8,128)(2,1)} all-to-all(bf16[128,16,512]{2,1,0:T(8,128)(2,1)} %bitcast.7), channel_id=1, replica_groups=mesh['rows'=16,'cols'=4,'slab'=2] {'rows','cols','slab'}, dimensions={0} | all-to-all | bytes 4194304 | tf_op jit(solution)/shard_map/all_to_all | solution.py:299
  140.1 32.2 %matrices.1 = bf16[64,4096]{1,0:T(8,128)(2,1)} custom-call(s32[64,1]{1,0:T(8,128)} %copy.9.owner, s32[64,2]{1,0:T(8,128)} %copy.10.kinds, bf16[2048,512]{1,0:T(8,128)(2,1)} %bitcast.6, bf16[4,64,4096]{2,1,0:T(8,128)(2,1)} %basis_ref.3), custom_call_target="tpu_custom_call" | custom-call | tf_op jit(solution)/shard_map/matrices/pallas_call | solution.py:271
Async XLA Ops:
  87.6 4.7 %collective-permute-start.1 = (f32[8,4096]{1,0:T(8,128)}, f32[8,4096]{1,0:T(8,128)S(1)}, u32[]{:S(2)}, u32[]{:S(2)}) collective-permute-start(f32[8,4096]{1,0:T(8,128)} %get-tuple-element.11), channel_id=1, source_target_pairs={{0,127},{1,0},{2,1},{3,2},{4,3},{5,4},{6,5},{7,6},{8,7},{9,8},{10,... | collective-permute-start | bytes 393224 | tf_op jit(solution)/shard_map/ppermute | solution.py:295
  88.9 3.4 %collective-permute-start = (f32[8,4096]{1,0:T(8,128)}, f32[8,4096]{1,0:T(8,128)S(1)}, u32[]{:S(2)}, u32[]{:S(2)}) collective-permute-start(f32[8,4096]{1,0:T(8,128)} %get-tuple-element.10.rim_ref), channel_id=1, source_target_pairs={{0,1},{1,2},{2,3},{3,4},{4,5},{5,6},{6,7},{7,8},{8,9},{9,10},{10,1... | collective-permute-start | bytes 393224 | tf_op jit(solution)/shard_map/ppermute | solution.py:295
  92.2 0.6 copy-start
  92.2 0.7 copy-start.1

commit v2 on v1

v2 whole, which is shorter than its diff:
```python
import jax
import jax.numpy as jnp
from jax import lax
from jax.experimental import pallas as pl
from jax.experimental.pallas import tpu as pltpu
from jax.sharding import PartitionSpec as P

AXES = ("rows", "cols", "slab")
F32 = jnp.float32
BF16 = jnp.bfloat16
NB = 64
BS = 64
KINDS = 4
CZB = 8
SEGW = 512
SEGS = 8
DEVS = 128
PLANE = SEGS * SEGW
LANES = 128
HALVES = 2
HALF = SEGW // HALVES
LPS = HALF // LANES
STEPS = CZB // 2
GROUP = 32

SMEM = pl.BlockSpec(memory_space=pltpu.SMEM)
VMEM = pl.BlockSpec(memory_space=pltpu.VMEM)


def whole(shape):
    return pl.BlockSpec(shape, lambda i: (0,) * len(shape))


def basis_specs(h):
    def spec(t):
        return pl.BlockSpec((KINDS, BS, HALF), lambda i: (0, 0, (2 * i + t) * HALVES + h))

    return [spec(0), spec(1)]


def cost(flops, moved):
    return pl.CostEstimate(flops=flops, bytes_accessed=moved, transcendentals=0)


def joined(first, second):
    parts = [ref[...].reshape(KINDS * BS, HALF) for ref in (first, second)]
    return jnp.concatenate(parts, axis=1)


def even_rows_first():
    shape = (KINDS * BS, KINDS * BS)
    to = lax.broadcasted_iota(jnp.int32, shape, 0)
    source = lax.broadcasted_iota(jnp.int32, shape, 1)
    row = to & (BS - 1)
    half = BS // 2
    wanted = (to - row) + jnp.where(row < half, 2 * row, 2 * (row - half) + 1)
    return jnp.where(source == wanted, 1.0, 0.0).astype(BF16)


def tiles_kernel(
    h, owner, plane, seg, kinds, dens_ref, first, second, out_ref, pn, lhs, a32, perm, tiles, idx
):
    i = pl.program_id(0)
    pairs = BS // 2

    @pl.when(i == 0)
    def _():
        @pl.loop(0, 2 * DEVS, unroll=16)
        def _(o):
            idx[o] = NB

        @pl.loop(0, NB, unroll=4)
        def _(b):
            o = owner[b, 0]
            was = idx[2 * o]
            after = idx[2 * o + 1]
            free = was == NB
            idx[2 * o] = jnp.where(free, b, was)
            idx[2 * o + 1] = jnp.where(free, after, b)

        perm[...] = even_rows_first()
        pn[...] = dens_ref[...].astype(F32).reshape(NB, pairs, LANES)
        low = lax.broadcasted_iota(jnp.int32, (pairs, LANES), 1) < BS

        @pl.loop(0, NB, unroll=4)
        def _(b):
            rows = pl.ds(pl.multiple_of(b * BS, BS), BS)
            kb = kinds[b, 1]
            odd = (kb & 1) == 1
            v = pn[b]
            r = pltpu.roll(v, BS, 1)
            keep = low != odd
            evens = jnp.where(keep, jnp.where(odd, r, v), 0.0)
            odds = jnp.where(keep, jnp.where(odd, v, r), 0.0)
            v = jnp.concatenate([evens, odds], axis=0)
            lhs[rows, 0:LANES] = jnp.where(kb < 2, v, 0.0).astype(BF16)
            lhs[rows, LANES : 2 * LANES] = jnp.where(kb < 2, 0.0, v).astype(BF16)

        tiles[pl.ds(NB * CZB, CZB), :] = jnp.zeros((CZB, HALF), F32)

    a32[...] = jnp.dot(perm[...], joined(first, second), preferred_element_type=F32)

    @pl.loop(0, NB // GROUP)
    def _(g):
        rows = pl.ds(pl.multiple_of(g * GROUP * BS, GROUP * BS), GROUP * BS)
        half = jnp.dot(lhs[rows, :], joined(first, second), preferred_element_type=F32)
        for t in range(GROUP):
            b = g * GROUP + t
            a = a32[pl.ds(pl.multiple_of(kinds[b, 0] * BS, BS), BS), :]
            part = jnp.sum(a * half[t * BS : (t + 1) * BS], axis=0, keepdims=True)
            tiles[pl.ds(b * CZB + 2 * i, 1), :] = part[:, :HALF]
            tiles[pl.ds(b * CZB + 2 * i + 1, 1), :] = part[:, HALF:]

    @pl.when(i == STEPS - 1)
    def _():
        lane = lax.broadcasted_iota(jnp.int32, (CZB, LANES), 1)

        @pl.loop(0, DEVS // 2, unroll=4)
        def _(q):
            rows = pl.ds(pl.multiple_of(q * 16, 16), 16)
            slots = [idx[4 * q + r] for r in range(4)]
            parts = [tiles[pl.ds(pl.multiple_of(b * CZB, CZB), CZB), :] for b in slots]
            out_ref[rows, 0:HALF] = jnp.concatenate([parts[0], parts[2]], axis=0).astype(BF16)
            out_ref[rows, HALF : 2 * HALF] = jnp.concatenate(
                [parts[1], parts[3]], axis=0
            ).astype(BF16)
            if h == 0:
                codes = []
                for b in slots:
                    held = jnp.minimum(b, NB - 1)
                    codes.append((plane[held] * SEGS + seg[held]).astype(F32))
                marks = [
                    jnp.where(lane == 0, codes[2 * r], jnp.where(lane == 1, codes[2 * r + 1], 0.0))
                    for r in range(2)
                ]
                out_ref[rows, 2 * HALF :] = jnp.concatenate(marks, axis=0).astype(BF16)


def spread(at_ref, got_ref, ext_ref, own_ref, rim_ref, half_ref, acc, h):
    acc[...] = jnp.zeros_like(acc)

    @pl.loop(0, DEVS // 2, unroll=2)
    def _(q):
        rows = pl.ds(pl.multiple_of(q * 16, 16), 16)
        for r in range(2):
            both = got_ref[rows, r * HALF : (r + 1) * HALF].astype(F32)
            for t in range(2):
                p = at_ref[r, 2 * q + t]
                s = at_ref[2 + r, 2 * q + t]
                for l in range(LPS):
                    at = (s + l, pl.ds(p, CZB), slice(None))
                    acc[at] = acc[at] + both[t * CZB : (t + 1) * CZB, l * LANES : (l + 1) * LANES]

    for s in range(SEGS):
        for l in range(LPS):
            n = s * LPS + l
            cells = slice(n * LANES, (n + 1) * LANES)
            grid = slice(s * SEGW + h * HALF + l * LANES, s * SEGW + h * HALF + (l + 1) * LANES)
            own = acc[n, 0:CZB, :]
            own_ref[:, cells] = own
            rim_ref[:, cells] = acc[n, CZB : 2 * CZB, :]
            half_ref[:, cells] = ext_ref[:, grid] + 0.5 * own


def gather_first(got_ref, ext_ref, own_ref, rim_ref, half_ref, at_ref, marks, places, acc, sem):
    marks[...] = got_ref[:, 2 * HALF :].astype(F32)
    across = marks[pl.ds(0, DEVS, stride=CZB), :].T
    codes = across[0:2, :].astype(jnp.int32)
    places[0:2, :] = codes >> 3
    places[2:4, :] = (codes & 7) * LPS
    copy = pltpu.make_async_copy(places, at_ref, sem)
    copy.start()
    copy.wait()
    spread(at_ref, got_ref, ext_ref, own_ref, rim_ref, half_ref, acc, 0)


def gather_second(at_ref, got_ref, ext_ref, own_ref, rim_ref, half_ref, acc):
    spread(at_ref, got_ref, ext_ref, own_ref, rim_ref, half_ref, acc, 1)


def cubes_kernel(h, at_ref, own_ref, rim_ref, ext_ref, below_ref, above_ref, *rest):
    if h == 0:
        dens_ref, out_ref, pot = rest
    else:
        other_ref, dens_ref, out_ref, pot = rest
    for s in range(SEGS):
        for l in range(LPS):
            n = s * LPS + l
            cells = slice(n * LANES, (n + 1) * LANES)
            grid = slice(s * SEGW + h * HALF + l * LANES, s * SEGW + h * HALF + (l + 1) * LANES)
            density = own_ref[:, cells] + below_ref[:, cells]
            if h == 0:
                dens_ref[:, cells] = density
            else:
                dens_ref[:, grid] = density
                dens_ref[:, s * SEGW + l * LANES : s * SEGW + (l + 1) * LANES] = other_ref[:, cells]
            pot[n, 0:CZB, :] = ext_ref[:, grid] + 0.5 * density
            pot[n, CZB : 2 * CZB, :] = above_ref[:, cells] + 0.5 * rim_ref[:, cells]

    @pl.loop(0, DEVS, unroll=4)
    def _(d):
        rows = pl.ds(pl.multiple_of(d * 16, 16), 16)
        for l in range(LPS):
            cubes = [pot[at_ref[2 + r, d] + l, pl.ds(at_ref[r, d], CZB), :] for r in range(2)]
            out_ref[rows, l * LANES : (l + 1) * LANES] = jnp.concatenate(cubes, axis=0).astype(BF16)


def matrix_kernel(h, owner, kinds, ret_ref, first, second, *rest):
    if h == 0:
        out_ref, acc, pot, perm, shuffled, seen, base = rest
    else:
        other_ref, out_ref, acc, pot, perm, shuffled, seen, base, vn = rest
    i = pl.program_id(0)
    pairs = BS // 2

    @pl.when(i == 0)
    def _():
        @pl.loop(0, DEVS, unroll=16)
        def _(o):
            seen[o] = 0

        @pl.loop(0, NB, unroll=4)
        def _(b):
            o = owner[b, 0]
            rank = seen[o]
            seen[o] = rank + 1
            base[b] = b * 16 + rank * CZB
            pot[pl.ds(pl.multiple_of(b * 16, 16), 16), :] = ret_ref[
                pl.ds(pl.multiple_of(o * 16, 16), 16), :
            ].astype(F32)

        perm[...] = even_rows_first()
        acc[...] = jnp.zeros_like(acc)

    shuffled[...] = jnp.dot(
        perm[...], joined(first, second), preferred_element_type=F32
    ).astype(BF16)

    @pl.loop(0, NB // GROUP)
    def _(g):
        rows = pl.ds(pl.multiple_of(g * GROUP * BS, GROUP * BS), GROUP * BS)
        parts = []
        for t in range(GROUP):
            b = g * GROUP + t
            cells = [pot[pl.ds(base[b] + 2 * i + k, 1), :] for k in range(2)]
            cell = jnp.broadcast_to(jnp.concatenate(cells, axis=1), (BS, SEGW)).astype(BF16)
            parts.append(shuffled[pl.ds(pl.multiple_of(kinds[b, 0] * BS, BS), BS), :] * cell)
        weighted = jnp.concatenate(parts, axis=0)
        acc[rows, :] = acc[rows, :] + lax.dot_general(
            weighted,
            joined(first, second),
            (((1,), (1,)), ((), ())),
            preferred_element_type=F32,
        )

    @pl.when(i == STEPS - 1)
    def _():
        low = lax.broadcasted_iota(jnp.int32, (pairs, LANES), 1) < BS

        @pl.loop(0, NB, unroll=4)
        def _(b):
            rows = pl.ds(pl.multiple_of(b * BS, BS), BS)
            kb = kinds[b, 1]
            odd = (kb & 1) == 1
            v = jnp.where(kb < 2, acc[rows, 0:LANES], acc[rows, LANES : 2 * LANES])
            r = pltpu.roll(v, BS, 1)
            evens = jnp.where(odd, r[:pairs], v[:pairs])
            odds = jnp.where(odd, v[pairs:], r[pairs:])
            block = jnp.where(low, evens, odds)
            if h == 0:
                out_ref[b] = block
            else:
                vn[b] = block + other_ref[b]

        if h == 1:
            out_ref[...] = vn[...].reshape(NB, BS * BS).astype(BF16)


def make_tiles(h, owner, plane, seg, kinds, density_blocks, basis):
    width = 2 * HALF + (LANES if h == 0 else 0)
    return pl.pallas_call(
        lambda *refs: tiles_kernel(h, *refs),
        grid=(STEPS,),
        in_specs=[SMEM, SMEM, SMEM, SMEM, whole((NB, BS * BS))] + basis_specs(h),
        out_specs=whole((DEVS * CZB, width)),
        out_shape=jax.ShapeDtypeStruct((DEVS * CZB, width), BF16),
        scratch_shapes=[
            pltpu.VMEM((NB, BS // 2, LANES), F32),
            pltpu.VMEM((NB * BS, KINDS * BS), BF16),
            pltpu.VMEM((KINDS * BS, SEGW), F32),
            pltpu.VMEM((KINDS * BS, KINDS * BS), BF16),
            pltpu.VMEM(((NB + 1) * CZB, HALF), F32),
            pltpu.SMEM((2 * DEVS,), jnp.int32),
        ],
        cost_estimate=cost(2 * NB * BS * KINDS * BS * CZB * HALF, 4 << 20),
        name=f"tiles{h}",
    )(owner, plane, seg, kinds, density_blocks, basis, basis)


def gather_tiles(h, got, ext_potential, places=None):
    part = jax.ShapeDtypeStruct((CZB, PLANE // HALVES), F32)
    acc = pltpu.VMEM((SEGS * LPS, 2 * CZB, LANES), F32)
    if h == 0:
        return pl.pallas_call(
            gather_first,
            in_specs=[VMEM, VMEM],
            out_specs=[VMEM, VMEM, VMEM, SMEM],
            out_shape=[part, part, part, jax.ShapeDtypeStruct((8, DEVS), jnp.int32)],
            scratch_shapes=[
                pltpu.VMEM((DEVS * CZB, LANES), F32),
                pltpu.VMEM((8, DEVS), jnp.int32),
                acc,
                pltpu.SemaphoreType.DMA,
            ],
            cost_estimate=cost(1 << 20, 3 << 20),
            name="gather_tiles0",
        )(got, ext_potential)
    return pl.pallas_call(
        gather_second,
        in_specs=[SMEM, VMEM, VMEM],
        out_specs=[VMEM, VMEM, VMEM],
        out_shape=[part, part, part],
        scratch_shapes=[acc],
        cost_estimate=cost(1 << 20, 3 << 20),
        name="gather_tiles1",
    )(places, got, ext_potential)


def cut_cubes(h, places, own, rim, ext_potential, below, above, *other):
    width = PLANE // HALVES if h == 0 else PLANE
    return pl.pallas_call(
        lambda *refs: cubes_kernel(h, *refs),
        in_specs=[SMEM] + [VMEM] * (5 + len(other)),
        out_specs=[VMEM, VMEM],
        out_shape=[
            jax.ShapeDtypeStruct((CZB, width), F32),
            jax.ShapeDtypeStruct((DEVS * 16, HALF), BF16),
        ],
        scratch_shapes=[pltpu.VMEM((SEGS * LPS, 2 * CZB, LANES), F32)],
        cost_estimate=cost(1 << 20, 3 << 20),
        name=f"cut_cubes{h}",
    )(places, own, rim, ext_potential, below, above, *other)


def make_matrices(h, owner, kinds, returned, basis, *other):
    blocks = (NB, BS // 2, LANES)
    out = (blocks, F32) if h == 0 else ((NB, BS * BS), BF16)
    return pl.pallas_call(
        lambda *refs: matrix_kernel(h, *refs),
        grid=(STEPS,),
        in_specs=[SMEM, SMEM, whole((DEVS * 16, HALF))]
        + basis_specs(h)
        + [whole(blocks)] * len(other),
        out_specs=whole(out[0]),
        out_shape=jax.ShapeDtypeStruct(*out),
        scratch_shapes=[
            pltpu.VMEM((NB * BS, KINDS * BS), F32),
            pltpu.VMEM((NB * 16, HALF), F32),
            pltpu.VMEM((KINDS * BS, KINDS * BS), BF16),
            pltpu.VMEM((KINDS * BS, SEGW), BF16),
            pltpu.SMEM((DEVS,), jnp.int32),
            pltpu.SMEM((NB,), jnp.int32),
        ]
        + [pltpu.VMEM(blocks, F32)] * h,
        cost_estimate=cost(2 * NB * BS * KINDS * BS * CZB * HALF, 4 << 20),
        name=f"matrices{h}",
    )(owner, kinds, returned, basis, basis, *other)


def shifted(x, by):
    size = lax.axis_size(AXES)
    return lax.ppermute(x, AXES, [(i, (i + by) % size) for i in range(size)])


def exchanged(x):
    return lax.all_to_all(x, AXES, split_axis=0, concat_axis=0, tiled=True)


def local(
    density_blocks, block_owner, block_plane, block_segment, block_kinds, basis, ext_potential
):
    sent = [
        make_tiles(h, block_owner, block_plane, block_segment, block_kinds, density_blocks, basis)
        for h in range(HALVES)
    ]
    got = [exchanged(x) for x in sent]

    own0, rim0, half0, places = gather_tiles(0, got[0], ext_potential)
    below0, above0 = shifted(rim0, 1), shifted(half0, -1)
    density0, cubes0 = cut_cubes(0, places, own0, rim0, ext_potential, below0, above0)
    returned0 = exchanged(cubes0)

    own1, rim1, half1 = gather_tiles(1, got[1], ext_potential, places)
    below1, above1 = shifted(rim1, 1), shifted(half1, -1)
    density, cubes1 = cut_cubes(
        1, places, own1, rim1, ext_potential, below1, above1, density0
    )
    returned1 = exchanged(cubes1)

    matrices0 = make_matrices(0, block_owner, block_kinds, returned0, basis)
    matrices = make_matrices(1, block_owner, block_kinds, returned1, basis, matrices0)
    return density, matrices


def solution(mesh):
    rows = P(AXES, None)
    flat = P(AXES)
    return jax.shard_map(
        local,
        mesh=mesh,
        in_specs=(rows, rows, flat, flat, rows, P(), rows),
        out_specs=(rows, rows),
        check_vma=False,
    )
```

time: 173 us -> 145 us (0.84)
  blocking collectives: 86.6 us -> 0 us
  starting transfers between devices: 1.81 us -> 37.5 us
  waiting for transfers between devices: 2.86 us -> 35.9 us
  Pallas kernels: 76.9 us -> 65 us
    all_to_all x2 -> x0, blocking collectives: 86.6 us -> none  [exchanged(): return lax.all_to_all(x, AXES, split_axis=0, concat_axis=0, tiled=True)]
    all_to_all x0 -> x4, starting transfers between devices: none -> 34.1 us  [exchanged(): return lax.all_to_all(x, AXES, split_axis=0, concat_axis=0, tiled=True)]
    all_to_all x0 -> x4, waiting for transfers between devices: none -> 22.6 us  [exchanged(): return lax.all_to_all(x, AXES, split_axis=0, concat_axis=0, tiled=True)]
    pallas_call x4 -> x8, Pallas kernels: 76.9 us -> 65 us  [the longest x2 26.4 us: make_tiles(): pl.pallas_call(lambda *refs: tiles_kernel(h, *refs), grid=(STEPS,), in_sp...]
    ppermute x2 -> x4, waiting for transfers between devices: 2.86 us -> 13.3 us  [shifted(): return lax.ppermute(x, AXES, [(i, (i + by) % size) for i in range(size)])]
    unnamed x6 -> x18, local copies, waits for them, and re-layouts: 3.42 us -> 4.92 us
  transfers between devices with their start and end apart: 2 -> 8, of which waited for: 1 -> 8; matrix products, arithmetic and copies ran while one was open for 0% -> 0% of each run, Pallas kernels for 0% -> 27%
where the time goes in v2:
time: 145 us; the launch traced here: 144 us
  Pallas kernels  65 us (45%)
  starting transfers between devices  37.5 us (26%)
  waiting for transfers between devices  35.9 us (25%)
  local copies, waits for them, and re-layouts  4.92 us (3%)
    all_to_all x4, starting transfers between devices, exchanged(): return lax.all_to_all(x, AXES, split_axis=0, concat_axis=0, tiled=True)  34.1 us
    pallas_call x2, Pallas kernels, make_tiles(): pl.pallas_call(lambda *refs: tiles_kernel(h, *refs), grid=(STEPS,), in_sp...  26.4 us
    pallas_call x2, Pallas kernels, make_matrices(): pl.pallas_call(lambda *refs: matrix_kernel(h, *refs), grid=(STEPS,), in_s...  24.8 us
    all_to_all x4, waiting for transfers between devices, exchanged(): return lax.all_to_all(x, AXES, split_axis=0, concat_axis=0, tiled=True)  22.6 us
    ppermute x4, waiting for transfers between devices, shifted(): return lax.ppermute(x, AXES, [(i, (i + by) % size) for i in range(size)])  13.3 us
    pallas_call x2, Pallas kernels, cut_cubes(): pl.pallas_call(lambda *refs: cubes_kernel(h, *refs), in_specs=[SMEM] + [V...  6.9 us
    unnamed x18, local copies, waits for them, and re-layouts  4.92 us
    pallas_call x1, Pallas kernels, gather_tiles(): pl.pallas_call(gather_first, in_specs=[VMEM, VMEM], out_specs=[VMEM, VMEM...  3.83 us
  transfers between devices with their start and end apart: 8, of which 8 were waited for; matrix products, arithmetic and copies ran while one was open for 0% of the time, Pallas kernels for 27%

profile of v2, /device:TPU:1, one launch (start us, length us, event | category | flops | bytes accessed | tf_op | source)
XLA Modules:
  0.0 143.9 jit_solution(14414330020327947395)
XLA Ops:
  0.6 1.3 copy.9.refs_0_
  2.0 1.4 copy.10.refs_3_.refs_1_
  3.3 13.5 %tiles0.1 = bf16[1024,640]{1,0:T(8,128)(2,1)} custom-call(s32[64,1]{1,0:T(8,128)} %copy.9.refs_0_, s32[64]{0:T(128)} %refs_1_.5, s32[64]{0:T(128)} %refs_2_.3, s32[64,2]{1,0:T(8,128)} %copy.10.refs_3_.refs_1_, bf16[64,4096]{1,0:T(8,128)(2,1)} %refs_4_.5, bf16[4,64,4096]{2,1,0:T(8,128)(2,1)} %refs_4_.7, bf16[4,64,4096]{2,1,0:T(8,128)(2,1)} %refs_4_.7), custom_call_target="tpu_custom_call" | custom-call | flops 4294967296 | bytes 4194304 | tf_op jit(solution)/shard_map/tiles0/pallas_call | solution.py:281
  16.9 11.5 %all-to-all-start = ((bf16[128,8,640]{2,1,0:T(8,128)(2,1)}), bf16[128,8,640]{2,1,0:T(8,128)(2,1)S(1)}, u32[]{:S(2)}, u32[]{:S(2)}) async-start(bf16[128,8,640]{2,1,0:T(8,128)(2,1)} %bitcast.10), calls=%async_computation | async-start | bytes 2621440 | tf_op jit(solution)/shard_map/all_to_all | solution.py:376
  28.4 12.8 %tiles1.1 = bf16[1024,512]{1,0:T(8,128)(2,1)} custom-call(s32[64,1]{1,0:T(8,128)} %copy.9.refs_0_, s32[64]{0:T(128)} %refs_1_.5, s32[64]{0:T(128)} %refs_2_.3, s32[64,2]{1,0:T(8,128)} %copy.10.refs_3_.refs_1_, bf16[64,4096]{1,0:T(8,128)(2,1)} %refs_4_.5, bf16[4,64,4096]{2,1,0:T(8,128)(2,1)} %refs_4_.7, bf16[4,64,4096]{2,1,0:T(8,128)(2,1)} %refs_4_.7), custom_call_target="tpu_custom_call" | custom-call | flops 4294967296 | bytes 4194304 | tf_op jit(solution)/shard_map/tiles1/pallas_call | solution.py:281
  41.2 8.9 %all-to-all-done = bf16[128,8,640]{2,1,0:T(8,128)(2,1)S(1)} async-done(((bf16[128,8,640]{2,1,0:T(8,128)(2,1)}), bf16[128,8,640]{2,1,0:T(8,128)(2,1)S(1)}, u32[]{:S(2)}, u32[]{:S(2)}) %all-to-all-start) | async-done | bytes 1310752 | tf_op jit(solution)/shard_map/all_to_all | solution.py:376
  50.1 0.0 copy-start
  50.1 4.7 %all-to-all-start.1 = ((bf16[128,8,512]{2,1,0:T(8,128)(2,1)}), bf16[128,8,512]{2,1,0:T(8,128)(2,1)S(1)}, u32[]{:S(2)}, u32[]{:S(2)}) async-start(bf16[128,8,512]{2,1,0:T(8,128)(2,1)} %bitcast.13), calls=%async_computation.1 | async-start | bytes 2097152 | tf_op jit(solution)/shard_map/all_to_all | solution.py:376
  54.9 0.0 copy-done
  54.9 3.8 %gather_tiles0.1 = (f32[8,2048]{1,0:T(8,128)}, f32[8,2048]{1,0:T(8,128)}, f32[8,2048]{1,0:T(8,128)}, s32[8,128]{1,0:T(8,128)}) custom-call(bf16[1024,640]{1,0:T(8,128)(2,1)} %bitcast.8, f32[8,4096]{1,0:T(8,128)} %refs_3_.7), custom_call_target="tpu_custom_call" | custom-call | flops 1048576 | bytes 3145728 | tf_op jit(solution)/shard_map/gather_tiles0/pallas_call | solution.py:304
  58.7 1.7 %collective-permute-start.2 = (f32[8,2048]{1,0:T(8,128)}, f32[8,2048]{1,0:T(8,128)S(1)}, u32[]{:S(2)}, u32[]{:S(2)}) collective-permute-start(f32[8,2048]{1,0:T(8,128)} %get-tuple-element.18.refs_2_), channel_id=1, source_target_pairs={{0,1},{1,2},{2,3},{3,4},{4,5},{5,6},{6,7},{7,8},{8,9},{9,10},{10,1... | collective-permute-start | bytes 196616 | tf_op jit(solution)/shard_map/ppermute | solution.py:372
  60.4 0.0 collective-permute-start.3
  60.4 3.8 %collective-permute-done.2.refs_4_ = f32[8,2048]{1,0:T(8,128)S(1)} collective-permute-done((f32[8,2048]{1,0:T(8,128)}, f32[8,2048]{1,0:T(8,128)S(1)}, u32[]{:S(2)}, u32[]{:S(2)}) %collective-permute-start.2) | collective-permute-done | bytes 65568 | tf_op jit(solution)/shard_map/ppermute | solution.py:372
  64.3 0.0 copy-start.5
  64.3 2.5 %collective-permute-done.3.refs_5_ = f32[8,2048]{1,0:T(8,128)S(1)} collective-permute-done((f32[8,2048]{1,0:T(8,128)}, f32[8,2048]{1,0:T(8,128)S(1)}, u32[]{:S(2)}, u32[]{:S(2)}) %collective-permute-start.3) | collective-permute-done | bytes 65568 | tf_op jit(solution)/shard_map/ppermute | solution.py:372
  66.8 0.0 copy-start.7
  66.8 0.0 copy-done.5
  66.8 0.6 copy-done.7
  67.4 3.4 %cut_cubes0.1 = (f32[8,2048]{1,0:T(8,128)}, bf16[2048,256]{1,0:T(8,128)(2,1)}) custom-call(s32[8,128]{1,0:T(8,128)} %get-tuple-element.13.at_ref.refs_0_, f32[8,2048]{1,0:T(8,128)} %get-tuple-element.17.refs_1_, f32[8,2048]{1,0:T(8,128)} %get-tuple-element.18.refs_2_, f32[8,4096]{1,0:T(8,128)} %refs_3_.7, f32[8,2048]{1,0:T(8,128)} %copy-done.5, ...), custom_call_target="tpu_custom_call" | custom-call | flops 1048576 | bytes 3145728 | tf_op jit(solution)/shard_map/cut_cubes0/pallas_call | solution.py:331
  70.9 3.3 %all-to-all-done.1 = bf16[128,8,512]{2,1,0:T(8,128)(2,1)S(1)} async-done(((bf16[128,8,512]{2,1,0:T(8,128)(2,1)}), bf16[128,8,512]{2,1,0:T(8,128)(2,1)S(1)}, u32[]{:S(2)}, u32[]{:S(2)}) %all-to-all-start.1) | async-done | bytes 1048608 | tf_op jit(solution)/shard_map/all_to_all | solution.py:376
  74.2 0.0 copy-start.1
  74.2 8.9 %all-to-all-start.3 = ((bf16[128,16,256]{2,1,0:T(8,128)(2,1)}), bf16[128,16,256]{2,1,0:T(8,128)(2,1)S(1)}, u32[]{:S(2)}, u32[]{:S(2)}) async-start(bf16[128,16,256]{2,1,0:T(8,128)(2,1)} %bitcast.12), calls=%async_computation.3 | async-start | bytes 2097152 | tf_op jit(solution)/shard_map/all_to_all | solution.py:376
  83.1 0.0 copy-done.1
  83.1 3.0 %gather_tiles1.1 = (f32[8,2048]{1,0:T(8,128)}, f32[8,2048]{1,0:T(8,128)}, f32[8,2048]{1,0:T(8,128)}) custom-call(s32[8,128]{1,0:T(8,128)} %get-tuple-element.13.at_ref.refs_0_, bf16[1024,512]{1,0:T(8,128)(2,1)} %bitcast.9, f32[8,4096]{1,0:T(8,128)} %refs_3_.7), custom_call_target="tpu_custom_call" | custom-call | flops 1048576 | bytes 3145728 | tf_op jit(solution)/shard_map/gather_tiles1/pallas_call | solution.py:318
  86.2 1.7 %collective-permute-start = (f32[8,2048]{1,0:T(8,128)}, f32[8,2048]{1,0:T(8,128)S(1)}, u32[]{:S(2)}, u32[]{:S(2)}) collective-permute-start(f32[8,2048]{1,0:T(8,128)} %get-tuple-element.15.refs_2_), channel_id=1, source_target_pairs={{0,1},{1,2},{2,3},{3,4},{4,5},{5,6},{6,7},{7,8},{8,9},{9,10},{10,1... | collective-permute-start | bytes 196616 | tf_op jit(solution)/shard_map/ppermute | solution.py:372
  87.9 0.0 collective-permute-start.1
  87.9 3.9 %collective-permute-done.refs_4_ = f32[8,2048]{1,0:T(8,128)S(1)} collective-permute-done((f32[8,2048]{1,0:T(8,128)}, f32[8,2048]{1,0:T(8,128)S(1)}, u32[]{:S(2)}, u32[]{:S(2)}) %collective-permute-start) | collective-permute-done | bytes 65568 | tf_op jit(solution)/shard_map/ppermute | solution.py:372
  91.8 0.0 copy-start.4
  91.8 3.0 %collective-permute-done.1.refs_5_ = f32[8,2048]{1,0:T(8,128)S(1)} collective-permute-done((f32[8,2048]{1,0:T(8,128)}, f32[8,2048]{1,0:T(8,128)S(1)}, u32[]{:S(2)}, u32[]{:S(2)}) %collective-permute-start.1) | collective-permute-done | bytes 65568 | tf_op jit(solution)/shard_map/ppermute | solution.py:372
  94.8 0.0 copy-start.6
  94.8 0.0 copy-done.4
  94.8 0.6 copy-done.6
  95.4 3.5 %cut_cubes1.1 = (f32[8,4096]{1,0:T(8,128)}, bf16[2048,256]{1,0:T(8,128)(2,1)}) custom-call(s32[8,128]{1,0:T(8,128)} %get-tuple-element.13.at_ref.refs_0_, f32[8,2048]{1,0:T(8,128)} %get-tuple-element.14.refs_1_, f32[8,2048]{1,0:T(8,128)} %get-tuple-element.15.refs_2_, f32[8,4096]{1,0:T(8,128)} %refs_3_.7, f32[8,2048]{1,0:T(8,128)} %copy-done.4, ...), custom_call_target="tpu_custom_call" | custom-call | flops 1048576 | bytes 3145728 | tf_op jit(solution)/shard_map/cut_cubes1/pallas_call | solution.py:331
  98.9 3.6 %all-to-all-done.3 = bf16[128,16,256]{2,1,0:T(8,128)(2,1)S(1)} async-done(((bf16[128,16,256]{2,1,0:T(8,128)(2,1)}), bf16[128,16,256]{2,1,0:T(8,128)(2,1)S(1)}, u32[]{:S(2)}, u32[]{:S(2)}) %all-to-all-start.3) | async-done | bytes 1048608 | tf_op jit(solution)/shard_map/all_to_all | solution.py:376
  102.5 0.0 copy-start.2
  102.5 8.9 %all-to-all-start.2 = ((bf16[128,16,256]{2,1,0:T(8,128)(2,1)}), bf16[128,16,256]{2,1,0:T(8,128)(2,1)S(1)}, u32[]{:S(2)}, u32[]{:S(2)}) async-start(bf16[128,16,256]{2,1,0:T(8,128)(2,1)} %bitcast.14), calls=%async_computation.2 | async-start | bytes 2097152 | tf_op jit(solution)/shard_map/all_to_all | solution.py:376
  111.4 0.0 copy-done.2
  111.4 12.4 %matrices0.1.refs_5_ = f32[64,32,128]{2,1,0:T(8,128)} custom-call(s32[64,1]{1,0:T(8,128)} %copy.9.refs_0_, s32[64,2]{1,0:T(8,128)} %copy.10.refs_3_.refs_1_, bf16[2048,256]{1,0:T(8,128)(2,1)} %bitcast.11, bf16[4,64,4096]{2,1,0:T(8,128)(2,1)} %refs_4_.7, bf16[4,64,4096]{2,1,0:T(8,128)(2,1)} %refs_4_.7), custom_call_target="tpu_custom_call" | custom-call | flops 4294967296 | bytes 4194304 | tf_op jit(solution)/shard_map/matrices0/pallas_call | solution.py:348
  123.9 6.7 %all-to-all-done.2 = bf16[128,16,256]{2,1,0:T(8,128)(2,1)S(1)} async-done(((bf16[128,16,256]{2,1,0:T(8,128)(2,1)}), bf16[128,16,256]{2,1,0:T(8,128)(2,1)S(1)}, u32[]{:S(2)}, u32[]{:S(2)}) %all-to-all-start.2) | async-done | bytes 1048608 | tf_op jit(solution)/shard_map/all_to_all | solution.py:376
  130.6 0.0 copy-start.3
  130.6 1.0 copy-done.3
  131.5 12.4 %matrices1.1 = bf16[64,4096]{1,0:T(8,128)(2,1)} custom-call(s32[64,1]{1,0:T(8,128)} %copy.9.refs_0_, s32[64,2]{1,0:T(8,128)} %copy.10.refs_3_.refs_1_, bf16[2048,256]{1,0:T(8,128)(2,1)} %bitcast.15, bf16[4,64,4096]{2,1,0:T(8,128)(2,1)} %refs_4_.7, bf16[4,64,4096]{2,1,0:T(8,128)(2,1)} %refs_4_.7, f32[64,32,128]{2,1,0:T(8,128)} %matrices0.1.refs_5_), custom_call_target="tpu_custom_call" | custom-call | flops 4294967296 | bytes 4194304 | tf_op jit(solution)/shard_map/matrices1/pallas_call | solution.py:348
Async XLA Ops:
  16.9 33.3 %all-to-all-start = ((bf16[128,8,640]{2,1,0:T(8,128)(2,1)}), bf16[128,8,640]{2,1,0:T(8,128)(2,1)S(1)}, u32[]{:S(2)}, u32[]{:S(2)}) async-start(bf16[128,8,640]{2,1,0:T(8,128)(2,1)} %bitcast.10), calls=%async_computation | async-start | bytes 2621440 | tf_op jit(solution)/shard_map/all_to_all | solution.py:376
  50.1 4.7 %copy-start = (bf16[128,8,640]{2,1,0:T(8,128)(2,1)}, bf16[128,8,640]{2,1,0:T(8,128)(2,1)S(1)}, u32[]{:S(2)}) copy-start(bf16[128,8,640]{2,1,0:T(8,128)(2,1)S(1)} %all-to-all-done) | copy-start | bytes 3932164
  50.1 24.0 %all-to-all-start.1 = ((bf16[128,8,512]{2,1,0:T(8,128)(2,1)}), bf16[128,8,512]{2,1,0:T(8,128)(2,1)S(1)}, u32[]{:S(2)}, u32[]{:S(2)}) async-start(bf16[128,8,512]{2,1,0:T(8,128)(2,1)} %bitcast.13), calls=%async_computation.1 | async-start | bytes 2097152 | tf_op jit(solution)/shard_map/all_to_all | solution.py:376
  58.7 5.6 %collective-permute-start.2 = (f32[8,2048]{1,0:T(8,128)}, f32[8,2048]{1,0:T(8,128)S(1)}, u32[]{:S(2)}, u32[]{:S(2)}) collective-permute-start(f32[8,2048]{1,0:T(8,128)} %get-tuple-element.18.refs_2_), channel_id=1, source_target_pairs={{0,1},{1,2},{2,3},{3,4},{4,5},{5,6},{6,7},{7,8},{8,9},{9,10},{10,1... | collective-permute-start | bytes 196616 | tf_op jit(solution)/shard_map/ppermute | solution.py:372
  60.4 6.4 %collective-permute-start.3 = (f32[8,2048]{1,0:T(8,128)}, f32[8,2048]{1,0:T(8,128)S(1)}, u32[]{:S(2)}, u32[]{:S(2)}) collective-permute-start(f32[8,2048]{1,0:T(8,128)} %get-tuple-element.19), channel_id=1, source_target_pairs={{0,127},{1,0},{2,1},{3,2},{4,3},{5,4},{6,5},{7,6},{8,7},{9,8},{10,... | collective-permute-start | bytes 196616 | tf_op jit(solution)/shard_map/ppermute | solution.py:372
  64.3 2.5 %copy-start.5 = (f32[8,2048]{1,0:T(8,128)}, f32[8,2048]{1,0:T(8,128)S(1)}, u32[]{:S(2)}) copy-start(f32[8,2048]{1,0:T(8,128)S(1)} %collective-permute-done.2.refs_4_) | copy-start | bytes 196612
  66.8 0.6 copy-start.7
  74.2 9.0 %copy-start.1 = (bf16[128,8,512]{2,1,0:T(8,128)(2,1)}, bf16[128,8,512]{2,1,0:T(8,128)(2,1)S(1)}, u32[]{:S(2)}) copy-start(bf16[128,8,512]{2,1,0:T(8,128)(2,1)S(1)} %all-to-all-done.1) | copy-start | bytes 3145732
  74.2 28.3 %all-to-all-start.3 = ((bf16[128,16,256]{2,1,0:T(8,128)(2,1)}), bf16[128,16,256]{2,1,0:T(8,128)(2,1)S(1)}, u32[]{:S(2)}, u32[]{:S(2)}) async-start(bf16[128,16,256]{2,1,0:T(8,128)(2,1)} %bitcast.12), calls=%async_computation.3 | async-start | bytes 2097152 | tf_op jit(solution)/shard_map/all_to_all | solution.py:376
  86.2 5.6 %collective-permute-start = (f32[8,2048]{1,0:T(8,128)}, f32[8,2048]{1,0:T(8,128)S(1)}, u32[]{:S(2)}, u32[]{:S(2)}) collective-permute-start(f32[8,2048]{1,0:T(8,128)} %get-tuple-element.15.refs_2_), channel_id=1, source_target_pairs={{0,1},{1,2},{2,3},{3,4},{4,5},{5,6},{6,7},{7,8},{8,9},{9,10},{10,1... | collective-permute-start | bytes 196616 | tf_op jit(solution)/shard_map/ppermute | solution.py:372
  87.9 6.9 %collective-permute-start.1 = (f32[8,2048]{1,0:T(8,128)}, f32[8,2048]{1,0:T(8,128)S(1)}, u32[]{:S(2)}, u32[]{:S(2)}) collective-permute-start(f32[8,2048]{1,0:T(8,128)} %get-tuple-element.16), channel_id=1, source_target_pairs={{0,127},{1,0},{2,1},{3,2},{4,3},{5,4},{6,5},{7,6},{8,7},{9,8},{10,... | collective-permute-start | bytes 196616 | tf_op jit(solution)/shard_map/ppermute | solution.py:372
  91.8 3.0 %copy-start.4 = (f32[8,2048]{1,0:T(8,128)}, f32[8,2048]{1,0:T(8,128)S(1)}, u32[]{:S(2)}) copy-start(f32[8,2048]{1,0:T(8,128)S(1)} %collective-permute-done.refs_4_) | copy-start | bytes 196612
  94.8 0.6 copy-start.6
  102.5 8.9 %copy-start.2 = (bf16[128,16,256]{2,1,0:T(8,128)(2,1)}, bf16[128,16,256]{2,1,0:T(8,128)(2,1)S(1)}, u32[]{:S(2)}) copy-start(bf16[128,16,256]{2,1,0:T(8,128)(2,1)S(1)} %all-to-all-done.3) | copy-start | bytes 3145732
  102.5 28.1 %all-to-all-start.2 = ((bf16[128,16,256]{2,1,0:T(8,128)(2,1)}), bf16[128,16,256]{2,1,0:T(8,128)(2,1)S(1)}, u32[]{:S(2)}, u32[]{:S(2)}) async-start(bf16[128,16,256]{2,1,0:T(8,128)(2,1)} %bitcast.14), calls=%async_computation.2 | async-start | bytes 2097152 | tf_op jit(solution)/shard_map/all_to_all | solution.py:376
  130.6 1.0 copy-start.3

commit v3 on v2

--- a/solution.py
+++ b/solution.py
@@ -4,6 +4,7 @@
 from jax.experimental import pallas as pl
 from jax.experimental.pallas import tpu as pltpu
 from jax.sharding import PartitionSpec as P
+
 
 AXES = ("rows", "cols", "slab")
 F32 = jnp.float32
@@ -21,7 +22,7 @@
 HALF = SEGW // HALVES
 LPS = HALF // LANES
 STEPS = CZB // 2
-GROUP = 32
+GROUP = 64
 
 SMEM = pl.BlockSpec(memory_space=pltpu.SMEM)
 VMEM = pl.BlockSpec(memory_space=pltpu.VMEM)
@@ -45,6 +46,14 @@
 def joined(first, second):
     parts = [ref[...].reshape(KINDS * BS, HALF) for ref in (first, second)]
     return jnp.concatenate(parts, axis=1)
+
+
+def home(slab):
+    chip = slab >> 1
+    x, zi, yi = chip >> 4, (chip >> 2) & 3, chip & 3
+    z = zi + (x & 1) * (3 - 2 * zi)
+    y = yi + (zi & 1) * (3 - 2 * yi)
+    return (x * 4 + z) * 8 + y * 2 + (slab & 1)
 
 
 def even_rows_first():
@@ -57,9 +66,9 @@
     return jnp.where(source == wanted, 1.0, 0.0).astype(BF16)
 
 
-def tiles_kernel(
-    h, owner, plane, seg, kinds, dens_ref, first, second, out_ref, pn, lhs, a32, perm, tiles, idx
-):
+def tiles_kernel(h, *refs):
+    owner, kinds, plane, seg, dens_ref, first, second, out_ref, base = refs[:9]
+    pn, lhs, a32, perm, tiles, idx = refs[9:]
     i = pl.program_id(0)
     pairs = BS // 2
 
@@ -71,12 +80,13 @@
 
         @pl.loop(0, NB, unroll=4)
         def _(b):
-            o = owner[b, 0]
+            o = home(owner[0, b])
             was = idx[2 * o]
             after = idx[2 * o + 1]
             free = was == NB
             idx[2 * o] = jnp.where(free, b, was)
             idx[2 * o + 1] = jnp.where(free, after, b)
+            base[b] = o * 16 + jnp.where(free, 0, CZB)
 
         perm[...] = even_rows_first()
         pn[...] = dens_ref[...].astype(F32).reshape(NB, pairs, LANES)
@@ -85,7 +95,7 @@
         @pl.loop(0, NB, unroll=4)
         def _(b):
             rows = pl.ds(pl.multiple_of(b * BS, BS), BS)
-            kb = kinds[b, 1]
+            kb = kinds[1, b]
             odd = (kb & 1) == 1
             v = pn[b]
             r = pltpu.roll(v, BS, 1)
@@ -106,7 +116,7 @@
         half = jnp.dot(lhs[rows, :], joined(first, second), preferred_element_type=F32)
         for t in range(GROUP):
             b = g * GROUP + t
-            a = a32[pl.ds(pl.multiple_of(kinds[b, 0] * BS, BS), BS), :]
+            a = a32[pl.ds(pl.multiple_of(kinds[0, b] * BS, BS), BS), :]
             part = jnp.sum(a * half[t * BS : (t + 1) * BS], axis=0, keepdims=True)
             tiles[pl.ds(b * CZB + 2 * i, 1), :] = part[:, :HALF]
             tiles[pl.ds(b * CZB + 2 * i + 1, 1), :] = part[:, HALF:]
@@ -145,10 +155,9 @@
         for r in range(2):
             both = got_ref[rows, r * HALF : (r + 1) * HALF].astype(F32)
             for t in range(2):
-                p = at_ref[r, 2 * q + t]
-                s = at_ref[2 + r, 2 * q + t]
+                row = at_ref[r, 2 * q + t]
                 for l in range(LPS):
-                    at = (s + l, pl.ds(p, CZB), slice(None))
+                    at = (pl.ds(row + 2 * CZB * l, CZB), slice(None))
                     acc[at] = acc[at] + both[t * CZB : (t + 1) * CZB, l * LANES : (l + 1) * LANES]
 
     for s in range(SEGS):
@@ -156,9 +165,10 @@
             n = s * LPS + l
             cells = slice(n * LANES, (n + 1) * LANES)
             grid = slice(s * SEGW + h * HALF + l * LANES, s * SEGW + h * HALF + (l + 1) * LANES)
-            own = acc[n, 0:CZB, :]
+            row = 2 * CZB * n
+            own = acc[row : row + CZB, :]
             own_ref[:, cells] = own
-            rim_ref[:, cells] = acc[n, CZB : 2 * CZB, :]
+            rim_ref[:, cells] = acc[row + CZB : row + 2 * CZB, :]
             half_ref[:, cells] = ext_ref[:, grid] + 0.5 * own
 
 
@@ -166,8 +176,7 @@
     marks[...] = got_ref[:, 2 * HALF :].astype(F32)
     across = marks[pl.ds(0, DEVS, stride=CZB), :].T
     codes = across[0:2, :].astype(jnp.int32)
-    places[0:2, :] = codes >> 3
-    places[2:4, :] = (codes & 7) * LPS
+    places[0:2, :] = (codes >> 3) + (codes & 7) * (2 * CZB * LPS)
     copy = pltpu.make_async_copy(places, at_ref, sem)
     copy.start()
     copy.wait()
@@ -194,41 +203,29 @@
             else:
                 dens_ref[:, grid] = density
                 dens_ref[:, s * SEGW + l * LANES : s * SEGW + (l + 1) * LANES] = other_ref[:, cells]
-            pot[n, 0:CZB, :] = ext_ref[:, grid] + 0.5 * density
-            pot[n, CZB : 2 * CZB, :] = above_ref[:, cells] + 0.5 * rim_ref[:, cells]
+            row = 2 * CZB * n
+            pot[row : row + CZB, :] = ext_ref[:, grid] + 0.5 * density
+            pot[row + CZB : row + 2 * CZB, :] = above_ref[:, cells] + 0.5 * rim_ref[:, cells]
 
     @pl.loop(0, DEVS, unroll=4)
     def _(d):
         rows = pl.ds(pl.multiple_of(d * 16, 16), 16)
         for l in range(LPS):
-            cubes = [pot[at_ref[2 + r, d] + l, pl.ds(at_ref[r, d], CZB), :] for r in range(2)]
+            cubes = [pot[pl.ds(at_ref[r, d] + 2 * CZB * l, CZB), :] for r in range(2)]
             out_ref[rows, l * LANES : (l + 1) * LANES] = jnp.concatenate(cubes, axis=0).astype(BF16)
 
 
-def matrix_kernel(h, owner, kinds, ret_ref, first, second, *rest):
+def matrix_kernel(h, base, kinds, ret_ref, first, second, *rest):
     if h == 0:
-        out_ref, acc, pot, perm, shuffled, seen, base = rest
+        out_ref, acc, pot, perm, shuffled = rest
     else:
-        other_ref, out_ref, acc, pot, perm, shuffled, seen, base, vn = rest
+        other_ref, out_ref, acc, pot, perm, shuffled, vn = rest
     i = pl.program_id(0)
     pairs = BS // 2
 
     @pl.when(i == 0)
     def _():
-        @pl.loop(0, DEVS, unroll=16)
-        def _(o):
-            seen[o] = 0
-
-        @pl.loop(0, NB, unroll=4)
-        def _(b):
-            o = owner[b, 0]
-            rank = seen[o]
-            seen[o] = rank + 1
-            base[b] = b * 16 + rank * CZB
-            pot[pl.ds(pl.multiple_of(b * 16, 16), 16), :] = ret_ref[
-                pl.ds(pl.multiple_of(o * 16, 16), 16), :
-            ].astype(F32)
-
+        pot[...] = ret_ref[...].astype(F32)
         perm[...] = even_rows_first()
         acc[...] = jnp.zeros_like(acc)
 
@@ -244,7 +241,7 @@
             b = g * GROUP + t
             cells = [pot[pl.ds(base[b] + 2 * i + k, 1), :] for k in range(2)]
             cell = jnp.broadcast_to(jnp.concatenate(cells, axis=1), (BS, SEGW)).astype(BF16)
-            parts.append(shuffled[pl.ds(pl.multiple_of(kinds[b, 0] * BS, BS), BS), :] * cell)
+            parts.append(shuffled[pl.ds(pl.multiple_of(kinds[0, b] * BS, BS), BS), :] * cell)
         weighted = jnp.concatenate(parts, axis=0)
         acc[rows, :] = acc[rows, :] + lax.dot_general(
             weighted,
@@ -260,7 +257,7 @@
         @pl.loop(0, NB, unroll=4)
         def _(b):
             rows = pl.ds(pl.multiple_of(b * BS, BS), BS)
-            kb = kinds[b, 1]
+            kb = kinds[1, b]
             odd = (kb & 1) == 1
             v = jnp.where(kb < 2, acc[rows, 0:LANES], acc[rows, LANES : 2 * LANES])
             r = pltpu.roll(v, BS, 1)
@@ -276,14 +273,17 @@
             out_ref[...] = vn[...].reshape(NB, BS * BS).astype(BF16)
 
 
-def make_tiles(h, owner, plane, seg, kinds, density_blocks, basis):
+def make_tiles(h, small, density_blocks, basis):
     width = 2 * HALF + (LANES if h == 0 else 0)
     return pl.pallas_call(
         lambda *refs: tiles_kernel(h, *refs),
         grid=(STEPS,),
-        in_specs=[SMEM, SMEM, SMEM, SMEM, whole((NB, BS * BS))] + basis_specs(h),
-        out_specs=whole((DEVS * CZB, width)),
-        out_shape=jax.ShapeDtypeStruct((DEVS * CZB, width), BF16),
+        in_specs=[SMEM] * 4 + [whole((NB, BS * BS))] + basis_specs(h),
+        out_specs=[whole((DEVS * CZB, width)), SMEM],
+        out_shape=[
+            jax.ShapeDtypeStruct((DEVS * CZB, width), BF16),
+            jax.ShapeDtypeStruct((NB,), jnp.int32),
+        ],
         scratch_shapes=[
             pltpu.VMEM((NB, BS // 2, LANES), F32),
             pltpu.VMEM((NB * BS, KINDS * BS), BF16),
@@ -293,13 +293,12 @@
             pltpu.SMEM((2 * DEVS,), jnp.int32),
         ],
         cost_estimate=cost(2 * NB * BS * KINDS * BS * CZB * HALF, 4 << 20),
-        name=f"tiles{h}",
-    )(owner, plane, seg, kinds, density_blocks, basis, basis)
+    )(*small, density_blocks, basis, basis)
 
 
 def gather_tiles(h, got, ext_potential, places=None):
     part = jax.ShapeDtypeStruct((CZB, PLANE // HALVES), F32)
-    acc = pltpu.VMEM((SEGS * LPS, 2 * CZB, LANES), F32)
+    acc = pltpu.VMEM((SEGS * LPS * 2 * CZB, LANES), F32)
     if h == 0:
         return pl.pallas_call(
             gather_first,
@@ -336,13 +335,12 @@
             jax.ShapeDtypeStruct((CZB, width), F32),
             jax.ShapeDtypeStruct((DEVS * 16, HALF), BF16),
         ],
-        scratch_shapes=[pltpu.VMEM((SEGS * LPS, 2 * CZB, LANES), F32)],
+        scratch_shapes=[pltpu.VMEM((SEGS * LPS * 2 * CZB, LANES), F32)],
         cost_estimate=cost(1 << 20, 3 << 20),
-        name=f"cut_cubes{h}",
     )(places, own, rim, ext_potential, below, above, *other)
 
 
-def make_matrices(h, owner, kinds, returned, basis, *other):
+def make_matrices(h, base, kinds, returned, basis, *other):
     blocks = (NB, BS // 2, LANES)
     out = (blocks, F32) if h == 0 else ((NB, BS * BS), BF16)
     return pl.pallas_call(
@@ -355,21 +353,25 @@
         out_shape=jax.ShapeDtypeStruct(*out),
         scratch_shapes=[
             pltpu.VMEM((NB * BS, KINDS * BS), F32),
-            pltpu.VMEM((NB * 16, HALF), F32),
+            pltpu.VMEM((DEVS * 16, HALF), F32),
             pltpu.VMEM((KINDS * BS, KINDS * BS), BF16),
             pltpu.VMEM((KINDS * BS, SEGW), BF16),
-            pltpu.SMEM((DEVS,), jnp.int32),
-            pltpu.SMEM((NB,), jnp.int32),
         ]
         + [pltpu.VMEM(blocks, F32)] * h,
         cost_estimate=cost(2 * NB * BS * KINDS * BS * CZB * HALF, 4 << 20),
-        name=f"matrices{h}",
-    )(owner, kinds, returned, basis, basis, *other)
+    )(base, kinds, returned, basis, basis, *other)
 
 
 def shifted(x, by):
-    size = lax.axis_size(AXES)
-    return lax.ppermute(x, AXES, [(i, (i + by) % size) for i in range(size)])
+    return lax.ppermute(x, AXES, [(home(e), home((e + by) % DEVS)) for e in range(DEVS)])
+
+
+def to_homes(x):
+    return lax.ppermute(x, AXES, [(e, home(e)) for e in range(DEVS)])
+
+
+def from_homes(x):
+    return lax.ppermute(x, AXES, [(home(e), e) for e in range(DEVS)])
 
 
 def exchanged(x):
@@ -379,26 +381,26 @@
 def local(
     density_blocks, block_owner, block_plane, block_segment, block_kinds, basis, ext_potential
 ):
-    sent = [
-        make_tiles(h, block_owner, block_plane, block_segment, block_kinds, density_blocks, basis)
-        for h in range(HALVES)
-    ]
-    got = [exchanged(x) for x in sent]
-
-    own0, rim0, half0, places = gather_tiles(0, got[0], ext_potential)
-    below0, above0 = shifted(rim0, 1), shifted(half0, -1)
-    density0, cubes0 = cut_cubes(0, places, own0, rim0, ext_potential, below0, above0)
-    returned0 = exchanged(cubes0)
-
-    own1, rim1, half1 = gather_tiles(1, got[1], ext_potential, places)
-    below1, above1 = shifted(rim1, 1), shifted(half1, -1)
-    density, cubes1 = cut_cubes(
-        1, places, own1, rim1, ext_potential, below1, above1, density0
-    )
-    returned1 = exchanged(cubes1)
-
-    matrices0 = make_matrices(0, block_owner, block_kinds, returned0, basis)
-    matrices = make_matrices(1, block_owner, block_kinds, returned1, basis, matrices0)
+    owner, kinds = block_owner.T, block_kinds.T
+    ext_potential = to_homes(ext_potential)
+    small = (owner, kinds, block_plane, block_segment)
+    sent0, base = make_tiles(0, small, density_blocks, basis)
+    sent1, _ = make_tiles(1, small, density_blocks, basis)
+    got = [exchanged(sent0), exchanged(sent1)]
+
+    own, rim, half, places = gather_tiles(0, got[0], ext_potential)
+    below, above = shifted(rim, 1), shifted(half, -1)
+    density, cubes = cut_cubes(0, places, own, rim, ext_potential, below, above)
+    returned0 = exchanged(cubes)
+
+    own, rim, half = gather_tiles(1, got[1], ext_potential, places)
+    below, above = shifted(rim, 1), shifted(half, -1)
+    density, cubes = cut_cubes(1, places, own, rim, ext_potential, below, above, density)
+    returned1 = exchanged(cubes)
+    density = from_homes(density)
+
+    matrices = make_matrices(0, base, kinds, returned0, basis)
+    matrices = make_matrices(1, base, kinds, returned1, basis, matrices)
     return density, matrices
 
 

time: 145 us -> 157 us (1.083)
  the two profiles are of different devices: /device:TPU:1 before, /device:TPU:3 now
where the time goes in v3:
time: 157 us; the launch traced here: 156 us
  Pallas kernels  56.8 us (36%)
  waiting for transfers between devices  48.7 us (31%)
  starting transfers between devices  46.2 us (29%)
  local copies, waits for them, and re-layouts  3.55 us (2%)
    all_to_all x4, starting transfers between devices, exchanged(): return lax.all_to_all(x, AXES, split_axis=0, concat_axis=0, tiled=True)  31.3 us
    pallas_call x2, Pallas kernels, make_tiles(): pl.pallas_call(lambda *refs: tiles_kernel(h, *refs), grid=(STEPS,), in_sp...  23.3 us
    pallas_call x2, Pallas kernels, make_matrices(): pl.pallas_call(lambda *refs: matrix_kernel(h, *refs), grid=(STEPS,), in_s...  21.4 us
    ppermute x1, waiting for transfers between devices, to_homes(): return lax.ppermute(x, AXES, [(e, home(e)) for e in range(DEVS)])  14.7 us
    ppermute x4, waiting for transfers between devices, shifted(): lax.ppermute(x, AXES, [(home(e), home((e + by) % DEVS)) for e in range(DE...  12.8 us
    ppermute x1, waiting for transfers between devices, from_homes(): return lax.ppermute(x, AXES, [(home(e), e) for e in range(DEVS)])  11 us
    all_to_all x4, waiting for transfers between devices, exchanged(): return lax.all_to_all(x, AXES, split_axis=0, concat_axis=0, tiled=True)  10.2 us
    ppermute x1, starting transfers between devices, from_homes(): return lax.ppermute(x, AXES, [(home(e), e) for e in range(DEVS)])  7.48 us
  transfers between devices with their start and end apart: 10, of which 8 were waited for; matrix products, arithmetic and copies ran while one was open for 0% of the time, Pallas kernels for 22%

profile of v3, /device:TPU:3, one launch (start us, length us, event | category | flops | bytes accessed | tf_op | source)
XLA Modules:
  0.0 156.0 jit_solution(201640845150405899)
XLA Ops:
  0.6 12.0 %shard_map.86 = (bf16[1024,640]{1,0:T(8,128)(2,1)}, s32[64]{0:T(128)}) custom-call(s32[1,64]{1,0:T(1,128)} %bitcast.22, s32[2,64]{1,0:T(2,128)} %bitcast.18, s32[64]{0:T(128)} %refs_2_.3, s32[64]{0:T(128)} %refs_3_.5, bf16[64,4096]{1,0:T(8,128)(2,1)} %refs_4_.5, bf16[4,64,4096]{2,1,0:T(8,128)(2,1)} %refs_4_.7, bf16[4,64,4096]{2,1,0:T(8,128)(2,1)} %refs_4_.7), custom_call_target="tpu_custom_call" | custom-call | flops 4294967296 | bytes 4194304 | tf_op jit(solution)/shard_map/pallas_call | solution.py:278
  12.6 10.8 %all-to-all-start = ((bf16[128,8,640]{2,1,0:T(8,128)(2,1)}), bf16[128,8,640]{2,1,0:T(8,128)(2,1)S(1)}, u32[]{:S(2)}, u32[]{:S(2)}) async-start(bf16[128,8,640]{2,1,0:T(8,128)(2,1)} %bitcast.12), calls=%async_computation | async-start | bytes 2621440 | tf_op jit(solution)/shard_map/all_to_all | solution.py:378
  23.5 11.3 %shard_map.87 = (bf16[1024,512]{1,0:T(8,128)(2,1)}, s32[64]{0:T(128)}) custom-call(s32[1,64]{1,0:T(1,128)} %bitcast.23, s32[2,64]{1,0:T(2,128)} %bitcast.19, s32[64]{0:T(128)} %refs_2_.3, s32[64]{0:T(128)} %refs_3_.5, bf16[64,4096]{1,0:T(8,128)(2,1)} %refs_4_.5, bf16[4,64,4096]{2,1,0:T(8,128)(2,1)} %refs_4_.7, bf16[4,64,4096]{2,1,0:T(8,128)(2,1)} %refs_4_.7), custom_call_target="tpu_custom_call" | custom-call | flops 4294967296 | bytes 4194304 | tf_op jit(solution)/shard_map/pallas_call | solution.py:278
  34.7 0.0 copy-start.9
  34.8 9.4 %all-to-all-done = bf16[128,8,640]{2,1,0:T(8,128)(2,1)S(1)} async-done(((bf16[128,8,640]{2,1,0:T(8,128)(2,1)}), bf16[128,8,640]{2,1,0:T(8,128)(2,1)S(1)}, u32[]{:S(2)}, u32[]{:S(2)}) %all-to-all-start) | async-done | bytes 1310752 | tf_op jit(solution)/shard_map/all_to_all | solution.py:378
  44.2 0.0 copy-start
  44.2 5.8 %all-to-all-start.1 = ((bf16[128,8,512]{2,1,0:T(8,128)(2,1)}), bf16[128,8,512]{2,1,0:T(8,128)(2,1)S(1)}, u32[]{:S(2)}, u32[]{:S(2)}) async-start(bf16[128,8,512]{2,1,0:T(8,128)(2,1)} %bitcast.14), calls=%async_computation.1 | async-start | bytes 2097152 | tf_op jit(solution)/shard_map/all_to_all | solution.py:378
  50.0 0.0 copy-done.9
  50.0 5.1 %collective-permute-start = (f32[8,4096]{1,0:T(8,128)S(1)}, f32[8,4096]{1,0:T(8,128)S(1)}, u32[]{:S(2)}, u32[]{:S(2)}) collective-permute-start(f32[8,4096]{1,0:T(8,128)S(1)} %copy-done.9), channel_id=1, source_target_pairs={{0,0},{1,1},{2,2},{3,3},{4,4},{5,5},{6,6},{7,7},{8,14},{9,15},{10,... | collective-permute-start | bytes 393224 | tf_op jit(solution)/shard_map/ppermute | solution.py:370
  55.1 14.7 %collective-permute-done.ext_ref.refs_3_ = f32[8,4096]{1,0:T(8,128)S(1)} collective-permute-done((f32[8,4096]{1,0:T(8,128)S(1)}, f32[8,4096]{1,0:T(8,128)S(1)}, u32[]{:S(2)}, u32[]{:S(2)}) %collective-permute-start) | collective-permute-done | bytes 131104 | tf_op jit(solution)/shard_map/ppermute | solution.py:370
  69.8 0.0 copy-start.2
  69.8 0.0 copy-done
  69.8 0.7 copy-done.2
  70.4 3.6 %gather_tiles0.1 = (f32[8,2048]{1,0:T(8,128)}, f32[8,2048]{1,0:T(8,128)}, f32[8,2048]{1,0:T(8,128)}, s32[8,128]{1,0:T(8,128)}) custom-call(bf16[1024,640]{1,0:T(8,128)(2,1)} %bitcast.10, f32[8,4096]{1,0:T(8,128)} %copy-done.2), custom_call_target="tpu_custom_call" | custom-call | flops 1048576 | bytes 3145728 | tf_op jit(solution)/shard_map/gather_tiles0/pallas_call | solution.py:303
  74.1 0.1 collective-permute-start.3
  74.1 0.8 collective-permute-start.4
  75.0 0.9 collective-permute-done.3.refs_4_
  75.8 0.0 copy-start.7
  75.8 2.5 %collective-permute-done.4.refs_5_ = f32[8,2048]{1,0:T(8,128)S(1)} collective-permute-done((f32[8,2048]{1,0:T(8,128)}, f32[8,2048]{1,0:T(8,128)S(1)}, u32[]{:S(2)}, u32[]{:S(2)}) %collective-permute-start.4) | collective-permute-done | bytes 65568 | tf_op jit(solution)/shard_map/ppermute | solution.py:366
  78.4 0.0 copy-start.8
  78.4 0.0 copy-done.7
  78.4 0.6 copy-done.8
  79.0 2.8 %shard_map.88 = (f32[8,2048]{1,0:T(8,128)}, bf16[2048,256]{1,0:T(8,128)(2,1)}) custom-call(s32[8,128]{1,0:T(8,128)} %get-tuple-element.17.at_ref.refs_0_, f32[8,2048]{1,0:T(8,128)} %get-tuple-element.22.refs_1_, f32[8,2048]{1,0:T(8,128)} %get-tuple-element.23.refs_2_, f32[8,4096]{1,0:T(8,128)} %copy-done.2, f32[8,2048]{1,0:T(8,128)} %copy-done.7, ...), custom_call_target="tpu_custom_call" | custom-call | flops 1048576 | bytes 3145728 | tf_op jit(solution)/shard_map/pallas_call | solution.py:330
  81.8 0.0 all-to-all-done.1
  81.8 0.0 copy-start.1
  81.8 5.9 %all-to-all-start.3 = ((bf16[128,16,256]{2,1,0:T(8,128)(2,1)}), bf16[128,16,256]{2,1,0:T(8,128)(2,1)S(1)}, u32[]{:S(2)}, u32[]{:S(2)}) async-start(bf16[128,16,256]{2,1,0:T(8,128)(2,1)} %bitcast.15), calls=%async_computation.3 | async-start | bytes 2097152 | tf_op jit(solution)/shard_map/all_to_all | solution.py:378
  87.7 0.0 copy-done.1
  87.8 2.9 %gather_tiles1.1 = (f32[8,2048]{1,0:T(8,128)}, f32[8,2048]{1,0:T(8,128)}, f32[8,2048]{1,0:T(8,128)}) custom-call(s32[8,128]{1,0:T(8,128)} %get-tuple-element.17.at_ref.refs_0_, bf16[1024,512]{1,0:T(8,128)(2,1)} %bitcast.11, f32[8,4096]{1,0:T(8,128)} %copy-done.2), custom_call_target="tpu_custom_call" | custom-call | flops 1048576 | bytes 3145728 | tf_op jit(solution)/shard_map/gather_tiles1/pallas_call | solution.py:317
  90.6 1.5 collective-permute-start.1
  92.1 0.0 collective-permute-start.2
  92.1 7.5 %collective-permute-done.1.refs_4_ = f32[8,2048]{1,0:T(8,128)S(1)} collective-permute-done((f32[8,2048]{1,0:T(8,128)}, f32[8,2048]{1,0:T(8,128)S(1)}, u32[]{:S(2)}, u32[]{:S(2)}) %collective-permute-start.1) | collective-permute-done | bytes 65568 | tf_op jit(solution)/shard_map/ppermute | solution.py:366
  99.5 0.0 copy-start.5
  99.6 1.9 %collective-permute-done.2.refs_5_ = f32[8,2048]{1,0:T(8,128)S(1)} collective-permute-done((f32[8,2048]{1,0:T(8,128)}, f32[8,2048]{1,0:T(8,128)S(1)}, u32[]{:S(2)}, u32[]{:S(2)}) %collective-permute-start.2) | collective-permute-done | bytes 65568 | tf_op jit(solution)/shard_map/ppermute | solution.py:366
  101.5 0.0 copy-start.6
  101.5 0.0 copy-done.5
  101.5 0.6 copy-done.6
  102.1 2.8 %shard_map.89 = (f32[8,4096]{1,0:T(8,128)}, bf16[2048,256]{1,0:T(8,128)(2,1)}) custom-call(s32[8,128]{1,0:T(8,128)} %get-tuple-element.17.at_ref.refs_0_, f32[8,2048]{1,0:T(8,128)} %get-tuple-element.19.refs_1_, f32[8,2048]{1,0:T(8,128)} %get-tuple-element.20.refs_2_, f32[8,4096]{1,0:T(8,128)} %copy-done.2, f32[8,2048]{1,0:T(8,128)} %copy-done.5, ...), custom_call_target="tpu_custom_call" | custom-call | flops 1048576 | bytes 3145728 | tf_op jit(solution)/shard_map/pallas_call | solution.py:330
  104.9 0.0 copy-start.10
  104.9 0.8 all-to-all-done.3
  105.7 0.0 copy-start.3
  105.7 8.8 %all-to-all-start.2 = ((bf16[128,16,256]{2,1,0:T(8,128)(2,1)}), bf16[128,16,256]{2,1,0:T(8,128)(2,1)S(1)}, u32[]{:S(2)}, u32[]{:S(2)}) async-start(bf16[128,16,256]{2,1,0:T(8,128)(2,1)} %bitcast.16), calls=%async_computation.2 | async-start | bytes 2097152 | tf_op jit(solution)/shard_map/all_to_all | solution.py:378
  114.5 0.0 copy-done.10
  114.5 7.5 %collective-permute-start.5 = (f32[8,4096]{1,0:T(8,128)S(1)}, f32[8,4096]{1,0:T(8,128)S(1)}, u32[]{:S(2)}, u32[]{:S(2)}) collective-permute-start(f32[8,4096]{1,0:T(8,128)S(1)} %copy-done.10), channel_id=1, source_target_pairs={{0,0},{1,1},{2,2},{3,3},{4,4},{5,5},{6,6},{7,7},{14,8},{15,9},{12,... | collective-permute-start | bytes 393224 | tf_op jit(solution)/shard_map/ppermute | solution.py:374
  122.0 11.0 %collective-permute-done.5 = f32[8,4096]{1,0:T(8,128)S(1)} collective-permute-done((f32[8,4096]{1,0:T(8,128)S(1)}, f32[8,4096]{1,0:T(8,128)S(1)}, u32[]{:S(2)}, u32[]{:S(2)}) %collective-permute-start.5) | collective-permute-done | bytes 131104 | tf_op jit(solution)/shard_map/ppermute | solution.py:374
  133.0 0.0 copy-done.3
  133.0 10.5 %shard_map.90.refs_5_ = f32[64,32,128]{2,1,0:T(8,128)} custom-call(s32[64]{0:T(128)} %get-tuple-element.27.refs_0_, s32[2,64]{1,0:T(2,128)} %bitcast.20, bf16[2048,256]{1,0:T(8,128)(2,1)} %bitcast.13, bf16[4,64,4096]{2,1,0:T(8,128)(2,1)} %refs_4_.7, bf16[4,64,4096]{2,1,0:T(8,128)(2,1)} %refs_4_.7), custom_call_target="tpu_custom_call" | custom-call | flops 4294967296 | bytes 4194304 | tf_op jit(solution)/shard_map/pallas_call | solution.py:346
  143.5 0.0 all-to-all-done.2
  143.5 0.0 copy-start.4
  143.5 1.0 copy-done.4
  144.5 10.8 %shard_map.91 = bf16[64,4096]{1,0:T(8,128)(2,1)} custom-call(s32[64]{0:T(128)} %get-tuple-element.27.refs_0_, s32[2,64]{1,0:T(2,128)} %bitcast.21, bf16[2048,256]{1,0:T(8,128)(2,1)} %bitcast.17, bf16[4,64,4096]{2,1,0:T(8,128)(2,1)} %refs_4_.7, bf16[4,64,4096]{2,1,0:T(8,128)(2,1)} %refs_4_.7, f32[64,32,128]{2,1,0:T(8,128)} %shard_map.90.refs_5_), custom_call_target="tpu_custom_call" | custom-call | flops 4294967296 | bytes 4194304 | tf_op jit(solution)/shard_map/pallas_call | solution.py:346
  155.3 0.7 copy.10
Async XLA Ops:
  12.6 31.5 %all-to-all-start = ((bf16[128,8,640]{2,1,0:T(8,128)(2,1)}), bf16[128,8,640]{2,1,0:T(8,128)(2,1)S(1)}, u32[]{:S(2)}, u32[]{:S(2)}) async-start(bf16[128,8,640]{2,1,0:T(8,128)(2,1)} %bitcast.12), calls=%async_computation | async-start | bytes 2621440 | tf_op jit(solution)/shard_map/all_to_all | solution.py:378
  34.7 15.2 %copy-start.9 = (f32[8,4096]{1,0:T(8,128)S(1)}, f32[8,4096]{1,0:T(8,128)}, u32[]{:S(2)}) copy-start(f32[8,4096]{1,0:T(8,128)} %param.13) | copy-start | bytes 393220
  44.2 25.6 %copy-start = (bf16[128,8,640]{2,1,0:T(8,128)(2,1)}, bf16[128,8,640]{2,1,0:T(8,128)(2,1)S(1)}, u32[]{:S(2)}) copy-start(bf16[128,8,640]{2,1,0:T(8,128)(2,1)S(1)} %all-to-all-done) | copy-start | bytes 3932164
  44.2 37.6 %all-to-all-start.1 = ((bf16[128,8,512]{2,1,0:T(8,128)(2,1)}), bf16[128,8,512]{2,1,0:T(8,128)(2,1)S(1)}, u32[]{:S(2)}, u32[]{:S(2)}) async-start(bf16[128,8,512]{2,1,0:T(8,128)(2,1)} %bitcast.14), calls=%async_computation.1 | async-start | bytes 2097152 | tf_op jit(solution)/shard_map/all_to_all | solution.py:378
  50.0 19.8 %collective-permute-start = (f32[8,4096]{1,0:T(8,128)S(1)}, f32[8,4096]{1,0:T(8,128)S(1)}, u32[]{:S(2)}, u32[]{:S(2)}) collective-permute-start(f32[8,4096]{1,0:T(8,128)S(1)} %copy-done.9), channel_id=1, source_target_pairs={{0,0},{1,1},{2,2},{3,3},{4,4},{5,5},{6,6},{7,7},{8,14},{9,15},{10,... | collective-permute-start | bytes 393224 | tf_op jit(solution)/shard_map/ppermute | solution.py:370
  69.8 0.7 copy-start.2
  74.1 1.8 %collective-permute-start.3 = (f32[8,2048]{1,0:T(8,128)}, f32[8,2048]{1,0:T(8,128)S(1)}, u32[]{:S(2)}, u32[]{:S(2)}) collective-permute-start(f32[8,2048]{1,0:T(8,128)} %get-tuple-element.23.refs_2_), channel_id=1, source_target_pairs={{0,1},{1,2},{2,3},{3,4},{4,5},{5,6},{6,7},{7,14},{14,15},{15,12},{... | collective-permute-start | bytes 196616 | tf_op jit(solution)/shard_map/ppermute | solution.py:366
  74.1 4.2 %collective-permute-start.4 = (f32[8,2048]{1,0:T(8,128)}, f32[8,2048]{1,0:T(8,128)S(1)}, u32[]{:S(2)}, u32[]{:S(2)}) collective-permute-start(f32[8,2048]{1,0:T(8,128)} %get-tuple-element.24), channel_id=1, source_target_pairs={{0,97},{1,0},{2,1},{3,2},{4,3},{5,4},{6,5},{7,6},{14,7},{15,14},{1... | collective-permute-start | bytes 196616 | tf_op jit(solution)/shard_map/ppermute | solution.py:366
  75.8 2.6 %copy-start.7 = (f32[8,2048]{1,0:T(8,128)}, f32[8,2048]{1,0:T(8,128)S(1)}, u32[]{:S(2)}) copy-start(f32[8,2048]{1,0:T(8,128)S(1)} %collective-permute-done.3.refs_4_) | copy-start | bytes 196612
  78.4 0.6 copy-start.8
  81.8 5.9 %copy-start.1 = (bf16[128,8,512]{2,1,0:T(8,128)(2,1)}, bf16[128,8,512]{2,1,0:T(8,128)(2,1)S(1)}, u32[]{:S(2)}) copy-start(bf16[128,8,512]{2,1,0:T(8,128)(2,1)S(1)} %all-to-all-done.1) | copy-start | bytes 3145732
  81.8 23.9 %all-to-all-start.3 = ((bf16[128,16,256]{2,1,0:T(8,128)(2,1)}), bf16[128,16,256]{2,1,0:T(8,128)(2,1)S(1)}, u32[]{:S(2)}, u32[]{:S(2)}) async-start(bf16[128,16,256]{2,1,0:T(8,128)(2,1)} %bitcast.15), calls=%async_computation.3 | async-start | bytes 2097152 | tf_op jit(solution)/shard_map/all_to_all | solution.py:378
  90.6 8.9 %collective-permute-start.1 = (f32[8,2048]{1,0:T(8,128)}, f32[8,2048]{1,0:T(8,128)S(1)}, u32[]{:S(2)}, u32[]{:S(2)}) collective-permute-start(f32[8,2048]{1,0:T(8,128)} %get-tuple-element.20.refs_2_), channel_id=1, source_target_pairs={{0,1},{1,2},{2,3},{3,4},{4,5},{5,6},{6,7},{7,14},{14,15},{15,12},{... | collective-permute-start | bytes 196616 | tf_op jit(solution)/shard_map/ppermute | solution.py:366
  92.1 9.4 %collective-permute-start.2 = (f32[8,2048]{1,0:T(8,128)}, f32[8,2048]{1,0:T(8,128)S(1)}, u32[]{:S(2)}, u32[]{:S(2)}) collective-permute-start(f32[8,2048]{1,0:T(8,128)} %get-tuple-element.21), channel_id=1, source_target_pairs={{0,97},{1,0},{2,1},{3,2},{4,3},{5,4},{6,5},{7,6},{14,7},{15,14},{1... | collective-permute-start | bytes 196616 | tf_op jit(solution)/shard_map/ppermute | solution.py:366
  99.5 1.9 %copy-start.5 = (f32[8,2048]{1,0:T(8,128)}, f32[8,2048]{1,0:T(8,128)S(1)}, u32[]{:S(2)}) copy-start(f32[8,2048]{1,0:T(8,128)S(1)} %collective-permute-done.1.refs_4_) | copy-start | bytes 196612
  101.5 0.6 copy-start.6
  104.9 9.6 %copy-start.10 = (f32[8,4096]{1,0:T(8,128)S(1)}, f32[8,4096]{1,0:T(8,128)}, u32[]{:S(2)}) copy-start(f32[8,4096]{1,0:T(8,128)} %get-tuple-element.26) | copy-start | bytes 393220
  105.7 27.2 %copy-start.3 = (bf16[128,16,256]{2,1,0:T(8,128)(2,1)}, bf16[128,16,256]{2,1,0:T(8,128)(2,1)S(1)}, u32[]{:S(2)}) copy-start(bf16[128,16,256]{2,1,0:T(8,128)(2,1)S(1)} %all-to-all-done.3) | copy-start | bytes 3145732
  105.7 37.8 %all-to-all-start.2 = ((bf16[128,16,256]{2,1,0:T(8,128)(2,1)}), bf16[128,16,256]{2,1,0:T(8,128)(2,1)S(1)}, u32[]{:S(2)}, u32[]{:S(2)}) async-start(bf16[128,16,256]{2,1,0:T(8,128)(2,1)} %bitcast.16), calls=%async_computation.2 | async-start | bytes 2097152 | tf_op jit(solution)/shard_map/all_to_all | solution.py:378
  114.5 18.5 %collective-permute-start.5 = (f32[8,4096]{1,0:T(8,128)S(1)}, f32[8,4096]{1,0:T(8,128)S(1)}, u32[]{:S(2)}, u32[]{:S(2)}) collective-permute-start(f32[8,4096]{1,0:T(8,128)S(1)} %copy-done.10), channel_id=1, source_target_pairs={{0,0},{1,1},{2,2},{3,3},{4,4},{5,5},{6,6},{7,7},{14,8},{15,9},{12,... | collective-permute-start | bytes 393224 | tf_op jit(solution)/shard_map/ppermute | solution.py:374
  143.5 1.0 copy-start.4

commit v4 on v3

--- a/solution.py
+++ b/solution.py
@@ -18,11 +18,13 @@
 DEVS = 128
 PLANE = SEGS * SEGW
 LANES = 128
+CODE = 1024
 HALVES = 2
 HALF = SEGW // HALVES
 LPS = HALF // LANES
 STEPS = CZB // 2
 GROUP = 64
+TILES_MIB, SMALL_MIB, MATRICES_MIB = 63, 12, 62
 
 SMEM = pl.BlockSpec(memory_space=pltpu.SMEM)
 VMEM = pl.BlockSpec(memory_space=pltpu.VMEM)
@@ -37,6 +39,10 @@
         return pl.BlockSpec((KINDS, BS, HALF), lambda i: (0, 0, (2 * i + t) * HALVES + h))
 
     return [spec(0), spec(1)]
+
+
+def room(mib):
+    return pltpu.CompilerParams(vmem_limit_bytes=mib << 20)
 
 
 def cost(flops, moved):
@@ -54,6 +60,13 @@
     z = zi + (x & 1) * (3 - 2 * zi)
     y = yi + (zi & 1) * (3 - 2 * yi)
     return (x * 4 + z) * 8 + y * 2 + (slab & 1)
+
+
+def first_slab(chip):
+    x, z, y = chip >> 4, (chip >> 2) & 3, chip & 3
+    zi = z + (x & 1) * (3 - 2 * z)
+    yi = y + (zi & 1) * (3 - 2 * y)
+    return 2 * (x * 16 + zi * 4 + yi)
 
 
 def even_rows_first():
@@ -67,8 +80,12 @@
 
 
 def tiles_kernel(h, *refs):
-    owner, kinds, plane, seg, dens_ref, first, second, out_ref, base = refs[:9]
-    pn, lhs, a32, perm, tiles, idx = refs[9:]
+    owner, kinds = refs[:2]
+    if h == 0:
+        plane, seg, dens_ref, first, second, out_ref = refs[2:8]
+    else:
+        dens_ref, first, second, out_ref, base = refs[2:7]
+    pn, lhs, a32, perm, tiles, idx = refs[-6:]
     i = pl.program_id(0)
     pairs = BS // 2
 
@@ -76,17 +93,21 @@
     def _():
         @pl.loop(0, 2 * DEVS, unroll=16)
         def _(o):
-            idx[o] = NB
+            idx[o] = NB * CZB
 
         @pl.loop(0, NB, unroll=4)
         def _(b):
-            o = home(owner[0, b])
+            o = owner[0, b]
             was = idx[2 * o]
             after = idx[2 * o + 1]
-            free = was == NB
-            idx[2 * o] = jnp.where(free, b, was)
-            idx[2 * o + 1] = jnp.where(free, after, b)
-            base[b] = o * 16 + jnp.where(free, 0, CZB)
+            free = was == NB * CZB
+            entry = b * CZB
+            if h == 0:
+                entry = entry + (plane[b] * SEGS + seg[b]) * CODE
+            else:
+                base[b] = home(o) * 16 + jnp.where(free, 0, CZB)
+            idx[2 * o] = jnp.where(free, entry, was)
+            idx[2 * o + 1] = jnp.where(free, after, entry)
 
         perm[...] = even_rows_first()
         pn[...] = dens_ref[...].astype(F32).reshape(NB, pairs, LANES)
@@ -102,9 +123,11 @@
             keep = low != odd
             evens = jnp.where(keep, jnp.where(odd, r, v), 0.0)
             odds = jnp.where(keep, jnp.where(odd, v, r), 0.0)
-            v = jnp.concatenate([evens, odds], axis=0)
-            lhs[rows, 0:LANES] = jnp.where(kb < 2, v, 0.0).astype(BF16)
-            lhs[rows, LANES : 2 * LANES] = jnp.where(kb < 2, 0.0, v).astype(BF16)
+            side = pl.multiple_of((kb >> 1) * LANES, LANES)
+            lhs[rows, pl.ds(side, LANES)] = jnp.concatenate([evens, odds], axis=0).astype(BF16)
+            lhs[rows, pl.ds(pl.multiple_of(LANES - side, LANES), LANES)] = jnp.zeros(
+                (BS, LANES), BF16
+            )
 
         tiles[pl.ds(NB * CZB, CZB), :] = jnp.zeros((CZB, HALF), F32)
 
@@ -128,17 +151,16 @@
         @pl.loop(0, DEVS // 2, unroll=4)
         def _(q):
             rows = pl.ds(pl.multiple_of(q * 16, 16), 16)
-            slots = [idx[4 * q + r] for r in range(4)]
-            parts = [tiles[pl.ds(pl.multiple_of(b * CZB, CZB), CZB), :] for b in slots]
+            slab = first_slab(q)
+            slots = [idx[2 * slab + r] for r in range(4)]
+            at = [pl.multiple_of(e & (CODE - 1), CZB) for e in slots]
+            parts = [tiles[pl.ds(row, CZB), :] for row in at]
             out_ref[rows, 0:HALF] = jnp.concatenate([parts[0], parts[2]], axis=0).astype(BF16)
             out_ref[rows, HALF : 2 * HALF] = jnp.concatenate(
                 [parts[1], parts[3]], axis=0
             ).astype(BF16)
             if h == 0:
-                codes = []
-                for b in slots:
-                    held = jnp.minimum(b, NB - 1)
-                    codes.append((plane[held] * SEGS + seg[held]).astype(F32))
+                codes = [(e >> 10).astype(F32) for e in slots]
                 marks = [
                     jnp.where(lane == 0, codes[2 * r], jnp.where(lane == 1, codes[2 * r + 1], 0.0))
                     for r in range(2)
@@ -219,7 +241,7 @@
     if h == 0:
         out_ref, acc, pot, perm, shuffled = rest
     else:
-        other_ref, out_ref, acc, pot, perm, shuffled, vn = rest
+        other_ref, dens_ref, out_ref, dens_out, acc, pot, perm, shuffled, vn = rest
     i = pl.program_id(0)
     pairs = BS // 2
 
@@ -227,7 +249,6 @@
     def _():
         pot[...] = ret_ref[...].astype(F32)
         perm[...] = even_rows_first()
-        acc[...] = jnp.zeros_like(acc)
 
     shuffled[...] = jnp.dot(
         perm[...], joined(first, second), preferred_element_type=F32
@@ -243,7 +264,7 @@
             cell = jnp.broadcast_to(jnp.concatenate(cells, axis=1), (BS, SEGW)).astype(BF16)
             parts.append(shuffled[pl.ds(pl.multiple_of(kinds[0, b] * BS, BS), BS), :] * cell)
         weighted = jnp.concatenate(parts, axis=0)
-        acc[rows, :] = acc[rows, :] + lax.dot_general(
+        acc[rows, :] = jnp.where(i == 0, 0.0, acc[rows, :]) + lax.dot_general(
             weighted,
             joined(first, second),
             (((1,), (1,)), ((), ())),
@@ -270,6 +291,7 @@
                 vn[b] = block + other_ref[b]
 
         if h == 1:
+            dens_out[...] = dens_ref[...]
             out_ref[...] = vn[...].reshape(NB, BS * BS).astype(BF16)
 
 
@@ -278,12 +300,10 @@
     return pl.pallas_call(
         lambda *refs: tiles_kernel(h, *refs),
         grid=(STEPS,),
-        in_specs=[SMEM] * 4 + [whole((NB, BS * BS))] + basis_specs(h),
-        out_specs=[whole((DEVS * CZB, width)), SMEM],
-        out_shape=[
-            jax.ShapeDtypeStruct((DEVS * CZB, width), BF16),
-            jax.ShapeDtypeStruct((NB,), jnp.int32),
-        ],
+        in_specs=[SMEM] * len(small) + [whole((NB, BS * BS))] + basis_specs(h),
+        out_specs=[whole((DEVS * CZB, width))] + [SMEM] * h,
+        out_shape=[jax.ShapeDtypeStruct((DEVS * CZB, width), BF16)]
+        + [jax.ShapeDtypeStruct((NB,), jnp.int32)] * h,
         scratch_shapes=[
             pltpu.VMEM((NB, BS // 2, LANES), F32),
             pltpu.VMEM((NB * BS, KINDS * BS), BF16),
@@ -293,6 +313,7 @@
             pltpu.SMEM((2 * DEVS,), jnp.int32),
         ],
         cost_estimate=cost(2 * NB * BS * KINDS * BS * CZB * HALF, 4 << 20),
+        compiler_params=room(TILES_MIB),
     )(*small, density_blocks, basis, basis)
 
 
@@ -312,6 +333,7 @@
                 pltpu.SemaphoreType.DMA,
             ],
             cost_estimate=cost(1 << 20, 3 << 20),
+            compiler_params=room(SMALL_MIB),
             name="gather_tiles0",
         )(got, ext_potential)
     return pl.pallas_call(
@@ -321,6 +343,7 @@
         out_shape=[part, part, part],
         scratch_shapes=[acc],
         cost_estimate=cost(1 << 20, 3 << 20),
+        compiler_params=room(SMALL_MIB),
         name="gather_tiles1",
     )(places, got, ext_potential)
 
@@ -337,6 +360,7 @@
         ],
         scratch_shapes=[pltpu.VMEM((SEGS * LPS * 2 * CZB, LANES), F32)],
         cost_estimate=cost(1 << 20, 3 << 20),
+        compiler_params=room(SMALL_MIB),
     )(places, own, rim, ext_potential, below, above, *other)
 
 
@@ -348,9 +372,9 @@
         grid=(STEPS,),
         in_specs=[SMEM, SMEM, whole((DEVS * 16, HALF))]
         + basis_specs(h)
-        + [whole(blocks)] * len(other),
-        out_specs=whole(out[0]),
-        out_shape=jax.ShapeDtypeStruct(*out),
+        + ([whole(blocks), whole((CZB, PLANE))] if h == 1 else []),
+        out_specs=[whole(out[0])] + [whole((CZB, PLANE))] * h,
+        out_shape=[jax.ShapeDtypeStruct(*out)] + [jax.ShapeDtypeStruct((CZB, PLANE), F32)] * h,
         scratch_shapes=[
             pltpu.VMEM((NB * BS, KINDS * BS), F32),
             pltpu.VMEM((DEVS * 16, HALF), F32),
@@ -359,6 +383,7 @@
         ]
         + [pltpu.VMEM(blocks, F32)] * h,
         cost_estimate=cost(2 * NB * BS * KINDS * BS * CZB * HALF, 4 << 20),
+        compiler_params=room(MATRICES_MIB),
     )(base, kinds, returned, basis, basis, *other)
 
 
@@ -383,9 +408,9 @@
 ):
     owner, kinds = block_owner.T, block_kinds.T
     ext_potential = to_homes(ext_potential)
-    small = (owner, kinds, block_plane, block_segment)
-    sent0, base = make_tiles(0, small, density_blocks, basis)
-    sent1, _ = make_tiles(1, small, density_blocks, basis)
+    small = (owner, kinds)
+    (sent0,) = make_tiles(0, small + (block_plane, block_segment), density_blocks, basis)
+    sent1, base = make_tiles(1, small, density_blocks, basis)
     got = [exchanged(sent0), exchanged(sent1)]
 
     own, rim, half, places = gather_tiles(0, got[0], ext_potential)
@@ -399,8 +424,8 @@
     returned1 = exchanged(cubes)
     density = from_homes(density)
 
-    matrices = make_matrices(0, base, kinds, returned0, basis)
-    matrices = make_matrices(1, base, kinds, returned1, basis, matrices)
+    (partial,) = make_matrices(0, base, kinds, returned0, basis)
+    matrices, density = make_matrices(1, base, kinds, returned1, basis, partial, density)
     return density, matrices
 
 

time: 157 us -> 142 us (0.904)
  the two profiles are of different devices: /device:TPU:3 before, /device:TPU:1 now
where the time goes in v4:
time: 142 us
  Pallas kernels  54 us (38%)
  starting transfers between devices  46.5 us (33%)
  waiting for transfers between devices  40.5 us (29%)
    all_to_all x4, starting transfers between devices, exchanged(): return lax.all_to_all(x, AXES, split_axis=0, concat_axis=0, tiled=True)  40.8 us
    all_to_all x4, waiting for transfers between devices, exchanged(): return lax.all_to_all(x, AXES, split_axis=0, concat_axis=0, tiled=True)  27 us
    pallas_call x2, Pallas kernels, make_tiles(): pl.pallas_call(lambda *refs: tiles_kernel(h, *refs), grid=(STEPS,), in_sp...  22.9 us
    pallas_call x2, Pallas kernels, make_matrices(): pl.pallas_call(lambda *refs: matrix_kernel(h, *refs), grid=(STEPS,), in_s...  21 us
    ppermute x4, waiting for transfers between devices, shifted(): lax.ppermute(x, AXES, [(home(e), home((e + by) % DEVS)) for e in range(DE...  13.5 us
    pallas_call x2, Pallas kernels, cut_cubes(): pl.pallas_call(lambda *refs: cubes_kernel(h, *refs), in_specs=[SMEM] + [V...  4.73 us
    ppermute x4, starting transfers between devices, shifted(): lax.ppermute(x, AXES, [(home(e), home((e + by) % DEVS)) for e in range(DE...  4.15 us
    pallas_call x1, Pallas kernels, gather_tiles(): pl.pallas_call(gather_first, in_specs=[VMEM, VMEM], out_specs=[VMEM, VMEM...  3.75 us
  transfers between devices with their start and end apart: 10, of which 8 were waited for; matrix products, arithmetic and copies ran while one was open for 0% of the time, Pallas kernels for 23%

profile of v4, /device:TPU:1, one launch (start us, length us, event | category | flops | bytes accessed | tf_op | source)
XLA Modules:
  0.0 141.8 jit_solution(10352024114648643142)
XLA Ops:
  0.6 11.4 %shard_map.87 = bf16[1024,640]{1,0:T(8,128)(2,1)} custom-call(s32[1,64]{1,0:T(1,128)} %bitcast.18, s32[2,64]{1,0:T(2,128)} %bitcast.14, s32[64]{0:T(128)} %refs_2_.3, s32[64]{0:T(128)} %refs_3_.5, bf16[64,4096]{1,0:T(8,128)(2,1)} %refs_4_.5, bf16[4,64,4096]{2,1,0:T(8,128)(2,1)} %refs_4_.7, bf16[4,64,4096]{2,1,0:T(8,128)(2,1)} %refs_4_.7), custom_call_target="tpu_custom_call" | custom-call | flops 4294967296 | bytes 4194304 | tf_op jit(solution)/shard_map/pallas_call | solution.py:300
  12.0 11.9 %all-to-all-start = ((bf16[128,8,640]{2,1,0:T(8,128)(2,1)}), bf16[128,8,640]{2,1,0:T(8,128)(2,1)}, u32[]{:S(2)}, u32[]{:S(2)}) async-start(bf16[128,8,640]{2,1,0:T(8,128)(2,1)} %bitcast.11), calls=%async_computation | async-start | bytes 2621440 | tf_op jit(solution)/shard_map/all_to_all | solution.py:403
  23.9 11.5 %shard_map.86 = (bf16[1024,512]{1,0:T(8,128)(2,1)}, s32[64]{0:T(128)}) custom-call(s32[1,64]{1,0:T(1,128)} %bitcast.19, s32[2,64]{1,0:T(2,128)} %bitcast.15, bf16[64,4096]{1,0:T(8,128)(2,1)} %refs_4_.5, bf16[4,64,4096]{2,1,0:T(8,128)(2,1)} %refs_4_.7, bf16[4,64,4096]{2,1,0:T(8,128)(2,1)} %refs_4_.7), custom_call_target="tpu_custom_call" | custom-call | flops 4294967296 | bytes 4194304 | tf_op jit(solution)/shard_map/pallas_call | solution.py:300
  35.4 0.0 copy-start.1
  35.4 9.9 %all-to-all-done = bf16[128,8,640]{2,1,0:T(8,128)(2,1)} async-done(((bf16[128,8,640]{2,1,0:T(8,128)(2,1)}), bf16[128,8,640]{2,1,0:T(8,128)(2,1)}, u32[]{:S(2)}, u32[]{:S(2)}) %all-to-all-start) | async-done | bytes 1310752 | tf_op jit(solution)/shard_map/all_to_all | solution.py:403
  45.4 4.7 %all-to-all-start.1 = ((bf16[128,8,512]{2,1,0:T(8,128)(2,1)}), bf16[128,8,512]{2,1,0:T(8,128)(2,1)S(1)}, u32[]{:S(2)}, u32[]{:S(2)}) async-start(bf16[128,8,512]{2,1,0:T(8,128)(2,1)} %bitcast.13), calls=%async_computation.1 | async-start | bytes 2097152 | tf_op jit(solution)/shard_map/all_to_all | solution.py:403
  50.1 0.0 copy-done.1
  50.1 0.7 collective-permute-start
  50.8 0.0 collective-permute-done.ext_ref.refs_3_
  50.8 3.7 %gather_tiles0.1 = (f32[8,2048]{1,0:T(8,128)S(1)}, f32[8,2048]{1,0:T(8,128)S(1)}, f32[8,2048]{1,0:T(8,128)S(1)}, s32[8,128]{1,0:T(8,128)S(1)}) custom-call(bf16[1024,640]{1,0:T(8,128)(2,1)} %bitcast.3.got_ref, f32[8,4096]{1,0:T(8,128)S(1)} %collective-permute-done.ext_ref.refs_3_), custom_call_target="tpu_custom_call" | custom-call | flops 1048576 | bytes 3145728 | tf_op jit(solution)/shard_map/gather_tiles0/pallas_call | solution.py:324
  54.5 2.1 %collective-permute-start.3 = (f32[8,2048]{1,0:T(8,128)S(1)}, f32[8,2048]{1,0:T(8,128)S(1)}, u32[]{:S(2)}, u32[]{:S(2)}) collective-permute-start(f32[8,2048]{1,0:T(8,128)S(1)} %get-tuple-element.24.refs_2_), channel_id=1, source_target_pairs={{0,1},{1,2},{2,3},{3,4},{4,5},{5,6},{6,7},{7,14},{14,15},{15,12},{... | collective-permute-start | bytes 196616 | tf_op jit(solution)/shard_map/ppermute | solution.py:391
  56.6 0.0 collective-permute-start.4
  56.6 2.7 %collective-permute-done.3.refs_4_ = f32[8,2048]{1,0:T(8,128)S(1)} collective-permute-done((f32[8,2048]{1,0:T(8,128)S(1)}, f32[8,2048]{1,0:T(8,128)S(1)}, u32[]{:S(2)}, u32[]{:S(2)}) %collective-permute-start.3) | collective-permute-done | bytes 65568 | tf_op jit(solution)/shard_map/ppermute | solution.py:391
  59.4 2.9 %collective-permute-done.4.refs_5_ = f32[8,2048]{1,0:T(8,128)S(1)} collective-permute-done((f32[8,2048]{1,0:T(8,128)S(1)}, f32[8,2048]{1,0:T(8,128)S(1)}, u32[]{:S(2)}, u32[]{:S(2)}) %collective-permute-start.4) | collective-permute-done | bytes 65568 | tf_op jit(solution)/shard_map/ppermute | solution.py:391
  62.3 2.3 %shard_map.88 = (f32[8,2048]{1,0:T(8,128)S(1)}, bf16[2048,256]{1,0:T(8,128)(2,1)}) custom-call(s32[8,128]{1,0:T(8,128)S(1)} %get-tuple-element.18.at_ref.refs_0_, f32[8,2048]{1,0:T(8,128)S(1)} %get-tuple-element.23.refs_1_, f32[8,2048]{1,0:T(8,128)S(1)} %get-tuple-element.24.refs_2_, f32[8,4096]{1,0:T(8,128)S(1)} %collective-permute-done.ext_ref.refs_3_, ...), custom_call_target="tpu_custom_call" | custom-call | flops 1048576 | bytes 3145728 | tf_op jit(solution)/shard_map/pallas_call | solution.py:353
  64.6 4.6 %all-to-all-done.1 = bf16[128,8,512]{2,1,0:T(8,128)(2,1)S(1)} async-done(((bf16[128,8,512]{2,1,0:T(8,128)(2,1)}), bf16[128,8,512]{2,1,0:T(8,128)(2,1)S(1)}, u32[]{:S(2)}, u32[]{:S(2)}) %all-to-all-start.1) | async-done | bytes 1048608 | tf_op jit(solution)/shard_map/all_to_all | solution.py:403
  69.2 17.2 %all-to-all-start.3 = ((bf16[128,16,256]{2,1,0:T(8,128)(2,1)}), bf16[128,16,256]{2,1,0:T(8,128)(2,1)S(1)}, u32[]{:S(2)}, u32[]{:S(2)}) async-start(bf16[128,16,256]{2,1,0:T(8,128)(2,1)} %bitcast.8), calls=%async_computation.3 | async-start | bytes 2097152 | tf_op jit(solution)/shard_map/all_to_all | solution.py:403
  86.4 1.7 %gather_tiles1.1 = (f32[8,2048]{1,0:T(8,128)S(1)}, f32[8,2048]{1,0:T(8,128)S(1)}, f32[8,2048]{1,0:T(8,128)S(1)}) custom-call(s32[8,128]{1,0:T(8,128)S(1)} %get-tuple-element.18.at_ref.refs_0_, bf16[1024,512]{1,0:T(8,128)(2,1)S(1)} %bitcast.10, f32[8,4096]{1,0:T(8,128)S(1)} %collective-permute-done.ext_ref.refs_3_), custom_call_target="tpu_custom_call" | custom-call | flops 1048576 | bytes 3145728 | tf_op jit(solution)/shard_map/gather_tiles1/pallas_call | solution.py:339
  88.1 2.1 %collective-permute-start.1 = (f32[8,2048]{1,0:T(8,128)S(1)}, f32[8,2048]{1,0:T(8,128)S(1)}, u32[]{:S(2)}, u32[]{:S(2)}) collective-permute-start(f32[8,2048]{1,0:T(8,128)S(1)} %get-tuple-element.21.refs_2_), channel_id=1, source_target_pairs={{0,1},{1,2},{2,3},{3,4},{4,5},{5,6},{6,7},{7,14},{14,15},{15,12},{... | collective-permute-start | bytes 196616 | tf_op jit(solution)/shard_map/ppermute | solution.py:391
  90.2 0.0 collective-permute-start.2
  90.2 4.7 %collective-permute-done.1.refs_4_ = f32[8,2048]{1,0:T(8,128)S(1)} collective-permute-done((f32[8,2048]{1,0:T(8,128)S(1)}, f32[8,2048]{1,0:T(8,128)S(1)}, u32[]{:S(2)}, u32[]{:S(2)}) %collective-permute-start.1) | collective-permute-done | bytes 65568 | tf_op jit(solution)/shard_map/ppermute | solution.py:391
  94.9 3.1 %collective-permute-done.2.refs_5_ = f32[8,2048]{1,0:T(8,128)S(1)} collective-permute-done((f32[8,2048]{1,0:T(8,128)S(1)}, f32[8,2048]{1,0:T(8,128)S(1)}, u32[]{:S(2)}, u32[]{:S(2)}) %collective-permute-start.2) | collective-permute-done | bytes 65568 | tf_op jit(solution)/shard_map/ppermute | solution.py:391
  98.0 2.4 %shard_map.89 = (f32[8,4096]{1,0:T(8,128)S(1)}, bf16[2048,256]{1,0:T(8,128)(2,1)}) custom-call(s32[8,128]{1,0:T(8,128)S(1)} %get-tuple-element.18.at_ref.refs_0_, f32[8,2048]{1,0:T(8,128)S(1)} %get-tuple-element.20.refs_1_, f32[8,2048]{1,0:T(8,128)S(1)} %get-tuple-element.21.refs_2_, f32[8,4096]{1,0:T(8,128)S(1)} %collective-permute-done.ext_ref.refs_3_, ...), custom_call_target="tpu_custom_call" | custom-call | flops 1048576 | bytes 3145728 | tf_op jit(solution)/shard_map/pallas_call | solution.py:353
  100.4 5.0 %all-to-all-done.3 = bf16[128,16,256]{2,1,0:T(8,128)(2,1)S(1)} async-done(((bf16[128,16,256]{2,1,0:T(8,128)(2,1)}), bf16[128,16,256]{2,1,0:T(8,128)(2,1)S(1)}, u32[]{:S(2)}, u32[]{:S(2)}) %all-to-all-start.3) | async-done | bytes 1048608 | tf_op jit(solution)/shard_map/all_to_all | solution.py:403
  105.4 0.0 copy-start
  105.4 7.1 %all-to-all-start.2 = ((bf16[128,16,256]{2,1,0:T(8,128)(2,1)}), bf16[128,16,256]{2,1,0:T(8,128)(2,1)}, u32[]{:S(2)}, u32[]{:S(2)}) async-start(bf16[128,16,256]{2,1,0:T(8,128)(2,1)} %bitcast.6), calls=%async_computation.2 | async-start | bytes 2097152 | tf_op jit(solution)/shard_map/all_to_all | solution.py:403
  112.5 0.8 collective-permute-start.5
  113.3 0.0 copy-done
  113.3 10.3 %shard_map.90.refs_5_ = f32[64,32,128]{2,1,0:T(8,128)} custom-call(s32[64]{0:T(128)} %get-tuple-element.17.refs_0_, s32[2,64]{1,0:T(2,128)} %bitcast.16, bf16[2048,256]{1,0:T(8,128)(2,1)} %bitcast.12, bf16[4,64,4096]{2,1,0:T(8,128)(2,1)} %refs_4_.7, bf16[4,64,4096]{2,1,0:T(8,128)(2,1)} %refs_4_.7), custom_call_target="tpu_custom_call" | custom-call | flops 4294967296 | bytes 4194304 | tf_op jit(solution)/shard_map/pallas_call | solution.py:370
  123.6 0.0 collective-permute-done.5.refs_6_
  123.6 0.0 copy-start.2
  123.6 7.5 %all-to-all-done.2 = bf16[128,16,256]{2,1,0:T(8,128)(2,1)} async-done(((bf16[128,16,256]{2,1,0:T(8,128)(2,1)}), bf16[128,16,256]{2,1,0:T(8,128)(2,1)}, u32[]{:S(2)}, u32[]{:S(2)}) %all-to-all-start.2) | async-done | bytes 1048608 | tf_op jit(solution)/shard_map/all_to_all | solution.py:403
  131.1 0.0 copy-done.2
  131.1 10.7 %shard_map.91 = (bf16[64,4096]{1,0:T(8,128)(2,1)}, f32[8,4096]{1,0:T(8,128)}) custom-call(s32[64]{0:T(128)} %get-tuple-element.17.refs_0_, s32[2,64]{1,0:T(2,128)} %bitcast.17, bf16[2048,256]{1,0:T(8,128)(2,1)} %bitcast.7.refs_2_, bf16[4,64,4096]{2,1,0:T(8,128)(2,1)} %refs_4_.7, bf16[4,64,4096]{2,1,0:T(8,128)(2,1)} %refs_4_.7, ...), custom_call_target="tpu_custom_call" | custom-call | flops 4294967296 | bytes 4194304 | tf_op jit(solution)/shard_map/pallas_call | solution.py:370
Async XLA Ops:
  12.0 33.4 %all-to-all-start = ((bf16[128,8,640]{2,1,0:T(8,128)(2,1)}), bf16[128,8,640]{2,1,0:T(8,128)(2,1)}, u32[]{:S(2)}, u32[]{:S(2)}) async-start(bf16[128,8,640]{2,1,0:T(8,128)(2,1)} %bitcast.11), calls=%async_computation | async-start | bytes 2621440 | tf_op jit(solution)/shard_map/all_to_all | solution.py:403
  35.4 14.7 %copy-start.1 = (f32[8,4096]{1,0:T(8,128)S(1)}, f32[8,4096]{1,0:T(8,128)}, u32[]{:S(2)}) copy-start(f32[8,4096]{1,0:T(8,128)} %param.13) | copy-start | bytes 393220
  45.4 23.8 %all-to-all-start.1 = ((bf16[128,8,512]{2,1,0:T(8,128)(2,1)}), bf16[128,8,512]{2,1,0:T(8,128)(2,1)S(1)}, u32[]{:S(2)}, u32[]{:S(2)}) async-start(bf16[128,8,512]{2,1,0:T(8,128)(2,1)} %bitcast.13), calls=%async_computation.1 | async-start | bytes 2097152 | tf_op jit(solution)/shard_map/all_to_all | solution.py:403
  50.1 0.7 collective-permute-start
  54.5 4.8 %collective-permute-start.3 = (f32[8,2048]{1,0:T(8,128)S(1)}, f32[8,2048]{1,0:T(8,128)S(1)}, u32[]{:S(2)}, u32[]{:S(2)}) collective-permute-start(f32[8,2048]{1,0:T(8,128)S(1)} %get-tuple-element.24.refs_2_), channel_id=1, source_target_pairs={{0,1},{1,2},{2,3},{3,4},{4,5},{5,6},{6,7},{7,14},{14,15},{15,12},{... | collective-permute-start | bytes 196616 | tf_op jit(solution)/shard_map/ppermute | solution.py:391
  56.6 5.7 %collective-permute-start.4 = (f32[8,2048]{1,0:T(8,128)S(1)}, f32[8,2048]{1,0:T(8,128)S(1)}, u32[]{:S(2)}, u32[]{:S(2)}) collective-permute-start(f32[8,2048]{1,0:T(8,128)S(1)} %get-tuple-element.25), channel_id=1, source_target_pairs={{0,97},{1,0},{2,1},{3,2},{4,3},{5,4},{6,5},{7,6},{14,7},{15,14},{1... | collective-permute-start | bytes 196616 | tf_op jit(solution)/shard_map/ppermute | solution.py:391
  69.2 36.2 %all-to-all-start.3 = ((bf16[128,16,256]{2,1,0:T(8,128)(2,1)}), bf16[128,16,256]{2,1,0:T(8,128)(2,1)S(1)}, u32[]{:S(2)}, u32[]{:S(2)}) async-start(bf16[128,16,256]{2,1,0:T(8,128)(2,1)} %bitcast.8), calls=%async_computation.3 | async-start | bytes 2097152 | tf_op jit(solution)/shard_map/all_to_all | solution.py:403
  88.1 6.8 %collective-permute-start.1 = (f32[8,2048]{1,0:T(8,128)S(1)}, f32[8,2048]{1,0:T(8,128)S(1)}, u32[]{:S(2)}, u32[]{:S(2)}) collective-permute-start(f32[8,2048]{1,0:T(8,128)S(1)} %get-tuple-element.21.refs_2_), channel_id=1, source_target_pairs={{0,1},{1,2},{2,3},{3,4},{4,5},{5,6},{6,7},{7,14},{14,15},{15,12},{... | collective-permute-start | bytes 196616 | tf_op jit(solution)/shard_map/ppermute | solution.py:391
  90.2 7.8 %collective-permute-start.2 = (f32[8,2048]{1,0:T(8,128)S(1)}, f32[8,2048]{1,0:T(8,128)S(1)}, u32[]{:S(2)}, u32[]{:S(2)}) collective-permute-start(f32[8,2048]{1,0:T(8,128)S(1)} %get-tuple-element.22), channel_id=1, source_target_pairs={{0,97},{1,0},{2,1},{3,2},{4,3},{5,4},{6,5},{7,6},{14,7},{15,14},{1... | collective-permute-start | bytes 196616 | tf_op jit(solution)/shard_map/ppermute | solution.py:391
  105.4 7.9 %copy-start = (bf16[128,16,256]{2,1,0:T(8,128)(2,1)}, bf16[128,16,256]{2,1,0:T(8,128)(2,1)S(1)}, u32[]{:S(2)}) copy-start(bf16[128,16,256]{2,1,0:T(8,128)(2,1)S(1)} %all-to-all-done.3) | copy-start | bytes 3145732
  105.4 25.7 %all-to-all-start.2 = ((bf16[128,16,256]{2,1,0:T(8,128)(2,1)}), bf16[128,16,256]{2,1,0:T(8,128)(2,1)}, u32[]{:S(2)}, u32[]{:S(2)}) async-start(bf16[128,16,256]{2,1,0:T(8,128)(2,1)} %bitcast.6), calls=%async_computation.2 | async-start | bytes 2097152 | tf_op jit(solution)/shard_map/all_to_all | solution.py:403
  112.5 11.2 %collective-permute-start.5 = (f32[8,4096]{1,0:T(8,128)S(1)}, f32[8,4096]{1,0:T(8,128)S(1)}, u32[]{:S(2)}, u32[]{:S(2)}) collective-permute-start(f32[8,4096]{1,0:T(8,128)S(1)} %get-tuple-element.29), channel_id=1, source_target_pairs={{0,0},{1,1},{2,2},{3,3},{4,4},{5,5},{6,6},{7,7},{14,8},{15,9},{12,... | collective-permute-start | bytes 393224 | tf_op jit(solution)/shard_map/ppermute | solution.py:399
  123.6 7.5 %copy-start.2 = (f32[8,4096]{1,0:T(8,128)}, f32[8,4096]{1,0:T(8,128)S(1)}, u32[]{:S(2)}) copy-start(f32[8,4096]{1,0:T(8,128)S(1)} %collective-permute-done.5.refs_6_) | copy-start | bytes 393220

commit v5 on v4

--- a/solution.py
+++ b/solution.py
@@ -168,8 +168,8 @@
                 out_ref[rows, 2 * HALF :] = jnp.concatenate(marks, axis=0).astype(BF16)
 
 
-def spread(at_ref, got_ref, ext_ref, own_ref, rim_ref, half_ref, acc, h):
-    acc[...] = jnp.zeros_like(acc)
+def spread(at_ref, got_ref, ext_ref, own_ref, rim_ref, near_ref, far_ref, acc, h):
+    even = lax.axis_index("slab") == 0
 
     @pl.loop(0, DEVS // 2, unroll=2)
     def _(q):
@@ -189,37 +189,48 @@
             grid = slice(s * SEGW + h * HALF + l * LANES, s * SEGW + h * HALF + (l + 1) * LANES)
             row = 2 * CZB * n
             own = acc[row : row + CZB, :]
+            rim = acc[row + CZB : row + 2 * CZB, :]
+            half = ext_ref[:, grid] + 0.5 * own
             own_ref[:, cells] = own
-            rim_ref[:, cells] = acc[row + CZB : row + 2 * CZB, :]
-            half_ref[:, cells] = ext_ref[:, grid] + 0.5 * own
-
-
-def gather_first(got_ref, ext_ref, own_ref, rim_ref, half_ref, at_ref, marks, places, acc, sem):
+            rim_ref[:, cells] = rim
+            near_ref[:, cells] = jnp.where(even, rim, half)
+            far_ref[:, cells] = jnp.where(even, half, rim)
+
+
+def gather_first(
+    got_ref, ext_ref, own_ref, rim_ref, near_ref, far_ref, at_ref, marks, places, acc, sem
+):
     marks[...] = got_ref[:, 2 * HALF :].astype(F32)
     across = marks[pl.ds(0, DEVS, stride=CZB), :].T
     codes = across[0:2, :].astype(jnp.int32)
     places[0:2, :] = (codes >> 3) + (codes & 7) * (2 * CZB * LPS)
     copy = pltpu.make_async_copy(places, at_ref, sem)
     copy.start()
+    acc[...] = jnp.zeros_like(acc)
     copy.wait()
-    spread(at_ref, got_ref, ext_ref, own_ref, rim_ref, half_ref, acc, 0)
-
-
-def gather_second(at_ref, got_ref, ext_ref, own_ref, rim_ref, half_ref, acc):
-    spread(at_ref, got_ref, ext_ref, own_ref, rim_ref, half_ref, acc, 1)
-
-
-def cubes_kernel(h, at_ref, own_ref, rim_ref, ext_ref, below_ref, above_ref, *rest):
+    spread(at_ref, got_ref, ext_ref, own_ref, rim_ref, near_ref, far_ref, acc, 0)
+
+
+def gather_second(at_ref, got_ref, ext_ref, own_ref, rim_ref, near_ref, far_ref, acc):
+    acc[...] = jnp.zeros_like(acc)
+    spread(at_ref, got_ref, ext_ref, own_ref, rim_ref, near_ref, far_ref, acc, 1)
+
+
+def cubes_kernel(h, at_ref, own_ref, rim_ref, ext_ref, near_ref, far_ref, *rest):
     if h == 0:
         dens_ref, out_ref, pot = rest
     else:
         other_ref, dens_ref, out_ref, pot = rest
+    even = lax.axis_index("slab") == 0
     for s in range(SEGS):
         for l in range(LPS):
             n = s * LPS + l
             cells = slice(n * LANES, (n + 1) * LANES)
             grid = slice(s * SEGW + h * HALF + l * LANES, s * SEGW + h * HALF + (l + 1) * LANES)
-            density = own_ref[:, cells] + below_ref[:, cells]
+            near, far = near_ref[:, cells], far_ref[:, cells]
+            below = jnp.where(even, far, near)
+            above = jnp.where(even, near, far)
+            density = own_ref[:, cells] + below
             if h == 0:
                 dens_ref[:, cells] = density
             else:
@@ -227,7 +238,7 @@
                 dens_ref[:, s * SEGW + l * LANES : s * SEGW + (l + 1) * LANES] = other_ref[:, cells]
             row = 2 * CZB * n
             pot[row : row + CZB, :] = ext_ref[:, grid] + 0.5 * density
-            pot[row + CZB : row + 2 * CZB, :] = above_ref[:, cells] + 0.5 * rim_ref[:, cells]
+            pot[row + CZB : row + 2 * CZB, :] = above + 0.5 * rim_ref[:, cells]
 
     @pl.loop(0, DEVS, unroll=4)
     def _(d):
@@ -241,7 +252,7 @@
     if h == 0:
         out_ref, acc, pot, perm, shuffled = rest
     else:
-        other_ref, dens_ref, out_ref, dens_out, acc, pot, perm, shuffled, vn = rest
+        other_ref, out_ref, acc, pot, perm, shuffled, vn = rest
     i = pl.program_id(0)
     pairs = BS // 2
 
@@ -291,7 +302,6 @@
                 vn[b] = block + other_ref[b]
 
         if h == 1:
-            dens_out[...] = dens_ref[...]
             out_ref[...] = vn[...].reshape(NB, BS * BS).astype(BF16)
 
 
@@ -324,8 +334,8 @@
         return pl.pallas_call(
             gather_first,
             in_specs=[VMEM, VMEM],
-            out_specs=[VMEM, VMEM, VMEM, SMEM],
-            out_shape=[part, part, part, jax.ShapeDtypeStruct((8, DEVS), jnp.int32)],
+            out_specs=[VMEM, VMEM, VMEM, VMEM, SMEM],
+            out_shape=[part, part, part, part, jax.ShapeDtypeStruct((8, DEVS), jnp.int32)],
             scratch_shapes=[
                 pltpu.VMEM((DEVS * CZB, LANES), F32),
                 pltpu.VMEM((8, DEVS), jnp.int32),
@@ -339,8 +349,8 @@
     return pl.pallas_call(
         gather_second,
         in_specs=[SMEM, VMEM, VMEM],
-        out_specs=[VMEM, VMEM, VMEM],
-        out_shape=[part, part, part],
+        out_specs=[VMEM, VMEM, VMEM, VMEM],
+        out_shape=[part, part, part, part],
         scratch_shapes=[acc],
         cost_estimate=cost(1 << 20, 3 << 20),
         compiler_params=room(SMALL_MIB),
@@ -348,7 +358,7 @@
     )(places, got, ext_potential)
 
 
-def cut_cubes(h, places, own, rim, ext_potential, below, above, *other):
+def cut_cubes(h, places, own, rim, ext_potential, near, far, *other):
     width = PLANE // HALVES if h == 0 else PLANE
     return pl.pallas_call(
         lambda *refs: cubes_kernel(h, *refs),
@@ -361,7 +371,7 @@
         scratch_shapes=[pltpu.VMEM((SEGS * LPS * 2 * CZB, LANES), F32)],
         cost_estimate=cost(1 << 20, 3 << 20),
         compiler_params=room(SMALL_MIB),
-    )(places, own, rim, ext_potential, below, above, *other)
+    )(places, own, rim, ext_potential, near, far, *other)
 
 
 def make_matrices(h, base, kinds, returned, basis, *other):
@@ -372,9 +382,9 @@
         grid=(STEPS,),
         in_specs=[SMEM, SMEM, whole((DEVS * 16, HALF))]
         + basis_specs(h)
-        + ([whole(blocks), whole((CZB, PLANE))] if h == 1 else []),
-        out_specs=[whole(out[0])] + [whole((CZB, PLANE))] * h,
-        out_shape=[jax.ShapeDtypeStruct(*out)] + [jax.ShapeDtypeStruct((CZB, PLANE), F32)] * h,
+        + [whole(blocks)] * h,
+        out_specs=whole(out[0]),
+        out_shape=jax.ShapeDtypeStruct(*out),
         scratch_shapes=[
             pltpu.VMEM((NB * BS, KINDS * BS), F32),
             pltpu.VMEM((DEVS * 16, HALF), F32),
@@ -387,8 +397,26 @@
     )(base, kinds, returned, basis, basis, *other)
 
 
-def shifted(x, by):
-    return lax.ppermute(x, AXES, [(home(e), home((e + by) % DEVS)) for e in range(DEVS)])
+def swapped(near, far):
+    pairs = [(home(e), home(e ^ 1)) for e in range(DEVS)]
+    next_pairs = [(home(e), home((((e + 1) ^ 1) - 1) % DEVS)) for e in range(DEVS)]
+    return lax.ppermute(near, AXES, pairs), lax.ppermute(far, AXES, next_pairs)
+
+
+def copy_kernel(in_ref, out_ref):
+    out_ref[...] = in_ref[...]
+
+
+def written(x):
+    return pl.pallas_call(
+        copy_kernel,
+        in_specs=[VMEM],
+        out_specs=VMEM,
+        out_shape=jax.ShapeDtypeStruct(x.shape, x.dtype),
+        compiler_params=room(SMALL_MIB),
+        cost_estimate=cost(1 << 10, 1 << 18),
+        name="written",
+    )(x)
 
 
 def to_homes(x):
@@ -413,19 +441,20 @@
     sent1, base = make_tiles(1, small, density_blocks, basis)
     got = [exchanged(sent0), exchanged(sent1)]
 
-    own, rim, half, places = gather_tiles(0, got[0], ext_potential)
-    below, above = shifted(rim, 1), shifted(half, -1)
-    density, cubes = cut_cubes(0, places, own, rim, ext_potential, below, above)
+    own, rim, near, far, places = gather_tiles(0, got[0], ext_potential)
+    near, far = swapped(near, far)
+    density, cubes = cut_cubes(0, places, own, rim, ext_potential, near, far)
     returned0 = exchanged(cubes)
 
-    own, rim, half = gather_tiles(1, got[1], ext_potential, places)
-    below, above = shifted(rim, 1), shifted(half, -1)
-    density, cubes = cut_cubes(1, places, own, rim, ext_potential, below, above, density)
+    own, rim, near, far = gather_tiles(1, got[1], ext_potential, places)
+    near, far = swapped(near, far)
+    density, cubes = cut_cubes(1, places, own, rim, ext_potential, near, far, density)
     returned1 = exchanged(cubes)
     density = from_homes(density)
 
-    (partial,) = make_matrices(0, base, kinds, returned0, basis)
-    matrices, density = make_matrices(1, base, kinds, returned1, basis, partial, density)
+    density = written(density)
+    partial = make_matrices(0, base, kinds, returned0, basis)
+    matrices = make_matrices(1, base, kinds, returned1, basis, partial)
     return density, matrices
 
 

time: 142 us -> 152 us (1.070)
  the two profiles are of different devices: /device:TPU:1 before, /device:TPU:3 now
where the time goes in v5:
time: 152 us; the launch traced here: 151 us
  Pallas kernels  55.4 us (36%)
  waiting for transfers between devices  50 us (33%)
  starting transfers between devices  45 us (30%)
    all_to_all x4, starting transfers between devices, exchanged(): return lax.all_to_all(x, AXES, split_axis=0, concat_axis=0, tiled=True)  30.1 us
    pallas_call x2, Pallas kernels, make_tiles(): pl.pallas_call(lambda *refs: tiles_kernel(h, *refs), grid=(STEPS,), in_sp...  22.9 us
    pallas_call x2, Pallas kernels, make_matrices(): pl.pallas_call(lambda *refs: matrix_kernel(h, *refs), grid=(STEPS,), in_s...  20.9 us
    ppermute x1, waiting for transfers between devices, to_homes(): return lax.ppermute(x, AXES, [(e, home(e)) for e in range(DEVS)])  14.7 us
    ppermute x2, waiting for transfers between devices, swapped(): lax.ppermute(far, AXES, next_pairs)  12.7 us
    ppermute x1, waiting for transfers between devices, from_homes(): return lax.ppermute(x, AXES, [(home(e), e) for e in range(DEVS)])  10.9 us
    all_to_all x4, waiting for transfers between devices, exchanged(): return lax.all_to_all(x, AXES, split_axis=0, concat_axis=0, tiled=True)  10.8 us
    ppermute x1, starting transfers between devices, from_homes(): return lax.ppermute(x, AXES, [(home(e), e) for e in range(DEVS)])  7.3 us
  transfers between devices with their start and end apart: 10, of which 7 were waited for; matrix products, arithmetic and copies ran while one was open for 0% of the time, Pallas kernels for 22%

profile of v5, /device:TPU:3, one launch (start us, length us, event | category | flops | bytes accessed | tf_op | source)
XLA Modules:
  0.0 151.1 jit_solution(789514632748041313)
XLA Ops:
  0.6 11.4 %shard_map.86 = bf16[1024,640]{1,0:T(8,128)(2,1)} custom-call(s32[1,64]{1,0:T(1,128)} %bitcast.18, s32[2,64]{1,0:T(2,128)} %bitcast.14, s32[64]{0:T(128)} %refs_2_.2, s32[64]{0:T(128)} %refs_3_.4, bf16[64,4096]{1,0:T(8,128)(2,1)} %refs_2_.3, bf16[4,64,4096]{2,1,0:T(8,128)(2,1)} %refs_4_.7, bf16[4,64,4096]{2,1,0:T(8,128)(2,1)} %refs_4_.7), custom_call_target="tpu_custom_call" | custom-call | flops 4294967296 | bytes 4194304 | tf_op jit(solution)/shard_map/pallas_call | solution.py:310
  12.0 11.2 %all-to-all-start = ((bf16[128,8,640]{2,1,0:T(8,128)(2,1)}), bf16[128,8,640]{2,1,0:T(8,128)(2,1)}, u32[]{:S(2)}, u32[]{:S(2)}) async-start(bf16[128,8,640]{2,1,0:T(8,128)(2,1)} %bitcast.11), calls=%async_computation | async-start | bytes 2621440 | tf_op jit(solution)/shard_map/all_to_all | solution.py:431
  23.2 11.5 %shard_map.87 = (bf16[1024,512]{1,0:T(8,128)(2,1)}, s32[64]{0:T(128)}) custom-call(s32[1,64]{1,0:T(1,128)} %bitcast.19, s32[2,64]{1,0:T(2,128)} %bitcast.15, bf16[64,4096]{1,0:T(8,128)(2,1)} %refs_2_.3, bf16[4,64,4096]{2,1,0:T(8,128)(2,1)} %refs_4_.7, bf16[4,64,4096]{2,1,0:T(8,128)(2,1)} %refs_4_.7), custom_call_target="tpu_custom_call" | custom-call | flops 4294967296 | bytes 4194304 | tf_op jit(solution)/shard_map/pallas_call | solution.py:310
  34.8 0.0 copy-start.1
  34.8 8.8 %all-to-all-done = bf16[128,8,640]{2,1,0:T(8,128)(2,1)} async-done(((bf16[128,8,640]{2,1,0:T(8,128)(2,1)}), bf16[128,8,640]{2,1,0:T(8,128)(2,1)}, u32[]{:S(2)}, u32[]{:S(2)}) %all-to-all-start) | async-done | bytes 1310752 | tf_op jit(solution)/shard_map/all_to_all | solution.py:431
  43.6 5.8 %all-to-all-start.1 = ((bf16[128,8,512]{2,1,0:T(8,128)(2,1)}), bf16[128,8,512]{2,1,0:T(8,128)(2,1)S(1)}, u32[]{:S(2)}, u32[]{:S(2)}) async-start(bf16[128,8,512]{2,1,0:T(8,128)(2,1)} %bitcast.13), calls=%async_computation.1 | async-start | bytes 2097152 | tf_op jit(solution)/shard_map/all_to_all | solution.py:431
  49.4 0.0 copy-done.1
  49.4 5.1 %collective-permute-start = (f32[8,4096]{1,0:T(8,128)S(1)}, f32[8,4096]{1,0:T(8,128)S(1)}, u32[]{:S(2)}, u32[]{:S(2)}) collective-permute-start(f32[8,4096]{1,0:T(8,128)S(1)} %copy-done.1), channel_id=1, source_target_pairs={{0,0},{1,1},{2,2},{3,3},{4,4},{5,5},{6,6},{7,7},{8,14},{9,15},{10,... | collective-permute-start | bytes 393224 | tf_op jit(solution)/shard_map/ppermute | solution.py:423
  54.5 14.7 %collective-permute-done.ext_ref.refs_3_ = f32[8,4096]{1,0:T(8,128)S(1)} collective-permute-done((f32[8,4096]{1,0:T(8,128)S(1)}, f32[8,4096]{1,0:T(8,128)S(1)}, u32[]{:S(2)}, u32[]{:S(2)}) %collective-permute-start) | collective-permute-done | bytes 131104 | tf_op jit(solution)/shard_map/ppermute | solution.py:423
  69.2 4.1 %gather_tiles0.1 = (f32[8,2048]{1,0:T(8,128)S(1)}, f32[8,2048]{1,0:T(8,128)S(1)}, f32[8,2048]{1,0:T(8,128)S(1)}, f32[8,2048]{1,0:T(8,128)S(1)}, s32[8,128]{1,0:T(8,128)S(1)}) custom-call(bf16[1024,640]{1,0:T(8,128)(2,1)} %bitcast.3.got_ref, f32[8,4096]{1,0:T(8,128)S(1)} %collective-permute-done.ext_ref.refs_3_), custom_call_target="tpu_custom_call" | custom-call | flops 1048576 | bytes 3145728 | tf_op jit(solution)/shard_map/gather_tiles0/pallas_call | solution.py:334
  73.3 0.9 collective-permute-start.3
  74.2 0.0 collective-permute-start.4
  74.2 0.9 collective-permute-done.3.refs_4_
  75.1 2.8 %collective-permute-done.4.refs_5_ = f32[8,2048]{1,0:T(8,128)S(1)} collective-permute-done((f32[8,2048]{1,0:T(8,128)S(1)}, f32[8,2048]{1,0:T(8,128)S(1)}, u32[]{:S(2)}, u32[]{:S(2)}) %collective-permute-start.4) | collective-permute-done | bytes 65568 | tf_op jit(solution)/shard_map/ppermute | solution.py:403
  77.9 2.4 %shard_map.88 = (f32[8,2048]{1,0:T(8,128)S(1)}, bf16[2048,256]{1,0:T(8,128)(2,1)}) custom-call(s32[8,128]{1,0:T(8,128)S(1)} %get-tuple-element.17.at_ref.refs_0_, f32[8,2048]{1,0:T(8,128)S(1)} %get-tuple-element.23.refs_1_, f32[8,2048]{1,0:T(8,128)S(1)} %get-tuple-element.24.refs_2_, f32[8,4096]{1,0:T(8,128)S(1)} %collective-permute-done.ext_ref.refs_3_, ...), custom_call_target="tpu_custom_call" | custom-call | flops 1048576 | bytes 3145728 | tf_op jit(solution)/shard_map/pallas_call | solution.py:363
  80.2 0.0 all-to-all-done.1
  80.3 5.0 %all-to-all-start.3 = ((bf16[128,16,256]{2,1,0:T(8,128)(2,1)}), bf16[128,16,256]{2,1,0:T(8,128)(2,1)S(1)}, u32[]{:S(2)}, u32[]{:S(2)}) async-start(bf16[128,16,256]{2,1,0:T(8,128)(2,1)} %bitcast.8), calls=%async_computation.3 | async-start | bytes 2097152 | tf_op jit(solution)/shard_map/all_to_all | solution.py:431
  85.3 2.1 %gather_tiles1.1 = (f32[8,2048]{1,0:T(8,128)S(1)}, f32[8,2048]{1,0:T(8,128)S(1)}, f32[8,2048]{1,0:T(8,128)S(1)}, f32[8,2048]{1,0:T(8,128)S(1)}) custom-call(s32[8,128]{1,0:T(8,128)S(1)} %get-tuple-element.17.at_ref.refs_0_, bf16[1024,512]{1,0:T(8,128)(2,1)S(1)} %bitcast.10, f32[8,4096]{1,0:T(8,128)S(1)} %collective-permute-done.ext_ref.refs_3_), custom_call_target="tpu_custom_call" | custom-call | flops 1048576 | bytes 3145728 | tf_op jit(solution)/shard_map/gather_tiles1/pallas_call | solution.py:349
  87.4 0.5 collective-permute-start.1
  87.9 1.2 collective-permute-start.2
  89.0 0.0 collective-permute-done.1.refs_4_
  89.0 9.9 %collective-permute-done.2.refs_5_ = f32[8,2048]{1,0:T(8,128)S(1)} collective-permute-done((f32[8,2048]{1,0:T(8,128)S(1)}, f32[8,2048]{1,0:T(8,128)S(1)}, u32[]{:S(2)}, u32[]{:S(2)}) %collective-permute-start.2) | collective-permute-done | bytes 65568 | tf_op jit(solution)/shard_map/ppermute | solution.py:403
  99.0 2.4 %shard_map.89 = (f32[8,4096]{1,0:T(8,128)S(1)}, bf16[2048,256]{1,0:T(8,128)(2,1)}) custom-call(s32[8,128]{1,0:T(8,128)S(1)} %get-tuple-element.17.at_ref.refs_0_, f32[8,2048]{1,0:T(8,128)S(1)} %get-tuple-element.19.refs_1_, f32[8,2048]{1,0:T(8,128)S(1)} %get-tuple-element.20.refs_2_, f32[8,4096]{1,0:T(8,128)S(1)} %collective-permute-done.ext_ref.refs_3_, ...), custom_call_target="tpu_custom_call" | custom-call | flops 1048576 | bytes 3145728 | tf_op jit(solution)/shard_map/pallas_call | solution.py:363
  101.3 1.9 %all-to-all-done.3 = bf16[128,16,256]{2,1,0:T(8,128)(2,1)S(1)} async-done(((bf16[128,16,256]{2,1,0:T(8,128)(2,1)}), bf16[128,16,256]{2,1,0:T(8,128)(2,1)S(1)}, u32[]{:S(2)}, u32[]{:S(2)}) %all-to-all-start.3) | async-done | bytes 1048608 | tf_op jit(solution)/shard_map/all_to_all | solution.py:431
  103.3 0.0 copy-start
  103.3 8.1 %all-to-all-start.2 = ((bf16[128,16,256]{2,1,0:T(8,128)(2,1)}), bf16[128,16,256]{2,1,0:T(8,128)(2,1)}, u32[]{:S(2)}, u32[]{:S(2)}) async-start(bf16[128,16,256]{2,1,0:T(8,128)(2,1)} %bitcast.6), calls=%async_computation.2 | async-start | bytes 2097152 | tf_op jit(solution)/shard_map/all_to_all | solution.py:431
  111.3 7.3 %collective-permute-start.5 = (f32[8,4096]{1,0:T(8,128)S(1)}, f32[8,4096]{1,0:T(8,128)S(1)}, u32[]{:S(2)}, u32[]{:S(2)}) collective-permute-start(f32[8,4096]{1,0:T(8,128)S(1)} %get-tuple-element.28), channel_id=1, source_target_pairs={{0,0},{1,1},{2,2},{3,3},{4,4},{5,5},{6,6},{7,7},{14,8},{15,9},{12,... | collective-permute-start | bytes 393224 | tf_op jit(solution)/shard_map/ppermute | solution.py:427
  118.6 10.9 %collective-permute-done.5.in_ref = f32[8,4096]{1,0:T(8,128)S(1)} collective-permute-done((f32[8,4096]{1,0:T(8,128)S(1)}, f32[8,4096]{1,0:T(8,128)S(1)}, u32[]{:S(2)}, u32[]{:S(2)}) %collective-permute-start.5) | collective-permute-done | bytes 131104 | tf_op jit(solution)/shard_map/ppermute | solution.py:427
  129.5 0.7 written.1
  130.2 0.0 copy-done
  130.2 10.2 %shard_map.90.refs_5_ = f32[64,32,128]{2,1,0:T(8,128)} custom-call(s32[64]{0:T(128)} %get-tuple-element.29.refs_0_, s32[2,64]{1,0:T(2,128)} %bitcast.16, bf16[2048,256]{1,0:T(8,128)(2,1)} %bitcast.12, bf16[4,64,4096]{2,1,0:T(8,128)(2,1)} %refs_4_.7, bf16[4,64,4096]{2,1,0:T(8,128)(2,1)} %refs_4_.7), custom_call_target="tpu_custom_call" | custom-call | flops 4294967296 | bytes 4194304 | tf_op jit(solution)/shard_map/pallas_call | solution.py:380
  140.4 0.0 all-to-all-done.2
  140.4 10.6 %shard_map.91 = bf16[64,4096]{1,0:T(8,128)(2,1)} custom-call(s32[64]{0:T(128)} %get-tuple-element.29.refs_0_, s32[2,64]{1,0:T(2,128)} %bitcast.17, bf16[2048,256]{1,0:T(8,128)(2,1)} %bitcast.7.refs_2_, bf16[4,64,4096]{2,1,0:T(8,128)(2,1)} %refs_4_.7, bf16[4,64,4096]{2,1,0:T(8,128)(2,1)} %refs_4_.7, f32[64,32,128]{2,1,0:T(8,128)} %shard_map.90.refs_5_), custom_call_target="tpu_custom_call" | custom-call | flops 4294967296 | bytes 4194304 | tf_op jit(solution)/shard_map/pallas_call | solution.py:380
Async XLA Ops:
  12.0 31.6 %all-to-all-start = ((bf16[128,8,640]{2,1,0:T(8,128)(2,1)}), bf16[128,8,640]{2,1,0:T(8,128)(2,1)}, u32[]{:S(2)}, u32[]{:S(2)}) async-start(bf16[128,8,640]{2,1,0:T(8,128)(2,1)} %bitcast.11), calls=%async_computation | async-start | bytes 2621440 | tf_op jit(solution)/shard_map/all_to_all | solution.py:431
  34.8 14.6 %copy-start.1 = (f32[8,4096]{1,0:T(8,128)S(1)}, f32[8,4096]{1,0:T(8,128)}, u32[]{:S(2)}) copy-start(f32[8,4096]{1,0:T(8,128)} %param.13) | copy-start | bytes 393220
  43.6 36.6 %all-to-all-start.1 = ((bf16[128,8,512]{2,1,0:T(8,128)(2,1)}), bf16[128,8,512]{2,1,0:T(8,128)(2,1)S(1)}, u32[]{:S(2)}, u32[]{:S(2)}) async-start(bf16[128,8,512]{2,1,0:T(8,128)(2,1)} %bitcast.13), calls=%async_computation.1 | async-start | bytes 2097152 | tf_op jit(solution)/shard_map/all_to_all | solution.py:431
  49.4 19.8 %collective-permute-start = (f32[8,4096]{1,0:T(8,128)S(1)}, f32[8,4096]{1,0:T(8,128)S(1)}, u32[]{:S(2)}, u32[]{:S(2)}) collective-permute-start(f32[8,4096]{1,0:T(8,128)S(1)} %copy-done.1), channel_id=1, source_target_pairs={{0,0},{1,1},{2,2},{3,3},{4,4},{5,5},{6,6},{7,7},{8,14},{9,15},{10,... | collective-permute-start | bytes 393224 | tf_op jit(solution)/shard_map/ppermute | solution.py:423
  73.3 1.8 %collective-permute-start.3 = (f32[8,2048]{1,0:T(8,128)S(1)}, f32[8,2048]{1,0:T(8,128)S(1)}, u32[]{:S(2)}, u32[]{:S(2)}) collective-permute-start(f32[8,2048]{1,0:T(8,128)S(1)} %get-tuple-element.25), channel_id=1, source_target_pairs={{0,1},{1,0},{2,3},{3,2},{4,5},{5,4},{6,7},{7,6},{14,15},{15,14},{1... | collective-permute-start | bytes 196616 | tf_op jit(solution)/shard_map/ppermute | solution.py:403
  74.2 3.7 %collective-permute-start.4 = (f32[8,2048]{1,0:T(8,128)S(1)}, f32[8,2048]{1,0:T(8,128)S(1)}, u32[]{:S(2)}, u32[]{:S(2)}) collective-permute-start(f32[8,2048]{1,0:T(8,128)S(1)} %get-tuple-element.26), channel_id=1, source_target_pairs={{0,97},{1,2},{2,1},{3,4},{4,3},{5,6},{6,5},{7,14},{14,7},{15,12},{... | collective-permute-start | bytes 196616 | tf_op jit(solution)/shard_map/ppermute | solution.py:403
  80.3 23.0 %all-to-all-start.3 = ((bf16[128,16,256]{2,1,0:T(8,128)(2,1)}), bf16[128,16,256]{2,1,0:T(8,128)(2,1)S(1)}, u32[]{:S(2)}, u32[]{:S(2)}) async-start(bf16[128,16,256]{2,1,0:T(8,128)(2,1)} %bitcast.8), calls=%async_computation.3 | async-start | bytes 2097152 | tf_op jit(solution)/shard_map/all_to_all | solution.py:431
  87.4 1.7 %collective-permute-start.1 = (f32[8,2048]{1,0:T(8,128)S(1)}, f32[8,2048]{1,0:T(8,128)S(1)}, u32[]{:S(2)}, u32[]{:S(2)}) collective-permute-start(f32[8,2048]{1,0:T(8,128)S(1)} %get-tuple-element.21), channel_id=1, source_target_pairs={{0,1},{1,0},{2,3},{3,2},{4,5},{5,4},{6,7},{7,6},{14,15},{15,14},{1... | collective-permute-start | bytes 196616 | tf_op jit(solution)/shard_map/ppermute | solution.py:403
  87.9 11.1 %collective-permute-start.2 = (f32[8,2048]{1,0:T(8,128)S(1)}, f32[8,2048]{1,0:T(8,128)S(1)}, u32[]{:S(2)}, u32[]{:S(2)}) collective-permute-start(f32[8,2048]{1,0:T(8,128)S(1)} %get-tuple-element.22), channel_id=1, source_target_pairs={{0,97},{1,2},{2,1},{3,4},{4,3},{5,6},{6,5},{7,14},{14,7},{15,12},{... | collective-permute-start | bytes 196616 | tf_op jit(solution)/shard_map/ppermute | solution.py:403
  103.3 26.9 %copy-start = (bf16[128,16,256]{2,1,0:T(8,128)(2,1)}, bf16[128,16,256]{2,1,0:T(8,128)(2,1)S(1)}, u32[]{:S(2)}) copy-start(bf16[128,16,256]{2,1,0:T(8,128)(2,1)S(1)} %all-to-all-done.3) | copy-start | bytes 3145732
  103.3 37.2 %all-to-all-start.2 = ((bf16[128,16,256]{2,1,0:T(8,128)(2,1)}), bf16[128,16,256]{2,1,0:T(8,128)(2,1)}, u32[]{:S(2)}, u32[]{:S(2)}) async-start(bf16[128,16,256]{2,1,0:T(8,128)(2,1)} %bitcast.6), calls=%async_computation.2 | async-start | bytes 2097152 | tf_op jit(solution)/shard_map/all_to_all | solution.py:431
  111.3 18.2 %collective-permute-start.5 = (f32[8,4096]{1,0:T(8,128)S(1)}, f32[8,4096]{1,0:T(8,128)S(1)}, u32[]{:S(2)}, u32[]{:S(2)}) collective-permute-start(f32[8,4096]{1,0:T(8,128)S(1)} %get-tuple-element.28), channel_id=1, source_target_pairs={{0,0},{1,1},{2,2},{3,3},{4,4},{5,5},{6,6},{7,7},{14,8},{15,9},{12,... | collective-permute-start | bytes 393224 | tf_op jit(solution)/shard_map/ppermute | solution.py:427

commit v6 on v5

--- a/solution.py
+++ b/solution.py
@@ -45,6 +45,10 @@
     return pltpu.CompilerParams(vmem_limit_bytes=mib << 20)
 
 
+def moved_spec():
+    return pl.BlockSpec((1, KINDS * BS, SEGW), lambda i: (i, 0, 0))
+
+
 def cost(flops, moved):
     return pl.CostEstimate(flops=flops, bytes_accessed=moved, transcendentals=0)
 
@@ -60,13 +64,6 @@
     z = zi + (x & 1) * (3 - 2 * zi)
     y = yi + (zi & 1) * (3 - 2 * yi)
     return (x * 4 + z) * 8 + y * 2 + (slab & 1)
-
-
-def first_slab(chip):
-    x, z, y = chip >> 4, (chip >> 2) & 3, chip & 3
-    zi = z + (x & 1) * (3 - 2 * z)
-    yi = y + (zi & 1) * (3 - 2 * y)
-    return 2 * (x * 16 + zi * 4 + yi)
 
 
 def even_rows_first():
@@ -84,7 +81,7 @@
     if h == 0:
         plane, seg, dens_ref, first, second, out_ref = refs[2:8]
     else:
-        dens_ref, first, second, out_ref, base = refs[2:7]
+        dens_ref, first, second, out_ref, base, moved_ref = refs[2:8]
     pn, lhs, a32, perm, tiles, idx = refs[-6:]
     i = pl.program_id(0)
     pairs = BS // 2
@@ -132,6 +129,8 @@
         tiles[pl.ds(NB * CZB, CZB), :] = jnp.zeros((CZB, HALF), F32)
 
     a32[...] = jnp.dot(perm[...], joined(first, second), preferred_element_type=F32)
+    if h == 1:
+        moved_ref[0] = a32[...].astype(BF16)
 
     @pl.loop(0, NB // GROUP)
     def _(g):
@@ -146,26 +145,28 @@
 
     @pl.when(i == STEPS - 1)
     def _():
-        lane = lax.broadcasted_iota(jnp.int32, (CZB, LANES), 1)
-
-        @pl.loop(0, DEVS // 2, unroll=4)
-        def _(q):
-            rows = pl.ds(pl.multiple_of(q * 16, 16), 16)
-            slab = first_slab(q)
-            slots = [idx[2 * slab + r] for r in range(4)]
-            at = [pl.multiple_of(e & (CODE - 1), CZB) for e in slots]
-            parts = [tiles[pl.ds(row, CZB), :] for row in at]
-            out_ref[rows, 0:HALF] = jnp.concatenate([parts[0], parts[2]], axis=0).astype(BF16)
-            out_ref[rows, HALF : 2 * HALF] = jnp.concatenate(
-                [parts[1], parts[3]], axis=0
-            ).astype(BF16)
-            if h == 0:
-                codes = [(e >> 10).astype(F32) for e in slots]
-                marks = [
-                    jnp.where(lane == 0, codes[2 * r], jnp.where(lane == 1, codes[2 * r + 1], 0.0))
-                    for r in range(2)
-                ]
-                out_ref[rows, 2 * HALF :] = jnp.concatenate(marks, axis=0).astype(BF16)
+        first_lane = lax.broadcasted_iota(jnp.int32, (CZB, LANES), 1) == 0
+
+        @pl.loop(0, DEVS // 8)
+        def _(g):
+            x, z = g >> 2, g & 3
+            zi = z + (x & 1) * (3 - 2 * z)
+            row_slab = 8 * (x * 4 + zi)
+            flip = zi & 1
+            for y in range(4):
+                rows = pl.ds(pl.multiple_of(g * 64, 64) + y * 16, 16)
+                slot = 2 * (row_slab + 2 * (y + flip * (3 - 2 * y)))
+                slots = [idx[slot + r] for r in range(4)]
+                at = [pl.multiple_of(e & (CODE - 1), CZB) for e in slots]
+                parts = [tiles[pl.ds(row, CZB), :] for row in at]
+                out_ref[rows, 0:HALF] = jnp.concatenate([parts[0], parts[2]], axis=0).astype(BF16)
+                out_ref[rows, HALF : 2 * HALF] = jnp.concatenate(
+                    [parts[1], parts[3]], axis=0
+                ).astype(BF16)
+                if h == 0:
+                    marks = [jnp.where(first_lane, slots[2 * r], slots[2 * r + 1]) for r in range(2)]
+                    marks = (jnp.concatenate(marks, axis=0) >> 10).astype(F32)
+                    out_ref[rows, 2 * HALF :] = marks.astype(BF16)
 
 
 def spread(at_ref, got_ref, ext_ref, own_ref, rim_ref, near_ref, far_ref, acc, h):
@@ -252,18 +253,21 @@
     if h == 0:
         out_ref, acc, pot, perm, shuffled = rest
     else:
-        other_ref, out_ref, acc, pot, perm, shuffled, vn = rest
+        other_ref, moved, out_ref, acc, pot, vn = rest
+        shuffled = moved.at[0]
     i = pl.program_id(0)
     pairs = BS // 2
 
     @pl.when(i == 0)
     def _():
         pot[...] = ret_ref[...].astype(F32)
-        perm[...] = even_rows_first()
-
-    shuffled[...] = jnp.dot(
-        perm[...], joined(first, second), preferred_element_type=F32
-    ).astype(BF16)
+        if h == 0:
+            perm[...] = even_rows_first()
+
+    if h == 0:
+        shuffled[...] = jnp.dot(
+            perm[...], joined(first, second), preferred_element_type=F32
+        ).astype(BF16)
 
     @pl.loop(0, NB // GROUP)
     def _(g):
@@ -311,9 +315,13 @@
         lambda *refs: tiles_kernel(h, *refs),
         grid=(STEPS,),
         in_specs=[SMEM] * len(small) + [whole((NB, BS * BS))] + basis_specs(h),
-        out_specs=[whole((DEVS * CZB, width))] + [SMEM] * h,
+        out_specs=[whole((DEVS * CZB, width))] + [SMEM, moved_spec()] * h,
         out_shape=[jax.ShapeDtypeStruct((DEVS * CZB, width), BF16)]
-        + [jax.ShapeDtypeStruct((NB,), jnp.int32)] * h,
+        + [
+            jax.ShapeDtypeStruct((NB,), jnp.int32),
+            jax.ShapeDtypeStruct((STEPS, KINDS * BS, SEGW), BF16),
+        ]
+        * h,
         scratch_shapes=[
             pltpu.VMEM((NB, BS // 2, LANES), F32),
             pltpu.VMEM((NB * BS, KINDS * BS), BF16),
@@ -382,15 +390,18 @@
         grid=(STEPS,),
         in_specs=[SMEM, SMEM, whole((DEVS * 16, HALF))]
         + basis_specs(h)
-        + [whole(blocks)] * h,
+        + [whole(blocks), moved_spec()] * h,
         out_specs=whole(out[0]),
         out_shape=jax.ShapeDtypeStruct(*out),
         scratch_shapes=[
             pltpu.VMEM((NB * BS, KINDS * BS), F32),
             pltpu.VMEM((DEVS * 16, HALF), F32),
+        ]
+        + [
             pltpu.VMEM((KINDS * BS, KINDS * BS), BF16),
             pltpu.VMEM((KINDS * BS, SEGW), BF16),
         ]
+        * (1 - h)
         + [pltpu.VMEM(blocks, F32)] * h,
         cost_estimate=cost(2 * NB * BS * KINDS * BS * CZB * HALF, 4 << 20),
         compiler_params=room(MATRICES_MIB),
@@ -438,7 +449,7 @@
     ext_potential = to_homes(ext_potential)
     small = (owner, kinds)
     (sent0,) = make_tiles(0, small + (block_plane, block_segment), density_blocks, basis)
-    sent1, base = make_tiles(1, small, density_blocks, basis)
+    sent1, base, moved = make_tiles(1, small, density_blocks, basis)
     got = [exchanged(sent0), exchanged(sent1)]
 
     own, rim, near, far, places = gather_tiles(0, got[0], ext_potential)
@@ -454,7 +465,7 @@
 
     density = written(density)
     partial = make_matrices(0, base, kinds, returned0, basis)
-    matrices = make_matrices(1, base, kinds, returned1, basis, partial)
+    matrices = make_matrices(1, base, kinds, returned1, basis, partial, moved)
     return density, matrices
 
 

time: 152 us -> 151 us (level)
  no operation moved by 1% of the time
where the time goes in v6:
time: 151 us; the launch traced here: 150 us
  Pallas kernels  54.5 us (36%)
  waiting for transfers between devices  50.1 us (33%)
  starting transfers between devices  44.9 us (30%)
    all_to_all x4, starting transfers between devices, exchanged(): return lax.all_to_all(x, AXES, split_axis=0, concat_axis=0, tiled=True)  30 us
    pallas_call x2, Pallas kernels, make_tiles(): pl.pallas_call(lambda *refs: tiles_kernel(h, *refs), grid=(STEPS,), in_sp...  22.5 us
    pallas_call x2, Pallas kernels, make_matrices(): pl.pallas_call(lambda *refs: matrix_kernel(h, *refs), grid=(STEPS,), in_s...  20.4 us
    ppermute x1, waiting for transfers between devices, to_homes(): return lax.ppermute(x, AXES, [(e, home(e)) for e in range(DEVS)])  14.7 us
    ppermute x2, waiting for transfers between devices, swapped(): lax.ppermute(far, AXES, next_pairs)  12.7 us
    all_to_all x4, waiting for transfers between devices, exchanged(): return lax.all_to_all(x, AXES, split_axis=0, concat_axis=0, tiled=True)  10.9 us
    ppermute x1, waiting for transfers between devices, from_homes(): return lax.ppermute(x, AXES, [(home(e), e) for e in range(DEVS)])  10.9 us
    ppermute x1, starting transfers between devices, from_homes(): return lax.ppermute(x, AXES, [(home(e), e) for e in range(DEVS)])  7.3 us
  transfers between devices with their start and end apart: 10, of which 7 were waited for; matrix products, arithmetic and copies ran while one was open for 0% of the time, Pallas kernels for 22%

profile of v6, /device:TPU:3, one launch (start us, length us, event | category | flops | bytes accessed | tf_op | source)
XLA Modules:
  0.0 150.3 jit_solution(2801939203658168820)
XLA Ops:
  0.6 11.1 %shard_map.86 = bf16[1024,640]{1,0:T(8,128)(2,1)} custom-call(s32[1,64]{1,0:T(1,128)} %bitcast.18, s32[2,64]{1,0:T(2,128)} %bitcast.14, s32[64]{0:T(128)} %refs_2_.2, s32[64]{0:T(128)} %refs_3_.4, bf16[64,4096]{1,0:T(8,128)(2,1)} %refs_2_.3, bf16[4,64,4096]{2,1,0:T(8,128)(2,1)} %refs_4_.7, bf16[4,64,4096]{2,1,0:T(8,128)(2,1)} %refs_4_.7), custom_call_target="tpu_custom_call" | custom-call | flops 4294967296 | bytes 4194304 | tf_op jit(solution)/shard_map/pallas_call | solution.py:314
  11.7 11.2 %all-to-all-start = ((bf16[128,8,640]{2,1,0:T(8,128)(2,1)}), bf16[128,8,640]{2,1,0:T(8,128)(2,1)}, u32[]{:S(2)}, u32[]{:S(2)}) async-start(bf16[128,8,640]{2,1,0:T(8,128)(2,1)} %bitcast.11), calls=%async_computation | async-start | bytes 2621440 | tf_op jit(solution)/shard_map/all_to_all | solution.py:442
  23.0 11.4 %shard_map.87 = (bf16[1024,512]{1,0:T(8,128)(2,1)}, s32[64]{0:T(128)}, bf16[4,256,512]{2,1,0:T(8,128)(2,1)}) custom-call(s32[1,64]{1,0:T(1,128)} %bitcast.19, s32[2,64]{1,0:T(2,128)} %bitcast.15, bf16[64,4096]{1,0:T(8,128)(2,1)} %refs_2_.3, bf16[4,64,4096]{2,1,0:T(8,128)(2,1)} %refs_4_.7, bf16[4,64,4096]{2,1,0:T(8,128)(2,1)} %refs_4_.7), custom_call_target="tpu_custom_call" | custom-call | flops 4294967296 | bytes 4194304 | tf_op jit(solution)/shard_map/pallas_call | solution.py:314
  34.4 0.0 copy-start.1
  34.4 9.0 %all-to-all-done = bf16[128,8,640]{2,1,0:T(8,128)(2,1)} async-done(((bf16[128,8,640]{2,1,0:T(8,128)(2,1)}), bf16[128,8,640]{2,1,0:T(8,128)(2,1)}, u32[]{:S(2)}, u32[]{:S(2)}) %all-to-all-start) | async-done | bytes 1310752 | tf_op jit(solution)/shard_map/all_to_all | solution.py:442
  43.4 5.8 %all-to-all-start.1 = ((bf16[128,8,512]{2,1,0:T(8,128)(2,1)}), bf16[128,8,512]{2,1,0:T(8,128)(2,1)S(1)}, u32[]{:S(2)}, u32[]{:S(2)}) async-start(bf16[128,8,512]{2,1,0:T(8,128)(2,1)} %bitcast.13), calls=%async_computation.1 | async-start | bytes 2097152 | tf_op jit(solution)/shard_map/all_to_all | solution.py:442
  49.1 0.0 copy-done.1
  49.2 5.1 %collective-permute-start = (f32[8,4096]{1,0:T(8,128)S(1)}, f32[8,4096]{1,0:T(8,128)S(1)}, u32[]{:S(2)}, u32[]{:S(2)}) collective-permute-start(f32[8,4096]{1,0:T(8,128)S(1)} %copy-done.1), channel_id=1, source_target_pairs={{0,0},{1,1},{2,2},{3,3},{4,4},{5,5},{6,6},{7,7},{8,14},{9,15},{10,... | collective-permute-start | bytes 393224 | tf_op jit(solution)/shard_map/ppermute | solution.py:434
  54.3 14.7 %collective-permute-done.ext_ref.refs_3_ = f32[8,4096]{1,0:T(8,128)S(1)} collective-permute-done((f32[8,4096]{1,0:T(8,128)S(1)}, f32[8,4096]{1,0:T(8,128)S(1)}, u32[]{:S(2)}, u32[]{:S(2)}) %collective-permute-start) | collective-permute-done | bytes 131104 | tf_op jit(solution)/shard_map/ppermute | solution.py:434
  68.9 4.1 %gather_tiles0.1 = (f32[8,2048]{1,0:T(8,128)S(1)}, f32[8,2048]{1,0:T(8,128)S(1)}, f32[8,2048]{1,0:T(8,128)S(1)}, f32[8,2048]{1,0:T(8,128)S(1)}, s32[8,128]{1,0:T(8,128)S(1)}) custom-call(bf16[1024,640]{1,0:T(8,128)(2,1)} %bitcast.3.got_ref, f32[8,4096]{1,0:T(8,128)S(1)} %collective-permute-done.ext_ref.refs_3_), custom_call_target="tpu_custom_call" | custom-call | flops 1048576 | bytes 3145728 | tf_op jit(solution)/shard_map/gather_tiles0/pallas_call | solution.py:342
  73.1 0.9 collective-permute-start.3
  73.9 0.0 collective-permute-start.4
  73.9 0.9 collective-permute-done.3.refs_4_
  74.8 2.8 %collective-permute-done.4.refs_5_ = f32[8,2048]{1,0:T(8,128)S(1)} collective-permute-done((f32[8,2048]{1,0:T(8,128)S(1)}, f32[8,2048]{1,0:T(8,128)S(1)}, u32[]{:S(2)}, u32[]{:S(2)}) %collective-permute-start.4) | collective-permute-done | bytes 65568 | tf_op jit(solution)/shard_map/ppermute | solution.py:414
  77.6 2.4 %shard_map.88 = (f32[8,2048]{1,0:T(8,128)S(1)}, bf16[2048,256]{1,0:T(8,128)(2,1)}) custom-call(s32[8,128]{1,0:T(8,128)S(1)} %get-tuple-element.18.at_ref.refs_0_, f32[8,2048]{1,0:T(8,128)S(1)} %get-tuple-element.24.refs_1_, f32[8,2048]{1,0:T(8,128)S(1)} %get-tuple-element.25.refs_2_, f32[8,4096]{1,0:T(8,128)S(1)} %collective-permute-done.ext_ref.refs_3_, ...), custom_call_target="tpu_custom_call" | custom-call | flops 1048576 | bytes 3145728 | tf_op jit(solution)/shard_map/pallas_call | solution.py:371
  80.0 0.0 all-to-all-done.1
  80.0 5.0 %all-to-all-start.3 = ((bf16[128,16,256]{2,1,0:T(8,128)(2,1)}), bf16[128,16,256]{2,1,0:T(8,128)(2,1)S(1)}, u32[]{:S(2)}, u32[]{:S(2)}) async-start(bf16[128,16,256]{2,1,0:T(8,128)(2,1)} %bitcast.8), calls=%async_computation.3 | async-start | bytes 2097152 | tf_op jit(solution)/shard_map/all_to_all | solution.py:442
  85.0 2.1 %gather_tiles1.1 = (f32[8,2048]{1,0:T(8,128)S(1)}, f32[8,2048]{1,0:T(8,128)S(1)}, f32[8,2048]{1,0:T(8,128)S(1)}, f32[8,2048]{1,0:T(8,128)S(1)}) custom-call(s32[8,128]{1,0:T(8,128)S(1)} %get-tuple-element.18.at_ref.refs_0_, bf16[1024,512]{1,0:T(8,128)(2,1)S(1)} %bitcast.10, f32[8,4096]{1,0:T(8,128)S(1)} %collective-permute-done.ext_ref.refs_3_), custom_call_target="tpu_custom_call" | custom-call | flops 1048576 | bytes 3145728 | tf_op jit(solution)/shard_map/gather_tiles1/pallas_call | solution.py:357
  87.1 0.5 collective-permute-start.1
  87.6 1.2 collective-permute-start.2
  88.8 0.0 collective-permute-done.1.refs_4_
  88.8 9.9 %collective-permute-done.2.refs_5_ = f32[8,2048]{1,0:T(8,128)S(1)} collective-permute-done((f32[8,2048]{1,0:T(8,128)S(1)}, f32[8,2048]{1,0:T(8,128)S(1)}, u32[]{:S(2)}, u32[]{:S(2)}) %collective-permute-start.2) | collective-permute-done | bytes 65568 | tf_op jit(solution)/shard_map/ppermute | solution.py:414
  98.7 2.4 %shard_map.89 = (f32[8,4096]{1,0:T(8,128)S(1)}, bf16[2048,256]{1,0:T(8,128)(2,1)}) custom-call(s32[8,128]{1,0:T(8,128)S(1)} %get-tuple-element.18.at_ref.refs_0_, f32[8,2048]{1,0:T(8,128)S(1)} %get-tuple-element.20.refs_1_, f32[8,2048]{1,0:T(8,128)S(1)} %get-tuple-element.21.refs_2_, f32[8,4096]{1,0:T(8,128)S(1)} %collective-permute-done.ext_ref.refs_3_, ...), custom_call_target="tpu_custom_call" | custom-call | flops 1048576 | bytes 3145728 | tf_op jit(solution)/shard_map/pallas_call | solution.py:371
  101.1 1.9 %all-to-all-done.3 = bf16[128,16,256]{2,1,0:T(8,128)(2,1)S(1)} async-done(((bf16[128,16,256]{2,1,0:T(8,128)(2,1)}), bf16[128,16,256]{2,1,0:T(8,128)(2,1)S(1)}, u32[]{:S(2)}, u32[]{:S(2)}) %all-to-all-start.3) | async-done | bytes 1048608 | tf_op jit(solution)/shard_map/all_to_all | solution.py:442
  103.0 0.0 copy-start
  103.0 8.1 %all-to-all-start.2 = ((bf16[128,16,256]{2,1,0:T(8,128)(2,1)}), bf16[128,16,256]{2,1,0:T(8,128)(2,1)}, u32[]{:S(2)}, u32[]{:S(2)}) async-start(bf16[128,16,256]{2,1,0:T(8,128)(2,1)} %bitcast.6), calls=%async_computation.2 | async-start | bytes 2097152 | tf_op jit(solution)/shard_map/all_to_all | solution.py:442
  111.1 7.3 %collective-permute-start.5 = (f32[8,4096]{1,0:T(8,128)S(1)}, f32[8,4096]{1,0:T(8,128)S(1)}, u32[]{:S(2)}, u32[]{:S(2)}) collective-permute-start(f32[8,4096]{1,0:T(8,128)S(1)} %get-tuple-element.29), channel_id=1, source_target_pairs={{0,0},{1,1},{2,2},{3,3},{4,4},{5,5},{6,6},{7,7},{14,8},{15,9},{12,... | collective-permute-start | bytes 393224 | tf_op jit(solution)/shard_map/ppermute | solution.py:438
  118.4 10.9 %collective-permute-done.5.in_ref = f32[8,4096]{1,0:T(8,128)S(1)} collective-permute-done((f32[8,4096]{1,0:T(8,128)S(1)}, f32[8,4096]{1,0:T(8,128)S(1)}, u32[]{:S(2)}, u32[]{:S(2)}) %collective-permute-start.5) | collective-permute-done | bytes 131104 | tf_op jit(solution)/shard_map/ppermute | solution.py:438
  129.2 0.7 written.1
  129.9 0.0 copy-done
  129.9 10.2 %shard_map.90.refs_5_ = f32[64,32,128]{2,1,0:T(8,128)} custom-call(s32[64]{0:T(128)} %get-tuple-element.30.refs_0_, s32[2,64]{1,0:T(2,128)} %bitcast.16, bf16[2048,256]{1,0:T(8,128)(2,1)} %bitcast.12, bf16[4,64,4096]{2,1,0:T(8,128)(2,1)} %refs_4_.7, bf16[4,64,4096]{2,1,0:T(8,128)(2,1)} %refs_4_.7), custom_call_target="tpu_custom_call" | custom-call | flops 4294967296 | bytes 4194304 | tf_op jit(solution)/shard_map/pallas_call | solution.py:388
  140.1 0.0 all-to-all-done.2
  140.1 10.1 %shard_map.91 = bf16[64,4096]{1,0:T(8,128)(2,1)} custom-call(s32[64]{0:T(128)} %get-tuple-element.30.refs_0_, s32[2,64]{1,0:T(2,128)} %bitcast.17, bf16[2048,256]{1,0:T(8,128)(2,1)} %bitcast.7.refs_2_, bf16[4,64,4096]{2,1,0:T(8,128)(2,1)} %refs_4_.7, bf16[4,64,4096]{2,1,0:T(8,128)(2,1)} %refs_4_.7, f32[64,32,128]{2,1,0:T(8,128)} %shard_map.90.refs_5_, ...), custom_call_target="tpu_custom_call" | custom-call | flops 4294967296 | bytes 4194304 | tf_op jit(solution)/shard_map/pallas_call | solution.py:388
Async XLA Ops:
  11.7 31.6 %all-to-all-start = ((bf16[128,8,640]{2,1,0:T(8,128)(2,1)}), bf16[128,8,640]{2,1,0:T(8,128)(2,1)}, u32[]{:S(2)}, u32[]{:S(2)}) async-start(bf16[128,8,640]{2,1,0:T(8,128)(2,1)} %bitcast.11), calls=%async_computation | async-start | bytes 2621440 | tf_op jit(solution)/shard_map/all_to_all | solution.py:442
  34.4 14.8 %copy-start.1 = (f32[8,4096]{1,0:T(8,128)S(1)}, f32[8,4096]{1,0:T(8,128)}, u32[]{:S(2)}) copy-start(f32[8,4096]{1,0:T(8,128)} %param.13) | copy-start | bytes 393220
  43.4 36.6 %all-to-all-start.1 = ((bf16[128,8,512]{2,1,0:T(8,128)(2,1)}), bf16[128,8,512]{2,1,0:T(8,128)(2,1)S(1)}, u32[]{:S(2)}, u32[]{:S(2)}) async-start(bf16[128,8,512]{2,1,0:T(8,128)(2,1)} %bitcast.13), calls=%async_computation.1 | async-start | bytes 2097152 | tf_op jit(solution)/shard_map/all_to_all | solution.py:442
  49.2 19.8 %collective-permute-start = (f32[8,4096]{1,0:T(8,128)S(1)}, f32[8,4096]{1,0:T(8,128)S(1)}, u32[]{:S(2)}, u32[]{:S(2)}) collective-permute-start(f32[8,4096]{1,0:T(8,128)S(1)} %copy-done.1), channel_id=1, source_target_pairs={{0,0},{1,1},{2,2},{3,3},{4,4},{5,5},{6,6},{7,7},{8,14},{9,15},{10,... | collective-permute-start | bytes 393224 | tf_op jit(solution)/shard_map/ppermute | solution.py:434
  73.1 1.8 %collective-permute-start.3 = (f32[8,2048]{1,0:T(8,128)S(1)}, f32[8,2048]{1,0:T(8,128)S(1)}, u32[]{:S(2)}, u32[]{:S(2)}) collective-permute-start(f32[8,2048]{1,0:T(8,128)S(1)} %get-tuple-element.26), channel_id=1, source_target_pairs={{0,1},{1,0},{2,3},{3,2},{4,5},{5,4},{6,7},{7,6},{14,15},{15,14},{1... | collective-permute-start | bytes 196616 | tf_op jit(solution)/shard_map/ppermute | solution.py:414
  73.9 3.7 %collective-permute-start.4 = (f32[8,2048]{1,0:T(8,128)S(1)}, f32[8,2048]{1,0:T(8,128)S(1)}, u32[]{:S(2)}, u32[]{:S(2)}) collective-permute-start(f32[8,2048]{1,0:T(8,128)S(1)} %get-tuple-element.27), channel_id=1, source_target_pairs={{0,97},{1,2},{2,1},{3,4},{4,3},{5,6},{6,5},{7,14},{14,7},{15,12},{... | collective-permute-start | bytes 196616 | tf_op jit(solution)/shard_map/ppermute | solution.py:414
  80.0 23.0 %all-to-all-start.3 = ((bf16[128,16,256]{2,1,0:T(8,128)(2,1)}), bf16[128,16,256]{2,1,0:T(8,128)(2,1)S(1)}, u32[]{:S(2)}, u32[]{:S(2)}) async-start(bf16[128,16,256]{2,1,0:T(8,128)(2,1)} %bitcast.8), calls=%async_computation.3 | async-start | bytes 2097152 | tf_op jit(solution)/shard_map/all_to_all | solution.py:442
  87.1 1.7 %collective-permute-start.1 = (f32[8,2048]{1,0:T(8,128)S(1)}, f32[8,2048]{1,0:T(8,128)S(1)}, u32[]{:S(2)}, u32[]{:S(2)}) collective-permute-start(f32[8,2048]{1,0:T(8,128)S(1)} %get-tuple-element.22), channel_id=1, source_target_pairs={{0,1},{1,0},{2,3},{3,2},{4,5},{5,4},{6,7},{7,6},{14,15},{15,14},{1... | collective-permute-start | bytes 196616 | tf_op jit(solution)/shard_map/ppermute | solution.py:414
  87.6 11.1 %collective-permute-start.2 = (f32[8,2048]{1,0:T(8,128)S(1)}, f32[8,2048]{1,0:T(8,128)S(1)}, u32[]{:S(2)}, u32[]{:S(2)}) collective-permute-start(f32[8,2048]{1,0:T(8,128)S(1)} %get-tuple-element.23), channel_id=1, source_target_pairs={{0,97},{1,2},{2,1},{3,4},{4,3},{5,6},{6,5},{7,14},{14,7},{15,12},{... | collective-permute-start | bytes 196616 | tf_op jit(solution)/shard_map/ppermute | solution.py:414
  103.0 26.9 %copy-start = (bf16[128,16,256]{2,1,0:T(8,128)(2,1)}, bf16[128,16,256]{2,1,0:T(8,128)(2,1)S(1)}, u32[]{:S(2)}) copy-start(bf16[128,16,256]{2,1,0:T(8,128)(2,1)S(1)} %all-to-all-done.3) | copy-start | bytes 3145732
  103.0 37.2 %all-to-all-start.2 = ((bf16[128,16,256]{2,1,0:T(8,128)(2,1)}), bf16[128,16,256]{2,1,0:T(8,128)(2,1)}, u32[]{:S(2)}, u32[]{:S(2)}) async-start(bf16[128,16,256]{2,1,0:T(8,128)(2,1)} %bitcast.6), calls=%async_computation.2 | async-start | bytes 2097152 | tf_op jit(solution)/shard_map/all_to_all | solution.py:442
  111.1 18.2 %collective-permute-start.5 = (f32[8,4096]{1,0:T(8,128)S(1)}, f32[8,4096]{1,0:T(8,128)S(1)}, u32[]{:S(2)}, u32[]{:S(2)}) collective-permute-start(f32[8,4096]{1,0:T(8,128)S(1)} %get-tuple-element.29), channel_id=1, source_target_pairs={{0,0},{1,1},{2,2},{3,3},{4,4},{5,5},{6,6},{7,7},{14,8},{15,9},{12,... | collective-permute-start | bytes 393224 | tf_op jit(solution)/shard_map/ppermute | solution.py:438

commit v7 on v6

--- a/solution.py
+++ b/solution.py
@@ -172,7 +172,7 @@
 def spread(at_ref, got_ref, ext_ref, own_ref, rim_ref, near_ref, far_ref, acc, h):
     even = lax.axis_index("slab") == 0
 
-    @pl.loop(0, DEVS // 2, unroll=2)
+    @pl.loop(0, DEVS // 2, unroll=8)
     def _(q):
         rows = pl.ds(pl.multiple_of(q * 16, 16), 16)
         for r in range(2):
@@ -194,8 +194,8 @@
             half = ext_ref[:, grid] + 0.5 * own
             own_ref[:, cells] = own
             rim_ref[:, cells] = rim
-            near_ref[:, cells] = jnp.where(even, rim, half)
-            far_ref[:, cells] = jnp.where(even, half, rim)
+            near_ref[:, cells] = jnp.where(even, rim, half).astype(BF16)
+            far_ref[:, cells] = jnp.where(even, half, rim).astype(BF16)
 
 
 def gather_first(
@@ -228,7 +228,7 @@
             n = s * LPS + l
             cells = slice(n * LANES, (n + 1) * LANES)
             grid = slice(s * SEGW + h * HALF + l * LANES, s * SEGW + h * HALF + (l + 1) * LANES)
-            near, far = near_ref[:, cells], far_ref[:, cells]
+            near, far = near_ref[:, cells].astype(F32), far_ref[:, cells].astype(F32)
             below = jnp.where(even, far, near)
             above = jnp.where(even, near, far)
             density = own_ref[:, cells] + below
@@ -241,7 +241,7 @@
             pot[row : row + CZB, :] = ext_ref[:, grid] + 0.5 * density
             pot[row + CZB : row + 2 * CZB, :] = above + 0.5 * rim_ref[:, cells]
 
-    @pl.loop(0, DEVS, unroll=4)
+    @pl.loop(0, DEVS, unroll=16)
     def _(d):
         rows = pl.ds(pl.multiple_of(d * 16, 16), 16)
         for l in range(LPS):
@@ -337,13 +337,14 @@
 
 def gather_tiles(h, got, ext_potential, places=None):
     part = jax.ShapeDtypeStruct((CZB, PLANE // HALVES), F32)
+    swap = jax.ShapeDtypeStruct((CZB, PLANE // HALVES), BF16)
     acc = pltpu.VMEM((SEGS * LPS * 2 * CZB, LANES), F32)
     if h == 0:
         return pl.pallas_call(
             gather_first,
             in_specs=[VMEM, VMEM],
             out_specs=[VMEM, VMEM, VMEM, VMEM, SMEM],
-            out_shape=[part, part, part, part, jax.ShapeDtypeStruct((8, DEVS), jnp.int32)],
+            out_shape=[part, part, swap, swap, jax.ShapeDtypeStruct((8, DEVS), jnp.int32)],
             scratch_shapes=[
                 pltpu.VMEM((DEVS * CZB, LANES), F32),
                 pltpu.VMEM((8, DEVS), jnp.int32),
@@ -358,7 +359,7 @@
         gather_second,
         in_specs=[SMEM, VMEM, VMEM],
         out_specs=[VMEM, VMEM, VMEM, VMEM],
-        out_shape=[part, part, part, part],
+        out_shape=[part, part, swap, swap],
         scratch_shapes=[acc],
         cost_estimate=cost(1 << 20, 3 << 20),
         compiler_params=room(SMALL_MIB),

time: 151 us -> 150 us (level)
  no operation moved by 1% of the time
where the time goes in v7:
time: 150 us
  Pallas kernels  54.5 us (36%)
  waiting for transfers between devices  49.7 us (33%)
  starting transfers between devices  44.7 us (30%)
    all_to_all x4, starting transfers between devices, exchanged(): return lax.all_to_all(x, AXES, split_axis=0, concat_axis=0, tiled=True)  29.7 us
    pallas_call x2, Pallas kernels, make_tiles(): pl.pallas_call(lambda *refs: tiles_kernel(h, *refs), grid=(STEPS,), in_sp...  22.5 us
    pallas_call x2, Pallas kernels, make_matrices(): pl.pallas_call(lambda *refs: matrix_kernel(h, *refs), grid=(STEPS,), in_s...  20.4 us
    ppermute x1, waiting for transfers between devices, to_homes(): return lax.ppermute(x, AXES, [(e, home(e)) for e in range(DEVS)])  14.7 us
    ppermute x2, waiting for transfers between devices, swapped(): lax.ppermute(far, AXES, next_pairs)  11.7 us
    all_to_all x4, waiting for transfers between devices, exchanged(): return lax.all_to_all(x, AXES, split_axis=0, concat_axis=0, tiled=True)  11.6 us
    ppermute x1, waiting for transfers between devices, from_homes(): return lax.ppermute(x, AXES, [(home(e), e) for e in range(DEVS)])  10.9 us
    ppermute x1, starting transfers between devices, from_homes(): return lax.ppermute(x, AXES, [(home(e), e) for e in range(DEVS)])  7.3 us
  transfers between devices with their start and end apart: 10, of which 7 were waited for; matrix products, arithmetic and copies ran while one was open for 0% of the time, Pallas kernels for 22%

profile of v7, /device:TPU:3, one launch (start us, length us, event | category | flops | bytes accessed | tf_op | source)
XLA Modules:
  0.0 149.6 jit_solution(10273097853705445628)
XLA Ops:
  0.6 11.1 %shard_map.86 = bf16[1024,640]{1,0:T(8,128)(2,1)} custom-call(s32[1,64]{1,0:T(1,128)} %bitcast.18, s32[2,64]{1,0:T(2,128)} %bitcast.14, s32[64]{0:T(128)} %refs_2_.2, s32[64]{0:T(128)} %refs_3_.4, bf16[64,4096]{1,0:T(8,128)(2,1)} %refs_2_.3, bf16[4,64,4096]{2,1,0:T(8,128)(2,1)} %refs_4_.7, bf16[4,64,4096]{2,1,0:T(8,128)(2,1)} %refs_4_.7), custom_call_target="tpu_custom_call" | custom-call | flops 4294967296 | bytes 4194304 | tf_op jit(solution)/shard_map/pallas_call | solution.py:314
  11.7 11.2 %all-to-all-start = ((bf16[128,8,640]{2,1,0:T(8,128)(2,1)}), bf16[128,8,640]{2,1,0:T(8,128)(2,1)}, u32[]{:S(2)}, u32[]{:S(2)}) async-start(bf16[128,8,640]{2,1,0:T(8,128)(2,1)} %bitcast.11), calls=%async_computation | async-start | bytes 2621440 | tf_op jit(solution)/shard_map/all_to_all | solution.py:443
  23.0 11.4 %shard_map.87 = (bf16[1024,512]{1,0:T(8,128)(2,1)}, s32[64]{0:T(128)}, bf16[4,256,512]{2,1,0:T(8,128)(2,1)}) custom-call(s32[1,64]{1,0:T(1,128)} %bitcast.19, s32[2,64]{1,0:T(2,128)} %bitcast.15, bf16[64,4096]{1,0:T(8,128)(2,1)} %refs_2_.3, bf16[4,64,4096]{2,1,0:T(8,128)(2,1)} %refs_4_.7, bf16[4,64,4096]{2,1,0:T(8,128)(2,1)} %refs_4_.7), custom_call_target="tpu_custom_call" | custom-call | flops 4294967296 | bytes 4194304 | tf_op jit(solution)/shard_map/pallas_call | solution.py:314
  34.4 0.0 copy-start.1
  34.4 9.0 %all-to-all-done = bf16[128,8,640]{2,1,0:T(8,128)(2,1)} async-done(((bf16[128,8,640]{2,1,0:T(8,128)(2,1)}), bf16[128,8,640]{2,1,0:T(8,128)(2,1)}, u32[]{:S(2)}, u32[]{:S(2)}) %all-to-all-start) | async-done | bytes 1310752 | tf_op jit(solution)/shard_map/all_to_all | solution.py:443
  43.4 5.8 %all-to-all-start.1 = ((bf16[128,8,512]{2,1,0:T(8,128)(2,1)}), bf16[128,8,512]{2,1,0:T(8,128)(2,1)S(1)}, u32[]{:S(2)}, u32[]{:S(2)}) async-start(bf16[128,8,512]{2,1,0:T(8,128)(2,1)} %bitcast.13), calls=%async_computation.1 | async-start | bytes 2097152 | tf_op jit(solution)/shard_map/all_to_all | solution.py:443
  49.1 0.0 copy-done.1
  49.2 5.1 %collective-permute-start = (f32[8,4096]{1,0:T(8,128)S(1)}, f32[8,4096]{1,0:T(8,128)S(1)}, u32[]{:S(2)}, u32[]{:S(2)}) collective-permute-start(f32[8,4096]{1,0:T(8,128)S(1)} %copy-done.1), channel_id=1, source_target_pairs={{0,0},{1,1},{2,2},{3,3},{4,4},{5,5},{6,6},{7,7},{8,14},{9,15},{10,... | collective-permute-start | bytes 393224 | tf_op jit(solution)/shard_map/ppermute | solution.py:435
  54.3 14.7 %collective-permute-done.ext_ref.refs_3_ = f32[8,4096]{1,0:T(8,128)S(1)} collective-permute-done((f32[8,4096]{1,0:T(8,128)S(1)}, f32[8,4096]{1,0:T(8,128)S(1)}, u32[]{:S(2)}, u32[]{:S(2)}) %collective-permute-start) | collective-permute-done | bytes 131104 | tf_op jit(solution)/shard_map/ppermute | solution.py:435
  68.9 4.0 %gather_tiles0.1 = (f32[8,2048]{1,0:T(8,128)S(1)}, f32[8,2048]{1,0:T(8,128)S(1)}, bf16[8,2048]{1,0:T(8,128)(2,1)S(1)}, bf16[8,2048]{1,0:T(8,128)(2,1)S(1)}, s32[8,128]{1,0:T(8,128)S(1)}) custom-call(bf16[1024,640]{1,0:T(8,128)(2,1)} %bitcast.3.got_ref, f32[8,4096]{1,0:T(8,128)S(1)} %collective-permute-done.ext_ref.refs_3_), custom_call_target="tpu_custom_call" | custom-call | flops 1048576 | bytes 3145728 | tf_op jit(solution)/shard_map/gather_tiles0/pallas_call | solution.py:343
  72.9 0.9 collective-permute-start.3
  73.8 0.0 collective-permute-start.4
  73.8 0.9 collective-permute-done.3.refs_4_
  74.7 2.5 %collective-permute-done.4.refs_5_ = bf16[8,2048]{1,0:T(8,128)(2,1)S(1)} collective-permute-done((bf16[8,2048]{1,0:T(8,128)(2,1)S(1)}, bf16[8,2048]{1,0:T(8,128)(2,1)S(1)}, u32[]{:S(2)}, u32[]{:S(2)}) %collective-permute-start.4) | collective-permute-done | bytes 32800 | tf_op jit(solution)/shard_map/ppermute | solution.py:415
  77.1 2.4 %shard_map.88 = (f32[8,2048]{1,0:T(8,128)S(1)}, bf16[2048,256]{1,0:T(8,128)(2,1)}) custom-call(s32[8,128]{1,0:T(8,128)S(1)} %get-tuple-element.18.at_ref.refs_0_, f32[8,2048]{1,0:T(8,128)S(1)} %get-tuple-element.24.refs_1_, f32[8,2048]{1,0:T(8,128)S(1)} %get-tuple-element.25.refs_2_, f32[8,4096]{1,0:T(8,128)S(1)} %collective-permute-done.ext_ref.refs_3_, ...), custom_call_target="tpu_custom_call" | custom-call | flops 1048576 | bytes 3145728 | tf_op jit(solution)/shard_map/pallas_call | solution.py:372
  79.6 0.0 all-to-all-done.1
  79.6 5.0 %all-to-all-start.3 = ((bf16[128,16,256]{2,1,0:T(8,128)(2,1)}), bf16[128,16,256]{2,1,0:T(8,128)(2,1)S(1)}, u32[]{:S(2)}, u32[]{:S(2)}) async-start(bf16[128,16,256]{2,1,0:T(8,128)(2,1)} %bitcast.8), calls=%async_computation.3 | async-start | bytes 2097152 | tf_op jit(solution)/shard_map/all_to_all | solution.py:443
  84.6 2.1 %gather_tiles1.1 = (f32[8,2048]{1,0:T(8,128)S(1)}, f32[8,2048]{1,0:T(8,128)S(1)}, bf16[8,2048]{1,0:T(8,128)(2,1)S(1)}, bf16[8,2048]{1,0:T(8,128)(2,1)S(1)}) custom-call(s32[8,128]{1,0:T(8,128)S(1)} %get-tuple-element.18.at_ref.refs_0_, bf16[1024,512]{1,0:T(8,128)(2,1)S(1)} %bitcast.10, f32[8,4096]{1,0:T(8,128)S(1)} %collective-permute-done.ext_ref.refs_3_), custom_call_target="tpu_custom_call" | custom-call | flops 1048576 | bytes 3145728 | tf_op jit(solution)/shard_map/gather_tiles1/pallas_call | solution.py:358
  86.7 0.5 collective-permute-start.1
  87.2 1.2 collective-permute-start.2
  88.3 0.0 collective-permute-done.1.refs_4_
  88.3 9.2 %collective-permute-done.2.refs_5_ = bf16[8,2048]{1,0:T(8,128)(2,1)S(1)} collective-permute-done((bf16[8,2048]{1,0:T(8,128)(2,1)S(1)}, bf16[8,2048]{1,0:T(8,128)(2,1)S(1)}, u32[]{:S(2)}, u32[]{:S(2)}) %collective-permute-start.2) | collective-permute-done | bytes 32800 | tf_op jit(solution)/shard_map/ppermute | solution.py:415
  97.5 2.4 %shard_map.89 = (f32[8,4096]{1,0:T(8,128)S(1)}, bf16[2048,256]{1,0:T(8,128)(2,1)}) custom-call(s32[8,128]{1,0:T(8,128)S(1)} %get-tuple-element.18.at_ref.refs_0_, f32[8,2048]{1,0:T(8,128)S(1)} %get-tuple-element.20.refs_1_, f32[8,2048]{1,0:T(8,128)S(1)} %get-tuple-element.21.refs_2_, f32[8,4096]{1,0:T(8,128)S(1)} %collective-permute-done.ext_ref.refs_3_, ...), custom_call_target="tpu_custom_call" | custom-call | flops 1048576 | bytes 3145728 | tf_op jit(solution)/shard_map/pallas_call | solution.py:372
  100.0 2.6 %all-to-all-done.3 = bf16[128,16,256]{2,1,0:T(8,128)(2,1)S(1)} async-done(((bf16[128,16,256]{2,1,0:T(8,128)(2,1)}), bf16[128,16,256]{2,1,0:T(8,128)(2,1)S(1)}, u32[]{:S(2)}, u32[]{:S(2)}) %all-to-all-start.3) | async-done | bytes 1048608 | tf_op jit(solution)/shard_map/all_to_all | solution.py:443
  102.6 0.0 copy-start
  102.6 7.8 %all-to-all-start.2 = ((bf16[128,16,256]{2,1,0:T(8,128)(2,1)}), bf16[128,16,256]{2,1,0:T(8,128)(2,1)}, u32[]{:S(2)}, u32[]{:S(2)}) async-start(bf16[128,16,256]{2,1,0:T(8,128)(2,1)} %bitcast.6), calls=%async_computation.2 | async-start | bytes 2097152 | tf_op jit(solution)/shard_map/all_to_all | solution.py:443
  110.4 7.3 %collective-permute-start.5 = (f32[8,4096]{1,0:T(8,128)S(1)}, f32[8,4096]{1,0:T(8,128)S(1)}, u32[]{:S(2)}, u32[]{:S(2)}) collective-permute-start(f32[8,4096]{1,0:T(8,128)S(1)} %get-tuple-element.29), channel_id=1, source_target_pairs={{0,0},{1,1},{2,2},{3,3},{4,4},{5,5},{6,6},{7,7},{14,8},{15,9},{12,... | collective-permute-start | bytes 393224 | tf_op jit(solution)/shard_map/ppermute | solution.py:439
  117.7 10.9 %collective-permute-done.5.in_ref = f32[8,4096]{1,0:T(8,128)S(1)} collective-permute-done((f32[8,4096]{1,0:T(8,128)S(1)}, f32[8,4096]{1,0:T(8,128)S(1)}, u32[]{:S(2)}, u32[]{:S(2)}) %collective-permute-start.5) | collective-permute-done | bytes 131104 | tf_op jit(solution)/shard_map/ppermute | solution.py:439
  128.5 0.7 written.1
  129.2 0.0 copy-done
  129.2 10.2 %shard_map.90.refs_5_ = f32[64,32,128]{2,1,0:T(8,128)} custom-call(s32[64]{0:T(128)} %get-tuple-element.30.refs_0_, s32[2,64]{1,0:T(2,128)} %bitcast.16, bf16[2048,256]{1,0:T(8,128)(2,1)} %bitcast.12, bf16[4,64,4096]{2,1,0:T(8,128)(2,1)} %refs_4_.7, bf16[4,64,4096]{2,1,0:T(8,128)(2,1)} %refs_4_.7), custom_call_target="tpu_custom_call" | custom-call | flops 4294967296 | bytes 4194304 | tf_op jit(solution)/shard_map/pallas_call | solution.py:389
  139.5 0.0 all-to-all-done.2
  139.5 10.1 %shard_map.91 = bf16[64,4096]{1,0:T(8,128)(2,1)} custom-call(s32[64]{0:T(128)} %get-tuple-element.30.refs_0_, s32[2,64]{1,0:T(2,128)} %bitcast.17, bf16[2048,256]{1,0:T(8,128)(2,1)} %bitcast.7.refs_2_, bf16[4,64,4096]{2,1,0:T(8,128)(2,1)} %refs_4_.7, bf16[4,64,4096]{2,1,0:T(8,128)(2,1)} %refs_4_.7, f32[64,32,128]{2,1,0:T(8,128)} %shard_map.90.refs_5_, ...), custom_call_target="tpu_custom_call" | custom-call | flops 4294967296 | bytes 4194304 | tf_op jit(solution)/shard_map/pallas_call | solution.py:389
Async XLA Ops:
  11.7 31.6 %all-to-all-start = ((bf16[128,8,640]{2,1,0:T(8,128)(2,1)}), bf16[128,8,640]{2,1,0:T(8,128)(2,1)}, u32[]{:S(2)}, u32[]{:S(2)}) async-start(bf16[128,8,640]{2,1,0:T(8,128)(2,1)} %bitcast.11), calls=%async_computation | async-start | bytes 2621440 | tf_op jit(solution)/shard_map/all_to_all | solution.py:443
  34.4 14.8 %copy-start.1 = (f32[8,4096]{1,0:T(8,128)S(1)}, f32[8,4096]{1,0:T(8,128)}, u32[]{:S(2)}) copy-start(f32[8,4096]{1,0:T(8,128)} %param.13) | copy-start | bytes 393220
  43.4 36.2 %all-to-all-start.1 = ((bf16[128,8,512]{2,1,0:T(8,128)(2,1)}), bf16[128,8,512]{2,1,0:T(8,128)(2,1)S(1)}, u32[]{:S(2)}, u32[]{:S(2)}) async-start(bf16[128,8,512]{2,1,0:T(8,128)(2,1)} %bitcast.13), calls=%async_computation.1 | async-start | bytes 2097152 | tf_op jit(solution)/shard_map/all_to_all | solution.py:443
  49.2 19.8 %collective-permute-start = (f32[8,4096]{1,0:T(8,128)S(1)}, f32[8,4096]{1,0:T(8,128)S(1)}, u32[]{:S(2)}, u32[]{:S(2)}) collective-permute-start(f32[8,4096]{1,0:T(8,128)S(1)} %copy-done.1), channel_id=1, source_target_pairs={{0,0},{1,1},{2,2},{3,3},{4,4},{5,5},{6,6},{7,7},{8,14},{9,15},{10,... | collective-permute-start | bytes 393224 | tf_op jit(solution)/shard_map/ppermute | solution.py:435
  72.9 1.7 %collective-permute-start.3 = (bf16[8,2048]{1,0:T(8,128)(2,1)S(1)}, bf16[8,2048]{1,0:T(8,128)(2,1)S(1)}, u32[]{:S(2)}, u32[]{:S(2)}) collective-permute-start(bf16[8,2048]{1,0:T(8,128)(2,1)S(1)} %get-tuple-element.26), channel_id=1, source_target_pairs={{0,1},{1,0},{2,3},{3,2},{4,5},{5,4},{6,7},{7,6},{14,15},{15,14},{1... | collective-permute-start | bytes 98312 | tf_op jit(solution)/shard_map/ppermute | solution.py:415
  73.8 3.3 %collective-permute-start.4 = (bf16[8,2048]{1,0:T(8,128)(2,1)S(1)}, bf16[8,2048]{1,0:T(8,128)(2,1)S(1)}, u32[]{:S(2)}, u32[]{:S(2)}) collective-permute-start(bf16[8,2048]{1,0:T(8,128)(2,1)S(1)} %get-tuple-element.27), channel_id=1, source_target_pairs={{0,97},{1,2},{2,1},{3,4},{4,3},{5,6},{6,5},{7,14},{14,7},{15,12},{... | collective-permute-start | bytes 98312 | tf_op jit(solution)/shard_map/ppermute | solution.py:415
  79.6 23.0 %all-to-all-start.3 = ((bf16[128,16,256]{2,1,0:T(8,128)(2,1)}), bf16[128,16,256]{2,1,0:T(8,128)(2,1)S(1)}, u32[]{:S(2)}, u32[]{:S(2)}) async-start(bf16[128,16,256]{2,1,0:T(8,128)(2,1)} %bitcast.8), calls=%async_computation.3 | async-start | bytes 2097152 | tf_op jit(solution)/shard_map/all_to_all | solution.py:443
  86.7 1.7 %collective-permute-start.1 = (bf16[8,2048]{1,0:T(8,128)(2,1)S(1)}, bf16[8,2048]{1,0:T(8,128)(2,1)S(1)}, u32[]{:S(2)}, u32[]{:S(2)}) collective-permute-start(bf16[8,2048]{1,0:T(8,128)(2,1)S(1)} %get-tuple-element.22), channel_id=1, source_target_pairs={{0,1},{1,0},{2,3},{3,2},{4,5},{5,4},{6,7},{7,6},{14,15},{15,14},{1... | collective-permute-start | bytes 98312 | tf_op jit(solution)/shard_map/ppermute | solution.py:415
  87.2 10.4 %collective-permute-start.2 = (bf16[8,2048]{1,0:T(8,128)(2,1)S(1)}, bf16[8,2048]{1,0:T(8,128)(2,1)S(1)}, u32[]{:S(2)}, u32[]{:S(2)}) collective-permute-start(bf16[8,2048]{1,0:T(8,128)(2,1)S(1)} %get-tuple-element.23), channel_id=1, source_target_pairs={{0,97},{1,2},{2,1},{3,4},{4,3},{5,6},{6,5},{7,14},{14,7},{15,12},{... | collective-permute-start | bytes 98312 | tf_op jit(solution)/shard_map/ppermute | solution.py:415
  102.6 26.6 %copy-start = (bf16[128,16,256]{2,1,0:T(8,128)(2,1)}, bf16[128,16,256]{2,1,0:T(8,128)(2,1)S(1)}, u32[]{:S(2)}) copy-start(bf16[128,16,256]{2,1,0:T(8,128)(2,1)S(1)} %all-to-all-done.3) | copy-start | bytes 3145732
  102.6 36.9 %all-to-all-start.2 = ((bf16[128,16,256]{2,1,0:T(8,128)(2,1)}), bf16[128,16,256]{2,1,0:T(8,128)(2,1)}, u32[]{:S(2)}, u32[]{:S(2)}) async-start(bf16[128,16,256]{2,1,0:T(8,128)(2,1)} %bitcast.6), calls=%async_computation.2 | async-start | bytes 2097152 | tf_op jit(solution)/shard_map/all_to_all | solution.py:443
  110.4 18.2 %collective-permute-start.5 = (f32[8,4096]{1,0:T(8,128)S(1)}, f32[8,4096]{1,0:T(8,128)S(1)}, u32[]{:S(2)}, u32[]{:S(2)}) collective-permute-start(f32[8,4096]{1,0:T(8,128)S(1)} %get-tuple-element.29), channel_id=1, source_target_pairs={{0,0},{1,1},{2,2},{3,3},{4,4},{5,5},{6,6},{7,7},{14,8},{15,9},{12,... | collective-permute-start | bytes 393224 | tf_op jit(solution)/shard_map/ppermute | solution.py:439
